TPU v7x, 32 devices: a whole 2x2x4 slice. The times are simulated.
32 devices in a mesh: seq: 8 (over y, x, core), dp: 4 (over z).
Axes of the slice: x: 2, y: 2, z: 4, core: 2. Of those that a mesh axis runs over, the one named last changes fastest.
Arguments:
- block_input: float32 [4, 1024, 2048], P('dp', 'seq'), may hold values from -6 to 6
- lengths: int32 [4, 4], P('dp'), may hold values from 1 to 512, 1024 in all within a row
- cotangent: float32 [4, 1024, 2048], P('dp', 'seq'), may hold values from -6 to 6
- attn_gain: float32 [2048], P(('seq', 'dp')), may hold values from 0.5 to 1.5
- w_qa: float32 [2048, 1024], P(('seq', 'dp')), may hold values from -0.125 to 0.125
- q_gain: float32 [1024], P(('seq', 'dp')), may hold values from 0.5 to 1.5
- w_qb: float32 [1024, 4096], P(('seq', 'dp')), may hold values from -0.1875 to 0.1875
- w_k: float32 [2048, 256], P(('seq', 'dp')), may hold values from -0.125 to 0.125
- k_gain: float32 [256], P(('seq', 'dp')), may hold values from 0.5 to 1.5
- w_v: float32 [2048, 256], P(('seq', 'dp')), may hold values from -0.125 to 0.125
- w_o: float32 [4096, 2048], P(('seq', 'dp')), may hold values from -1.5 to 1.5
- mlp_gain: float32 [2048], P(('seq', 'dp')), may hold values from 0.5 to 1.5
- w_gate: float32 [2048, 5632], P(('seq', 'dp')), may hold values from -0.125 to 0.125
- w_up: float32 [2048, 5632], P(('seq', 'dp')), may hold values from -0.125 to 0.125
- w_down: float32 [5632, 2048], P(('seq', 'dp')), may hold values from -0.078125 to 0.078125
Outputs:
- block_output: float32 [4, 1024, 2048], P('dp', 'seq')
- grad_input: float32 [4, 1024, 2048], P('dp', 'seq')
- grad_attn_gain: float32 [2048], P(('seq', 'dp'))
- grad_w_qa: float32 [2048, 1024], P(('seq', 'dp'))
- grad_q_gain: float32 [1024], P(('seq', 'dp'))
- grad_w_qb: float32 [1024, 4096], P(('seq', 'dp'))
- grad_w_k: float32 [2048, 256], P(('seq', 'dp'))
- grad_k_gain: float32 [256], P(('seq', 'dp'))
- grad_w_v: float32 [2048, 256], P(('seq', 'dp'))
- grad_w_o: float32 [4096, 2048], P(('seq', 'dp'))
- grad_mlp_gain: float32 [2048], P(('seq', 'dp'))
- grad_w_gate: float32 [2048, 5632], P(('seq', 'dp'))
- grad_w_up: float32 [2048, 5632], P(('seq', 'dp'))
- grad_w_down: float32 [5632, 2048], P(('seq', 'dp'))
Inputs may be any that keep to these rules, and one draw needn't show every extreme that they name: Each row of lengths holds the lengths of the 4 packed sequences of one group, in order, summing to 1024; in every row the longest is exactly 512.
All inputs are finite; a program needn't handle non-finite values.
Results may differ from a plain program's by a relative error of at most 0.018.
The roundings to bfloat16 on the way count: a program that leaves them out, or rounds other values in their place, can miss the bound.
Values may be sent and summed in bfloat16 or wider, within the bound.
A program may use at most 384 MiB of HBM per device.

v0:
```python
import math

import jax
import jax.numpy as jnp
from jax import lax
from jax.sharding import PartitionSpec as P

D = 2048
H = 16
E = 256


eps_norm = 1e-06
big_negative = -1e30


def rms_scale(values, gain_vec):
    inverse = lax.rsqrt(jnp.mean(values * values, axis=-1, keepdims=True) + eps_norm)
    return values * inverse * gain_vec


def norm_back(values, gain_vec, upstream):
    inverse = lax.rsqrt(jnp.mean(values * values, axis=-1, keepdims=True) + eps_norm)
    gain_grad = jnp.sum(upstream * values * inverse, axis=0)
    scaled = upstream * gain_vec
    value_grad = inverse * scaled - values * (inverse * inverse * inverse) * jnp.mean(
        scaled * values, axis=-1, keepdims=True
    )
    return (value_grad, gain_grad)


def rotate(values, cosine, sine_tab):
    half_width = values.shape[-1] // 2
    turned = jnp.concatenate([-values[..., half_width:], values[..., :half_width]], axis=-1)
    return values * cosine + turned * sine_tab


def rotate_back(upstream, cosine, sine_tab):
    half_width = upstream.shape[-1] // 2
    weighted = upstream * sine_tab
    turned = jnp.concatenate([weighted[..., half_width:], -weighted[..., :half_width]], axis=-1)
    return upstream * cosine + turned


def layout(seq_lengths, group_tokens):
    seq_ends = jnp.cumsum(seq_lengths)
    places = jnp.arange(group_tokens, dtype=jnp.int32)
    passed = places[:, None] >= seq_ends[None, :]
    segment = jnp.sum(passed.astype(jnp.int32), axis=1)
    starts = jnp.sum(jnp.where(passed, seq_lengths[None, :], 0), axis=1)
    return (segment, places, places - starts)


def rope_tables(offsets, width):
    half_width = width // 2
    frequency = jnp.exp(
        jnp.arange(half_width, dtype=jnp.float32) * (-2.0 * math.log(10000.0) / width)
    )
    angles = offsets.astype(jnp.float32)[:, None] * frequency[None, :]
    angles = jnp.concatenate([angles, angles], axis=-1)
    return (jnp.cos(angles), jnp.sin(angles))


def block_terms(
    queries, keys_all, seg_query, place_query, segment, places, key_start, key_width, score_scale
):
    key_block = lax.dynamic_slice_in_dim(keys_all, key_start, key_width, 0)
    scores = (
        jnp.einsum("thd,kd->thk", queries, key_block, preferred_element_type=jnp.float32)
        * score_scale
    )
    seg_keys = lax.dynamic_slice_in_dim(segment, key_start, key_width, 0)
    place_keys = lax.dynamic_slice_in_dim(places, key_start, key_width, 0)
    allowed = (seg_query[:, None] == seg_keys[None, :]) & (
        place_keys[None, :] <= place_query[:, None]
    )
    return (scores, allowed[:, None, :], key_block)


def local(
    block_input,
    lengths,
    cotangent,
    attn_gain,
    w_qa,
    q_gain,
    w_qb,
    w_k,
    k_gain,
    w_v,
    w_o,
    mlp_gain,
    w_gate,
    w_up,
    w_down,
):
    tok_rows = block_input.shape[1]
    seq_count = lax.axis_size("seq")
    group_tokens = tok_rows * seq_count
    first_row = lax.axis_index("seq") * tok_rows
    segment, places, offsets = layout(lengths[0], group_tokens)
    seg_query = lax.dynamic_slice_in_dim(segment, first_row, tok_rows, 0)
    place_query = lax.dynamic_slice_in_dim(places, first_row, tok_rows, 0)
    offset_query = lax.dynamic_slice_in_dim(offsets, first_row, tok_rows, 0)
    cosine, sine_tab = rope_tables(offset_query, E)
    key_width = min(256, group_tokens)
    score_scale = 1.0 / math.sqrt(E)
    first_block = (first_row - offset_query[0]) // key_width
    last_block = (first_row + tok_rows - 1) // key_width + 1
    flat_rows = block_input.reshape(tok_rows, D)
    attn_full = (
        lax.all_gather(attn_gain.astype(jnp.bfloat16), ("seq", "dp"), axis=0, tiled=True),
        lax.all_gather(w_qa.astype(jnp.bfloat16), ("seq", "dp"), axis=0, tiled=True),
        lax.all_gather(q_gain.astype(jnp.bfloat16), ("seq", "dp"), axis=0, tiled=True),
        lax.all_gather(w_qb.astype(jnp.bfloat16), ("seq", "dp"), axis=0, tiled=True),
        lax.all_gather(w_k.astype(jnp.bfloat16), ("seq", "dp"), axis=0, tiled=True),
        lax.all_gather(k_gain.astype(jnp.bfloat16), ("seq", "dp"), axis=0, tiled=True),
        lax.all_gather(w_v.astype(jnp.bfloat16), ("seq", "dp"), axis=0, tiled=True),
        lax.all_gather(w_o.astype(jnp.bfloat16), ("seq", "dp"), axis=0, tiled=True),
        lax.all_gather(mlp_gain.astype(jnp.bfloat16), ("seq", "dp"), axis=0, tiled=True),
    )
    gain_one, qa_full, gain_latent, qb_full, k_full, gain_key, v_full, o_full, gain_two = attn_full
    normed = rms_scale(flat_rows, gain_one.astype(jnp.float32)).astype(jnp.bfloat16)
    latent = jnp.dot(normed, qa_full, preferred_element_type=jnp.float32)
    latent_low = rms_scale(latent, gain_latent.astype(jnp.float32)).astype(jnp.bfloat16)
    query_pre = jnp.dot(latent_low, qb_full, preferred_element_type=jnp.float32).reshape(
        tok_rows, H, E
    )
    q_rot = rotate(query_pre, cosine[:, None, :], sine_tab[:, None, :]).astype(jnp.bfloat16)
    key_pre = jnp.dot(normed, k_full, preferred_element_type=jnp.float32)
    key_low = rotate(rms_scale(key_pre, gain_key.astype(jnp.float32)), cosine, sine_tab).astype(
        jnp.bfloat16
    )
    value_low = jnp.dot(normed, v_full, preferred_element_type=jnp.float32).astype(jnp.bfloat16)
    keys_all, values_all = (
        lax.all_gather(key_low, "seq", axis=0, tiled=True),
        lax.all_gather(value_low, "seq", axis=0, tiled=True),
    )

    def stat_step(block_id, running):
        top_now, total_now = running
        scores, allowed, key_block = block_terms(
            q_rot,
            keys_all,
            seg_query,
            place_query,
            segment,
            places,
            block_id * key_width,
            key_width,
            score_scale,
        )
        scores = jnp.where(allowed, scores, big_negative)
        top_next = jnp.maximum(top_now, jnp.max(scores, axis=-1))
        total_next = total_now * jnp.exp(top_now - top_next) + jnp.sum(
            jnp.where(allowed, jnp.exp(scores - top_next[..., None]), 0.0), axis=-1
        )
        return (top_next, total_next)

    top_init = jnp.full((tok_rows, H), big_negative, jnp.float32)
    top_end, total_end = lax.fori_loop(
        first_block, last_block, stat_step, (top_init, jnp.zeros((tok_rows, H), jnp.float32))
    )
    log_total = top_end + jnp.log(total_end)

    def value_step(block_id, summed):
        key_start = block_id * key_width
        scores, allowed, key_block = block_terms(
            q_rot,
            keys_all,
            seg_query,
            place_query,
            segment,
            places,
            key_start,
            key_width,
            score_scale,
        )
        value_block = lax.dynamic_slice_in_dim(values_all, key_start, key_width, 0)
        probs = jnp.where(allowed, jnp.exp(scores - log_total[..., None]), 0.0)
        return summed + jnp.einsum(
            "thk,kd->thd",
            probs.astype(jnp.bfloat16),
            value_block,
            preferred_element_type=jnp.float32,
        )

    attended = lax.fori_loop(
        first_block, last_block, value_step, jnp.zeros((tok_rows, H, E), jnp.float32)
    )
    attended_low = attended.astype(jnp.bfloat16).reshape(tok_rows, H * E)
    mixed_rows = flat_rows + jnp.dot(attended_low, o_full, preferred_element_type=jnp.float32)
    normed_two = rms_scale(mixed_rows, gain_two.astype(jnp.float32)).astype(jnp.bfloat16)
    out_grad = cotangent.reshape(tok_rows, D)
    out_grad_low = out_grad.astype(jnp.bfloat16)
    gate_full, up_full, down_full = (
        lax.all_gather(w_gate.astype(jnp.bfloat16), ("seq", "dp"), axis=0, tiled=True),
        lax.all_gather(w_up.astype(jnp.bfloat16), ("seq", "dp"), axis=0, tiled=True),
        lax.all_gather(w_down.astype(jnp.bfloat16), ("seq", "dp"), axis=0, tiled=True),
    )
    mlp_rows, grad_rows = (normed_two, out_grad_low)
    gate_act = jnp.dot(mlp_rows, gate_full, preferred_element_type=jnp.float32)
    up_act = jnp.dot(mlp_rows, up_full, preferred_element_type=jnp.float32)
    sigmoid_gate = jax.nn.sigmoid(gate_act)
    hidden = (gate_act * sigmoid_gate * up_act).astype(jnp.bfloat16)
    branch_out = jnp.dot(hidden, down_full, preferred_element_type=jnp.float32)
    output_rows = mixed_rows + branch_out
    down_wgrad = jnp.einsum("tf,td->fd", hidden, grad_rows, preferred_element_type=jnp.float32)
    hidden_grad = jnp.einsum("td,fd->tf", grad_rows, down_full, preferred_element_type=jnp.float32)
    gate_grad_low = (
        hidden_grad * up_act * (sigmoid_gate * (1.0 + gate_act * (1.0 - sigmoid_gate)))
    ).astype(jnp.bfloat16)
    up_grad_low = (hidden_grad * (gate_act * sigmoid_gate)).astype(jnp.bfloat16)
    gate_wgrad = jnp.einsum(
        "td,tf->df", mlp_rows, gate_grad_low, preferred_element_type=jnp.float32
    )
    up_wgrad = jnp.einsum("td,tf->df", mlp_rows, up_grad_low, preferred_element_type=jnp.float32)
    normed_two_grad = jnp.einsum(
        "tf,df->td", gate_grad_low, gate_full, preferred_element_type=jnp.float32
    ) + jnp.einsum("tf,df->td", up_grad_low, up_full, preferred_element_type=jnp.float32)
    mlp_shards = (
        lax.psum_scatter(gate_wgrad, ("seq", "dp"), scatter_dimension=0, tiled=True),
        lax.psum_scatter(up_wgrad, ("seq", "dp"), scatter_dimension=0, tiled=True),
        lax.psum_scatter(down_wgrad, ("seq", "dp"), scatter_dimension=0, tiled=True),
    )
    mixed_part, gain_two_grad = norm_back(mixed_rows, gain_two.astype(jnp.float32), normed_two_grad)
    mixed_grad = out_grad + mixed_part
    mixed_low = mixed_grad.astype(jnp.bfloat16)
    o_wgrad = jnp.einsum("tf,td->fd", attended_low, mixed_low, preferred_element_type=jnp.float32)
    attended_grad = (
        jnp.einsum("td,fd->tf", mixed_low, o_full, preferred_element_type=jnp.float32)
        .astype(jnp.bfloat16)
        .reshape(tok_rows, H, E)
    )
    delta_rows = jnp.sum(attended_grad.astype(jnp.float32) * attended, axis=-1)

    def grad_step(block_id, running):
        query_grad, key_grads, value_grads = running
        key_start = block_id * key_width
        scores, allowed, key_block = block_terms(
            q_rot,
            keys_all,
            seg_query,
            place_query,
            segment,
            places,
            key_start,
            key_width,
            score_scale,
        )
        value_block = lax.dynamic_slice_in_dim(values_all, key_start, key_width, 0)
        probs = jnp.where(allowed, jnp.exp(scores - log_total[..., None]), 0.0)
        value_piece = jnp.einsum(
            "thk,thd->kd",
            probs.astype(jnp.bfloat16),
            attended_grad,
            preferred_element_type=jnp.float32,
        )
        prob_grad = jnp.einsum(
            "thd,kd->thk", attended_grad, value_block, preferred_element_type=jnp.float32
        )
        score_grad = (probs * (prob_grad - delta_rows[..., None])).astype(jnp.bfloat16)
        query_grad = (
            query_grad
            + jnp.einsum("thk,kd->thd", score_grad, key_block, preferred_element_type=jnp.float32)
            * score_scale
        )
        key_piece = (
            jnp.einsum("thk,thd->kd", score_grad, q_rot, preferred_element_type=jnp.float32)
            * score_scale
        )
        key_grads = lax.dynamic_update_slice_in_dim(
            key_grads,
            lax.dynamic_slice_in_dim(key_grads, key_start, key_width, 0) + key_piece,
            key_start,
            0,
        )
        value_grads = lax.dynamic_update_slice_in_dim(
            value_grads,
            lax.dynamic_slice_in_dim(value_grads, key_start, key_width, 0) + value_piece,
            key_start,
            0,
        )
        return (query_grad, key_grads, value_grads)

    zero_keys = jnp.zeros((group_tokens, E), jnp.float32)
    query_grad, key_grads, value_grads = lax.fori_loop(
        first_block,
        last_block,
        grad_step,
        (jnp.zeros((tok_rows, H, E), jnp.float32), zero_keys, zero_keys),
    )
    key_own, value_own = (
        lax.psum_scatter(
            key_grads.astype(jnp.bfloat16), "seq", scatter_dimension=0, tiled=True
        ).astype(jnp.float32),
        lax.psum_scatter(
            value_grads.astype(jnp.bfloat16), "seq", scatter_dimension=0, tiled=True
        ).astype(jnp.float32),
    )
    key_rot_back = rotate_back(key_own, cosine, sine_tab)
    key_pre_grad, gain_key_grad = norm_back(key_pre, gain_key.astype(jnp.float32), key_rot_back)
    key_grad_low = key_pre_grad.astype(jnp.bfloat16)
    value_grad_low = value_own.astype(jnp.bfloat16)
    query_grad_low = (
        rotate_back(query_grad, cosine[:, None, :], sine_tab[:, None, :])
        .reshape(tok_rows, H * E)
        .astype(jnp.bfloat16)
    )
    qb_wgrad = jnp.einsum(
        "tr,tf->rf", latent_low, query_grad_low, preferred_element_type=jnp.float32
    )
    latent_low_grad = jnp.einsum(
        "tf,rf->tr", query_grad_low, qb_full, preferred_element_type=jnp.float32
    )
    latent_grad, gain_latent_grad = norm_back(
        latent, gain_latent.astype(jnp.float32), latent_low_grad
    )
    latent_grad_low = latent_grad.astype(jnp.bfloat16)
    qa_wgrad = jnp.einsum("td,tr->dr", normed, latent_grad_low, preferred_element_type=jnp.float32)
    k_wgrad = jnp.einsum("td,te->de", normed, key_grad_low, preferred_element_type=jnp.float32)
    v_wgrad = jnp.einsum("td,te->de", normed, value_grad_low, preferred_element_type=jnp.float32)
    normed_grad = (
        jnp.einsum("tr,dr->td", latent_grad_low, qa_full, preferred_element_type=jnp.float32)
        + jnp.einsum("te,de->td", key_grad_low, k_full, preferred_element_type=jnp.float32)
        + jnp.einsum("te,de->td", value_grad_low, v_full, preferred_element_type=jnp.float32)
    )
    input_part, gain_one_grad = norm_back(flat_rows, gain_one.astype(jnp.float32), normed_grad)
    input_grad = mixed_grad + input_part
    attn_shards = (
        lax.psum_scatter(gain_one_grad, ("seq", "dp"), scatter_dimension=0, tiled=True),
        lax.psum_scatter(qa_wgrad, ("seq", "dp"), scatter_dimension=0, tiled=True),
        lax.psum_scatter(gain_latent_grad, ("seq", "dp"), scatter_dimension=0, tiled=True),
        lax.psum_scatter(qb_wgrad, ("seq", "dp"), scatter_dimension=0, tiled=True),
        lax.psum_scatter(k_wgrad, ("seq", "dp"), scatter_dimension=0, tiled=True),
        lax.psum_scatter(gain_key_grad, ("seq", "dp"), scatter_dimension=0, tiled=True),
        lax.psum_scatter(v_wgrad, ("seq", "dp"), scatter_dimension=0, tiled=True),
        lax.psum_scatter(o_wgrad, ("seq", "dp"), scatter_dimension=0, tiled=True),
        lax.psum_scatter(gain_two_grad, ("seq", "dp"), scatter_dimension=0, tiled=True),
    )
    return (
        output_rows.reshape(1, tok_rows, D),
        input_grad.reshape(1, tok_rows, D),
        attn_shards[0],
        attn_shards[1],
        attn_shards[2],
        attn_shards[3],
        attn_shards[4],
        attn_shards[5],
        attn_shards[6],
        attn_shards[7],
        attn_shards[8],
        mlp_shards[0],
        mlp_shards[1],
        mlp_shards[2],
    )


def solution(mesh):
    return jax.shard_map(
        local,
        mesh=mesh,
        in_specs=(
            P("dp", "seq", None),
            P("dp", None),
            P("dp", "seq", None),
            P(("seq", "dp")),
            P(("seq", "dp"), None),
            P(("seq", "dp")),
            P(("seq", "dp"), None),
            P(("seq", "dp"), None),
            P(("seq", "dp")),
            P(("seq", "dp"), None),
            P(("seq", "dp"), None),
            P(("seq", "dp")),
            P(("seq", "dp"), None),
            P(("seq", "dp"), None),
            P(("seq", "dp"), None),
        ),
        out_specs=(
            P("dp", "seq", None),
            P("dp", "seq", None),
            P(("seq", "dp")),
            P(("seq", "dp"), None),
            P(("seq", "dp")),
            P(("seq", "dp"), None),
            P(("seq", "dp"), None),
            P(("seq", "dp")),
            P(("seq", "dp"), None),
            P(("seq", "dp"), None),
            P(("seq", "dp")),
            P(("seq", "dp"), None),
            P(("seq", "dp"), None),
            P(("seq", "dp"), None),
        ),
        check_vma=False,
    )
```

profile of v0, /device:TPU:0, one launch (start us, length us, event | category | flops | bytes accessed | tf_op | source)
XLA Modules:
  0.0 5459.8 jit_solution(9841759747237084181)
XLA Ops:
  7.2 1.6 convert_element_type.136
  8.9 1.5 convert_element_type.147
  10.5 1.6 convert_element_type.141
  12.2 1.8 convert_element_type.145
  17.5 2.4 convert_element_type.157
  21.6 42.1 all-reduce.9
  64.8 3.4 all-gather.9.cloned.1.call-done
  68.2 1.6 multiply_reduce_fusion.9
  71.2 9.8 all_gather.45
  80.9 43.6 all-gather.15.cloned.1.call-done
  124.5 1.5 convolution_convert_fusion.1
  126.1 10.8 all_gather.50
  136.8 52.3 all-gather.11.cloned.1.call-done
  189.2 3.0 multiply_reduce_fusion.6
  192.8 75.7 %all-gather.13.cloned.1.call-done = bf16[1024,4096]{1,0:T(8,128)(2,1)} async-done(((bf16[32,4096]{1,0:T(8,128)(2,1)}), bf16[1024,4096]{1,0:T(8,128)(2,1)}) %all-gather.13.cloned.1.call-update) | async-done | bytes 8388624 | tf_op jit(solution)/shard_map/all_gather | solution.py:115
  268.5 6.8 fusion.63
  276.4 1.8 while.36
  279.3 2.6 while.37
  279.6 2.2 convolution_add_fusion.6
  281.8 1.4 copy.74
  283.2 102.3 %all-gather.17.cloned.1.call-done = bf16[4096,2048]{1,0:T(8,128)(2,1)} async-done(((bf16[128,2048]{1,0:T(8,128)(2,1)}), bf16[4096,2048]{1,0:T(8,128)(2,1)}) %all-gather.17.cloned.1.call-update) | async-done | bytes 16777232 | tf_op jit(solution)/shard_map/all_gather | solution.py:119
  385.5 8.7 multiply_reduce_fusion.3
  396.1 135.4 %all-gather.19.cloned.1.call-done = bf16[2048,5632]{1,0:T(8,128)(2,1)} async-done(((bf16[64,5632]{1,0:T(8,128)(2,1)}), bf16[2048,5632]{1,0:T(8,128)(2,1)}) %all-gather.19.cloned.1.call-update) | async-done | bytes 23068688 | tf_op jit(solution)/shard_map/all_gather | solution.py:197
  531.6 12.6 fusion.74
  544.2 133.6 %all-gather.21.cloned.1.call-done = bf16[2048,5632]{1,0:T(8,128)(2,1)} async-done(((bf16[64,5632]{1,0:T(8,128)(2,1)}), bf16[2048,5632]{1,0:T(8,128)(2,1)}) %all-gather.21.cloned.1.call-update) | async-done | bytes 23068688 | tf_op jit(solution)/shard_map/all_gather | solution.py:198
  677.8 12.5 fusion.75
  690.2 133.7 %all-gather.23.cloned.1.call-done = bf16[5632,2048]{1,0:T(8,128)(2,1)} async-done(((bf16[176,2048]{1,0:T(8,128)(2,1)}), bf16[5632,2048]{1,0:T(8,128)(2,1)}) %all-gather.23.cloned.1.call-update) | async-done | bytes 23068688 | tf_op jit(solution)/shard_map/all_gather | solution.py:199
  824.0 15.5 multiply_convert_fusion
  839.5 13.0 fusion.76
  852.5 13.9 multiply_reduce_fusion.1
  866.5 2.8 bitcast_add_fusion
  869.3 12.7 convolution_convert_fusion
  882.1 2.4 copy.87
  884.9 1.6 broadcast.250
  888.6 7.9 while.38
  889.5 1.6 fusion.171
  891.9 2.3 fusion.172
  894.2 2.1 fusion.173
  896.5 2.2 convert_element_type.167
  899.7 46.0 reduce-scatter.11.cloned.1.call-done
  947.1 1.8 multiply_reduce_fusion.7
  949.9 1.8 fusion.80
  951.9 31.9 reduce-scatter.13.cloned.1.call-done
  983.7 2.6 fusion.81
  986.4 1.9 copy.78
  988.3 1.7 broadcast_multiply_fusion
  990.2 1.4 copy-done.11
  992.7 6.4 multiply_reduce_fusion.4
  999.2 4.7 fusion.79
  1004.0 8.3 fusion.62
  1013.8 13.2 fusion.54
  1028.5 17.9 fusion.82
  1047.8 18.1 fusion.83
  1067.6 17.9 fusion.70
  1086.7 11.9 fusion.38
  1100.3 1.8 fusion.51
  1102.1 39.9 all-reduce.8
  1145.6 117.9 %reduce-scatter.21.cloned.1.call-done = f32[64,256]{1,0:T(8,128)} async-done(((f32[2048,256]{1,0:T(8,128)}), f32[64,256]{1,0:T(8,128)}) %reduce-scatter.21.cloned.1.call-update) | async-done | bytes 65552 | tf_op jit(solution)/shard_map/reduce_scatter | solution.py:337
  1263.5 186.5 %reduce-scatter.15.cloned.1.call-done = f32[64,1024]{1,0:T(8,128)} async-done(((f32[2048,1024]{1,0:T(8,128)}), f32[64,1024]{1,0:T(8,128)}) %reduce-scatter.15.cloned.1.call-update) | async-done | bytes 262160 | tf_op jit(solution)/shard_map/reduce_scatter | solution.py:332
  1450.0 364.6 %reduce-scatter.17.cloned.1.call-done = f32[32,4096]{1,0:T(8,128)} async-done(((f32[1024,4096]{1,0:T(8,128)}), f32[32,4096]{1,0:T(8,128)}) %reduce-scatter.17.cloned.1.call-update) | async-done | bytes 524304 | tf_op jit(solution)/shard_map/reduce_scatter | solution.py:334
  1814.6 712.6 %reduce-scatter.23.cloned.1.call-done = f32[128,2048]{1,0:T(8,128)} async-done(((f32[4096,2048]{1,0:T(8,128)}), f32[128,2048]{1,0:T(8,128)}) %reduce-scatter.23.cloned.1.call-update) | async-done | bytes 1048592 | tf_op jit(solution)/shard_map/reduce_scatter | solution.py:338
  2527.2 974.5 %reduce-scatter.25.cloned.1.call-done = f32[64,5632]{1,0:T(8,128)} async-done(((f32[2048,5632]{1,0:T(8,128)}), f32[64,5632]{1,0:T(8,128)}) %reduce-scatter.25.cloned.1.call-update) | async-done | bytes 1441808 | tf_op jit(solution)/shard_map/reduce_scatter | solution.py:222
  3501.7 975.5 %reduce-scatter.27.cloned.1.call-done = f32[64,5632]{1,0:T(8,128)} async-done(((f32[2048,5632]{1,0:T(8,128)}), f32[64,5632]{1,0:T(8,128)}) %reduce-scatter.27.cloned.1.call-update) | async-done | bytes 1441808 | tf_op jit(solution)/shard_map/reduce_scatter | solution.py:223
  4477.2 975.5 %reduce-scatter.29.cloned.1.call-done = f32[176,2048]{1,0:T(8,128)} async-done(((f32[5632,2048]{1,0:T(8,128)}), f32[176,2048]{1,0:T(8,128)}) %reduce-scatter.29.cloned.1.call-update) | async-done | bytes 1441808 | tf_op jit(solution)/shard_map/reduce_scatter | solution.py:224
  (227 shorter events, 35.4 us)
Async XLA Ops:
  7.2 6.8 copy-start.34
  7.2 7.8 copy-start.30
  7.2 61.0 %all-gather.9.cloned.1.call-start = ((), (), s32[]{:S(2)}) async-start(), calls=%async_computation.10 | async-start | bytes 1081344 | tf_op jit(solution)/shard_map/all_gather | solution.py:116
  8.9 115.6 %all-gather.15.cloned.1.call-start = ((), (), s32[]{:S(2)}) async-start(), calls=%async_computation.13 | async-start | bytes 1081344 | tf_op jit(solution)/shard_map/all_gather | solution.py:118
  10.4 178.8 %all-gather.11.cloned.1.call-start = ((), (), s32[]{:S(2)}) async-start(), calls=%async_computation.11 | async-start | bytes 4325376 | tf_op jit(solution)/shard_map/all_gather | solution.py:113
  12.1 256.4 %all-gather.13.cloned.1.call-start = ((), (), s32[]{:S(2)}) async-start(), calls=%async_computation.12 | async-start | bytes 8650752 | tf_op jit(solution)/shard_map/all_gather | solution.py:115
  14.0 371.5 %all-gather.17.cloned.1.call-start = ((), (), s32[]{:S(2)}) async-start(), calls=%async_computation.14 | async-start | bytes 17301504 | tf_op jit(solution)/shard_map/all_gather | solution.py:119
  14.9 1.6 copy-start.31
  14.9 516.6 %all-gather.19.cloned.1.call-start = ((), (), s32[]{:S(2)}) async-start(), calls=%async_computation.15 | async-start | bytes 23789568 | tf_op jit(solution)/shard_map/all_gather | solution.py:197
  15.9 661.9 %all-gather.21.cloned.1.call-start = ((), (), s32[]{:S(2)}) async-start(), calls=%async_computation.16 | async-start | bytes 23789568 | tf_op jit(solution)/shard_map/all_gather | solution.py:198
  17.4 2.6 copy-start.46
  17.4 3.2 copy-start.48
  17.4 3.2 copy-start.49
  17.4 3.2 copy-start.50
  17.4 3.2 copy-start.51
  17.5 46.3 copy-start.9
  17.5 806.5 %all-gather.23.cloned.1.call-start = ((), (), s32[]{:S(2)}) async-start(), calls=%async_computation.17 | async-start | bytes 23789568 | tf_op jit(solution)/shard_map/all_gather | solution.py:199
  20.0 925.8 %reduce-scatter.11.cloned.1.call-start = ((), (), s32[]{:S(2)}) async-start(), calls=%async_computation.18 | async-start | bytes 589824 | tf_op jit(solution)/shard_map/reduce_scatter | solution.py:294
  63.7 6.1 copy-start.38
  64.5 6.4 copy-start.41
  64.7 124.4 %copy-start.4 = (bf16[128,2048]{1,0:T(8,128)(2,1)}, bf16[128,2048]{1,0:T(8,128)(2,1)S(1)}, u32[]{:S(2)}) copy-start(bf16[128,2048]{1,0:T(8,128)(2,1)S(1)} %fusion.44) | copy-start | bytes 1572868
  71.2 204.4 %copy-start.32 = (f32[128,256]{0,1:T(8,128)}, f32[128,256]{0,1:T(8,128)S(1)}, u32[]{:S(2)}) copy-start(f32[128,256]{0,1:T(8,128)S(1)} %copy.67) | copy-start | bytes 393220
  192.2 83.2 %copy-start.16 = (f32[128,1024]{1,0:T(8,128)}, f32[128,1024]{1,0:T(8,128)S(1)}, u32[]{:S(2)}) copy-start(f32[128,1024]{1,0:T(8,128)S(1)} %get-tuple-element.465) | copy-start | bytes 1572868
  839.5 13.0 copy-start.7
  882.1 2.4 copy-start.24
  884.9 3.8 copy-start
  884.9 3.7 copy-start.19
  889.5 1.7 copy-start.1
  891.9 4.4 copy-start.2
  896.5 2.3 copy-start.20
  898.7 50.1 copy-start.47
  898.7 51.2 copy-start.5
  898.7 85.0 %reduce-scatter.13.cloned.1.call-start = ((), (), s32[]{:S(2)}) async-start(), calls=%async_computation.19 | async-start | bytes 589824 | tf_op jit(solution)/shard_map/reduce_scatter | solution.py:297
  899.7 245.9 %reduce-scatter.19.cloned.1.call-start = ((), (), s32[]{:S(2)}) async-start(), calls=%async_computation.22 | async-start | bytes 2162688 | tf_op jit(solution)/shard_map/reduce_scatter | solution.py:335
  949.9 1.9 copy-start.35
  951.8 34.6 copy-start.3
  951.8 311.7 %reduce-scatter.21.cloned.1.call-start = ((), (), s32[]{:S(2)}) async-start(), calls=%async_computation.23 | async-start | bytes 2162688 | tf_op jit(solution)/shard_map/reduce_scatter | solution.py:337
  986.4 463.6 %reduce-scatter.15.cloned.1.call-start = ((), (), s32[]{:S(2)}) async-start(), calls=%async_computation.20 | async-start | bytes 8650752 | tf_op jit(solution)/shard_map/reduce_scatter | solution.py:332
  990.0 1.6 copy-start.11
  990.0 1.6 copy-start.33
  992.7 6.4 copy-start.45
  999.2 4.7 copy-start.28
  1003.9 810.7 %reduce-scatter.17.cloned.1.call-start = ((), (), s32[]{:S(2)}) async-start(), calls=%async_computation.21 | async-start | bytes 17301504 | tf_op jit(solution)/shard_map/reduce_scatter | solution.py:334
  1012.3 1.5 copy-start.15
  1012.3 1514.9 %reduce-scatter.23.cloned.1.call-start = ((), (), s32[]{:S(2)}) async-start(), calls=%async_computation.24 | async-start | bytes 34603008 | tf_op jit(solution)/shard_map/reduce_scatter | solution.py:338
  1027.0 1.5 copy-start.21
  1027.0 2474.7 %reduce-scatter.25.cloned.1.call-start = ((), (), s32[]{:S(2)}) async-start(), calls=%async_computation.25 | async-start | bytes 47579136 | tf_op jit(solution)/shard_map/reduce_scatter | solution.py:222
  1046.4 1.4 copy-start.22
  1046.5 3430.8 %reduce-scatter.27.cloned.1.call-start = ((), (), s32[]{:S(2)}) async-start(), calls=%async_computation.26 | async-start | bytes 47579136 | tf_op jit(solution)/shard_map/reduce_scatter | solution.py:223
  1065.9 1.4 copy-start.23
  1065.9 1.7 copy-start.25
  1065.9 4386.9 %reduce-scatter.29.cloned.1.call-start = ((), (), s32[]{:S(2)}) async-start(), calls=%async_computation.27 | async-start | bytes 47579136 | tf_op jit(solution)/shard_map/reduce_scatter | solution.py:224
  1086.6 11.9 copy-start.27
  1086.6 11.9 copy-start.37
  1086.7 12.4 copy-start.36
  1086.7 13.6 copy-start.13
  1098.6 1.2 copy-start.26
  1098.6 1.7 copy-start.10
  1098.6 1.7 copy-start.29
  1098.6 1.7 copy-start.39
  1098.6 1.7 copy-start.42
  1100.3 1.8 copy-start.40
  1100.3 1.8 copy-start.43
  1100.3 44.0 copy-start.44
  (6 other events, 6.3 us)
Sparse Core Ops, SparseCore 0:
  11.6 56.5 all-gather.8
  71.7 52.7 all-gather.14
  128.1 61.0 all-gather.10
  192.5 75.9 all-gather.12
  271.9 113.5 all-gather.16
  388.7 142.7 all-gather.18
  535.0 142.7 all-gather.20
  681.2 142.7 all-gather.22
  898.9 46.8 reduce-scatter.10
  949.5 34.1 reduce-scatter.12
  986.6 137.9 reduce-scatter.18
  1127.4 136.0 reduce-scatter.20
  1266.3 183.6 reduce-scatter.14
  1452.7 361.8 reduce-scatter.16
  1817.3 709.8 reduce-scatter.22
  2530.0 971.6 reduce-scatter.24
  3504.4 972.7 reduce-scatter.26
  4480.0 972.7 reduce-scatter.28
where the time goes:
time: 5470 us; the launch traced here: 5460 us
  waiting for transfers between devices  5070 us (93%)
  matrix products  217 us (4%)
  blocking collectives  102 us (2%)
    reduce_scatter x1, waiting for transfers between devices, local(): lax.psum_scatter(down_wgrad, ('seq', 'dp'), scatter_dimension=0, tiled=True)  976 us
    reduce_scatter x1, waiting for transfers between devices, local(): lax.psum_scatter(up_wgrad, ('seq', 'dp'), scatter_dimension=0, tiled=True)  976 us
    reduce_scatter x1, waiting for transfers between devices, local(): lax.psum_scatter(gate_wgrad, ('seq', 'dp'), scatter_dimension=0, tiled=True)  974 us
    reduce_scatter x1, waiting for transfers between devices, local(): lax.psum_scatter(o_wgrad, ('seq', 'dp'), scatter_dimension=0, tiled=True)  713 us
    reduce_scatter x1, waiting for transfers between devices, local(): lax.psum_scatter(qb_wgrad, ('seq', 'dp'), scatter_dimension=0, tiled=True)  365 us
    reduce_scatter x1, waiting for transfers between devices, local(): lax.psum_scatter(qa_wgrad, ('seq', 'dp'), scatter_dimension=0, tiled=True)  187 us
    all_gather x1, waiting for transfers between devices, local(): lax.all_gather(w_gate.astype(jnp.bfloat16), ('seq', 'dp'), axis=0, tiled=...  135 us
    all_gather x1, waiting for transfers between devices, local(): lax.all_gather(w_down.astype(jnp.bfloat16), ('seq', 'dp'), axis=0, tiled=...  134 us
  transfers between devices with their start and end apart: 18, of which 17 were waited for; matrix products, arithmetic and copies ran while one was open for 3% of the time, Pallas kernels for 0%

commit v1 on v0

v1 whole, which is shorter than its diff:
```python
import math

import jax
import jax.numpy as jnp
from jax import lax
from jax.sharding import PartitionSpec as P

D = 2048
H = 16
E = 256


eps_norm = 1e-06
big_negative = -1e30


def rms_scale(values, gain_vec):
    inverse = lax.rsqrt(jnp.mean(values * values, axis=-1, keepdims=True) + eps_norm)
    return values * inverse * gain_vec


def norm_back(values, gain_vec, upstream):
    inverse = lax.rsqrt(jnp.mean(values * values, axis=-1, keepdims=True) + eps_norm)
    gain_grad = jnp.sum(upstream * values * inverse, axis=0)
    scaled = upstream * gain_vec
    value_grad = inverse * scaled - values * (inverse * inverse * inverse) * jnp.mean(
        scaled * values, axis=-1, keepdims=True
    )
    return (value_grad, gain_grad)


def rotate(values, cosine, sine_tab):
    half_width = values.shape[-1] // 2
    turned = jnp.concatenate([-values[..., half_width:], values[..., :half_width]], axis=-1)
    return values * cosine + turned * sine_tab


def rotate_back(upstream, cosine, sine_tab):
    half_width = upstream.shape[-1] // 2
    weighted = upstream * sine_tab
    turned = jnp.concatenate([weighted[..., half_width:], -weighted[..., :half_width]], axis=-1)
    return upstream * cosine + turned


def layout(seq_lengths, group_tokens):
    seq_ends = jnp.cumsum(seq_lengths)
    places = jnp.arange(group_tokens, dtype=jnp.int32)
    passed = places[:, None] >= seq_ends[None, :]
    segment = jnp.sum(passed.astype(jnp.int32), axis=1)
    starts = jnp.sum(jnp.where(passed, seq_lengths[None, :], 0), axis=1)
    return (segment, places, places - starts)


def rope_tables(offsets, width):
    half_width = width // 2
    frequency = jnp.exp(
        jnp.arange(half_width, dtype=jnp.float32) * (-2.0 * math.log(10000.0) / width)
    )
    angles = offsets.astype(jnp.float32)[:, None] * frequency[None, :]
    angles = jnp.concatenate([angles, angles], axis=-1)
    return (jnp.cos(angles), jnp.sin(angles))


def gather_columns(weight, parts):
    rows, cols = weight.shape
    low = weight.astype(jnp.bfloat16).reshape(rows, parts, cols // parts)
    mine = lax.all_to_all(low, "seq", split_axis=1, concat_axis=0, tiled=False)
    mine = mine.reshape(parts, rows, cols // parts)
    full = lax.all_gather(mine, "dp", axis=1, tiled=False)
    return full.reshape(-1, cols // parts)


def gather_rows(weight):
    return lax.all_gather(weight.astype(jnp.bfloat16), "dp", axis=0, tiled=True)


def scatter_columns(grad, parts, groups):
    rows, cols = grad.shape
    piece = rows // (parts * groups)
    low = grad.astype(jnp.bfloat16).reshape(parts, groups, piece, cols)
    low = jnp.transpose(low, (1, 0, 2, 3)).reshape(rows, cols)
    own = lax.psum_scatter(low, "dp", scatter_dimension=0, tiled=True).reshape(parts, piece, cols)
    back = lax.all_to_all(own, "seq", split_axis=0, concat_axis=1, tiled=False)
    return back.reshape(piece, parts * cols).astype(jnp.float32)


def scatter_rows(grad):
    return lax.psum_scatter(
        grad.astype(jnp.bfloat16), "dp", scatter_dimension=0, tiled=True
    ).astype(jnp.float32)


def seq_gather(rows):
    return lax.all_gather(rows, "seq", axis=0, tiled=True)


def seq_scatter(rows):
    return lax.psum_scatter(
        rows.astype(jnp.bfloat16), "seq", scatter_dimension=0, tiled=True
    ).astype(jnp.float32)


def dot(left, right):
    return jnp.dot(left, right, preferred_element_type=jnp.float32)


def local(
    block_input,
    lengths,
    cotangent,
    attn_gain,
    w_qa,
    q_gain,
    w_qb,
    w_k,
    k_gain,
    w_v,
    w_o,
    mlp_gain,
    w_gate,
    w_up,
    w_down,
):
    tok_rows = block_input.shape[1]
    parts = lax.axis_size("seq")
    groups = lax.axis_size("dp")
    heads = H // parts
    group_tokens = tok_rows * parts
    first_row = lax.axis_index("seq") * tok_rows
    segment, places, offsets = layout(lengths[0], group_tokens)
    cos_all, sin_all = rope_tables(offsets, E)
    cosine = lax.dynamic_slice_in_dim(cos_all, first_row, tok_rows, 0)
    sine_tab = lax.dynamic_slice_in_dim(sin_all, first_row, tok_rows, 0)
    score_scale = 1.0 / math.sqrt(E)
    flat_rows = block_input.reshape(tok_rows, D)
    out_grad = cotangent.reshape(tok_rows, D)
    both = ("seq", "dp")
    rank = w_qa.shape[1]

    gains = jnp.concatenate([attn_gain, q_gain, k_gain, mlp_gain]).astype(jnp.bfloat16)
    gains = lax.all_gather(gains, both, axis=0, tiled=False).astype(jnp.float32)
    n1, n2, n3 = attn_gain.shape[0], q_gain.shape[0], k_gain.shape[0]
    gain_one = gains[:, :n1].reshape(-1)
    gain_latent = gains[:, n1 : n1 + n2].reshape(-1)
    gain_key = gains[:, n1 + n2 : n1 + n2 + n3].reshape(-1)
    gain_two = gains[:, n1 + n2 + n3 :].reshape(-1)

    w_in = jnp.concatenate([w_qa, w_k, w_v], axis=1).astype(jnp.bfloat16)
    w_in = lax.all_gather(w_in, both, axis=0, tiled=True)
    qb_cols = gather_columns(w_qb, parts)
    o_rows = gather_rows(w_o)
    gate_cols = gather_columns(w_gate, parts)
    up_cols = gather_columns(w_up, parts)
    down_rows = gather_rows(w_down)

    normed = rms_scale(flat_rows, gain_one).astype(jnp.bfloat16)
    projected = dot(normed, w_in)
    latent, key_pre, value_pre = (
        projected[:, :rank],
        projected[:, rank : rank + E],
        projected[:, rank + E :],
    )
    latent_low = rms_scale(latent, gain_latent).astype(jnp.bfloat16)
    key_low = rotate(rms_scale(key_pre, gain_key), cosine, sine_tab).astype(jnp.bfloat16)
    value_low = value_pre.astype(jnp.bfloat16)
    gathered = seq_gather(jnp.concatenate([latent_low, key_low, value_low], axis=1))
    latent_all = gathered[:, :rank]
    keys_all = gathered[:, rank : rank + E]
    values_all = gathered[:, rank + E :]
    grad_all = seq_gather(out_grad.astype(jnp.bfloat16))

    query = dot(latent_all, qb_cols).reshape(group_tokens, heads, E)
    query = jnp.transpose(query, (1, 0, 2))
    q_rot = rotate(query, cos_all[None], sin_all[None]).astype(jnp.bfloat16)
    allowed = (segment[:, None] == segment[None, :]) & (places[None, :] <= places[:, None])
    scores = (
        jnp.einsum("htd,kd->htk", q_rot, keys_all, preferred_element_type=jnp.float32)
        * score_scale
    )
    scores = jnp.where(allowed[None], scores, big_negative)
    shifted = jnp.exp(scores - jnp.max(scores, axis=-1, keepdims=True))
    probs = shifted / jnp.sum(shifted, axis=-1, keepdims=True)
    probs_low = probs.astype(jnp.bfloat16)
    attended = jnp.einsum("htk,kd->htd", probs_low, values_all, preferred_element_type=jnp.float32)
    attended_low = jnp.transpose(attended.astype(jnp.bfloat16), (1, 0, 2)).reshape(
        group_tokens, heads * E
    )
    mixed_rows = flat_rows + seq_scatter(dot(attended_low, o_rows))
    normed_two = rms_scale(mixed_rows, gain_two).astype(jnp.bfloat16)
    two_all = seq_gather(normed_two)

    gate_act = dot(two_all, gate_cols)
    up_act = dot(two_all, up_cols)
    sigmoid_gate = jax.nn.sigmoid(gate_act)
    hidden = (gate_act * sigmoid_gate * up_act).astype(jnp.bfloat16)
    hidden_grad = jnp.einsum("td,fd->tf", grad_all, down_rows, preferred_element_type=jnp.float32)
    gate_grad = (
        hidden_grad * up_act * (sigmoid_gate * (1.0 + gate_act * (1.0 - sigmoid_gate)))
    ).astype(jnp.bfloat16)
    up_grad = (hidden_grad * (gate_act * sigmoid_gate)).astype(jnp.bfloat16)
    two_grad = seq_scatter(
        jnp.einsum("tf,df->td", gate_grad, gate_cols, preferred_element_type=jnp.float32)
        + jnp.einsum("tf,df->td", up_grad, up_cols, preferred_element_type=jnp.float32)
    )
    output_rows = mixed_rows + seq_scatter(dot(hidden, down_rows))
    down_shard = scatter_rows(
        jnp.einsum("tf,td->fd", hidden, grad_all, preferred_element_type=jnp.float32)
    )
    gate_shard = scatter_columns(
        jnp.einsum("td,tf->df", two_all, gate_grad, preferred_element_type=jnp.float32),
        parts,
        groups,
    )
    up_shard = scatter_columns(
        jnp.einsum("td,tf->df", two_all, up_grad, preferred_element_type=jnp.float32),
        parts,
        groups,
    )

    mixed_part, gain_two_grad = norm_back(mixed_rows, gain_two, two_grad)
    mixed_grad = out_grad + mixed_part
    mixed_all = seq_gather(mixed_grad.astype(jnp.bfloat16))
    o_shard = scatter_rows(
        jnp.einsum("tf,td->fd", attended_low, mixed_all, preferred_element_type=jnp.float32)
    )
    att_grad = jnp.einsum("td,fd->tf", mixed_all, o_rows, preferred_element_type=jnp.float32)
    att_grad = jnp.transpose(
        att_grad.astype(jnp.bfloat16).reshape(group_tokens, heads, E), (1, 0, 2)
    )
    delta_rows = jnp.sum(att_grad.astype(jnp.float32) * attended, axis=-1)
    value_grads = jnp.einsum(
        "htk,htd->kd", probs_low, att_grad, preferred_element_type=jnp.float32
    )
    prob_grad = jnp.einsum("htd,kd->htk", att_grad, values_all, preferred_element_type=jnp.float32)
    score_grad = (probs * (prob_grad - delta_rows[..., None])).astype(jnp.bfloat16)
    query_grad = (
        jnp.einsum("htk,kd->htd", score_grad, keys_all, preferred_element_type=jnp.float32)
        * score_scale
    )
    key_grads = (
        jnp.einsum("htk,htd->kd", score_grad, q_rot, preferred_element_type=jnp.float32)
        * score_scale
    )
    query_grad = rotate_back(query_grad, cos_all[None], sin_all[None]).astype(jnp.bfloat16)
    query_grad = jnp.transpose(query_grad, (1, 0, 2)).reshape(group_tokens, heads * E)
    qb_shard = scatter_columns(
        jnp.einsum("tr,tf->rf", latent_all, query_grad, preferred_element_type=jnp.float32),
        parts,
        groups,
    )
    latent_part = jnp.einsum("tf,rf->tr", query_grad, qb_cols, preferred_element_type=jnp.float32)
    own = seq_scatter(jnp.concatenate([latent_part, key_grads, value_grads], axis=1))
    latent_grad, gain_latent_grad = norm_back(latent, gain_latent, own[:, :rank])
    key_back = rotate_back(own[:, rank : rank + E], cosine, sine_tab)
    key_grad, gain_key_grad = norm_back(key_pre, gain_key, key_back)
    in_grad = jnp.concatenate([latent_grad, key_grad, own[:, rank + E :]], axis=1).astype(
        jnp.bfloat16
    )
    in_wgrad = jnp.einsum("td,tr->dr", normed, in_grad, preferred_element_type=jnp.float32)
    in_shard = lax.psum_scatter(
        in_wgrad.astype(jnp.bfloat16), both, scatter_dimension=0, tiled=True
    ).astype(jnp.float32)
    normed_grad = jnp.einsum("tr,dr->td", in_grad, w_in, preferred_element_type=jnp.float32)
    input_part, gain_one_grad = norm_back(flat_rows, gain_one, normed_grad)
    input_grad = mixed_grad + input_part

    devices = parts * groups
    gain_grads = jnp.concatenate(
        [
            gain_one_grad.reshape(devices, -1),
            gain_latent_grad.reshape(devices, -1),
            gain_key_grad.reshape(devices, -1),
            gain_two_grad.reshape(devices, -1),
        ],
        axis=1,
    )
    gain_own = lax.psum_scatter(gain_grads, both, scatter_dimension=0, tiled=False)
    return (
        output_rows.reshape(1, tok_rows, D),
        input_grad.reshape(1, tok_rows, D),
        gain_own[:n1],
        in_shard[:, :rank],
        gain_own[n1 : n1 + n2],
        qb_shard,
        in_shard[:, rank : rank + E],
        gain_own[n1 + n2 : n1 + n2 + n3],
        in_shard[:, rank + E :],
        o_shard,
        gain_own[n1 + n2 + n3 :],
        gate_shard,
        up_shard,
        down_shard,
    )


def solution(mesh):
    return jax.shard_map(
        local,
        mesh=mesh,
        in_specs=(
            P("dp", "seq", None),
            P("dp", None),
            P("dp", "seq", None),
            P(("seq", "dp")),
            P(("seq", "dp"), None),
            P(("seq", "dp")),
            P(("seq", "dp"), None),
            P(("seq", "dp"), None),
            P(("seq", "dp")),
            P(("seq", "dp"), None),
            P(("seq", "dp"), None),
            P(("seq", "dp")),
            P(("seq", "dp"), None),
            P(("seq", "dp"), None),
            P(("seq", "dp"), None),
        ),
        out_specs=(
            P("dp", "seq", None),
            P("dp", "seq", None),
            P(("seq", "dp")),
            P(("seq", "dp"), None),
            P(("seq", "dp")),
            P(("seq", "dp"), None),
            P(("seq", "dp"), None),
            P(("seq", "dp")),
            P(("seq", "dp"), None),
            P(("seq", "dp"), None),
            P(("seq", "dp")),
            P(("seq", "dp"), None),
            P(("seq", "dp"), None),
            P(("seq", "dp"), None),
        ),
        check_vma=False,
    )
```

time: 5470 us -> 1160 us (0.21)
  waiting for transfers between devices: 5070 us -> 738 us
  matrix products: 217 us -> 121 us
    reduce_scatter x10, waiting for transfers between devices: 4390 us -> 391 us  [the longest x3 129 us: scatter_columns(): lax.psum_scatter(low, 'dp', scatter_dimension=0, tiled=True)]
    all_gather x8 -> x10, waiting for transfers between devices: 680 us -> 342 us  [the longest x4 137 us: seq_gather(): return lax.all_gather(rows, 'seq', axis=0, tiled=True)]
    dot_general x30 -> x23, matrix products: 211 us -> 112 us  [the longest x6 33.7 us: dot(): return jnp.dot(left, right, preferred_element_type=jnp.float32)]
  transfers between devices with their start and end apart: 18 -> 24, of which waited for: 17 -> 19; matrix products, arithmetic and copies ran while one was open for 3% -> 15% of each run, Pallas kernels for 0% -> 0%
where the time goes in v1:
time: 1160 us; the launch traced here: 1150 us
  waiting for transfers between devices  738 us (64%)
  blocking collectives  148 us (13%)
  matrix products  121 us (10%)
  local copies, waits for them, and re-layouts  60.4 us (5%)
  other arithmetic  51.2 us (4%)
  starting transfers between devices  18.7 us (2%)
  between operations  15.7 us (1%)
    all_gather x4, waiting for transfers between devices, seq_gather(): return lax.all_gather(rows, 'seq', axis=0, tiled=True)  137 us
    all_gather x3, waiting for transfers between devices, gather_columns(): full = lax.all_gather(mine, 'dp', axis=1, tiled=False)  131 us
    reduce_scatter x3, waiting for transfers between devices, scatter_columns(): lax.psum_scatter(low, 'dp', scatter_dimension=0, tiled=True)  129 us
    reduce_scatter x4, waiting for transfers between devices, seq_scatter(): lax.psum_scatter(rows.astype(jnp.bfloat16), 'seq', scatter_dimension=0, t...  111 us
    reduce_scatter x2, waiting for transfers between devices, scatter_rows(): lax.psum_scatter(grad.astype(jnp.bfloat16), 'dp', scatter_dimension=0, ti...  86.5 us
    all_gather x2, waiting for transfers between devices, gather_rows(): return lax.all_gather(weight.astype(jnp.bfloat16), 'dp', axis=0, tiled=True)  72.8 us
    all_gather x1, blocking collectives, local(): gains = lax.all_gather(gains, both, axis=0, tiled=False).astype(jnp.float32)  69.3 us
    reduce_scatter x1, waiting for transfers between devices, local(): lax.psum_scatter(in_wgrad.astype(jnp.bfloat16), both, scatter_dimension=0...  64.9 us
  transfers between devices with their start and end apart: 24, of which 19 were waited for; matrix products, arithmetic and copies ran while one was open for 15% of the time, Pallas kernels for 0%

profile of v1, /device:TPU:0, one launch (start us, length us, event | category | flops | bytes accessed | tf_op | source)
XLA Modules:
  0.0 1152.4 jit_solution(2403636363487769444)
XLA Ops:
  12.6 5.2 all-to-all-start
  18.0 69.3 %all-gather.3 = bf16[32,1,168]{2,1,0:T(2,128)(2,1)S(1)} all-gather(bf16[1,1,168]{2,1,0:T(2,128)(2,1)S(1)} %maximum_bitcast_fusion), channel_id=1, replica_groups=mesh['seq'=8,'dp'=4] {'seq','dp'}, dimensions={0}, use_global_device_ids=true | all-gather | bytes 11088 | tf_op jit(solution)/shard_map/all_gather | solution.py:141
  87.8 4.6 broadcast_multiply_fusion.2
  94.4 3.8 fusion.57
  100.7 2.1 convert_element_type.187
  106.3 12.4 %all-gather.29.cloned.1.call-done = bf16[8,4,32,1,512]{4,2,3,0,1:T(8,128)(2,1)} async-done(((bf16[8,1,32,1,512]{4,2,3,0,1:T(8,128)(2,1)}), bf16[8,4,32,1,512]{4,2,3,0,1:T(8,128)(2,1)}) %all-gather.29.cloned.1.call-update) | async-done | bytes 1048592 | tf_op jit(solution)/shard_map/all_gather | solution.py:69
  121.3 31.7 %all-gather.17.cloned.1.call-done = bf16[1024,1536]{1,0:T(8,128)(2,1)} async-done(((bf16[128,1536]{1,0:T(8,128)(2,1)}), bf16[1024,1536]{1,0:T(8,128)(2,1)}) %all-gather.17.cloned.1.call-update) | async-done | bytes 3145744 | tf_op jit(solution)/shard_map/all_gather | solution.py:94
  153.0 3.1 fusion.16
  158.2 8.2 fusion.65
  166.4 4.7 fusion.6
  171.1 1.9 copy-done.1
  173.0 3.7 fusion.66
  176.7 24.3 %all-gather.19.cloned.1.call-done = bf16[512,2048]{1,0:T(8,128)(2,1)} async-done(((bf16[128,2048]{1,0:T(8,128)(2,1)}), bf16[512,2048]{1,0:T(8,128)(2,1)}) %all-gather.19.cloned.1.call-update) | async-done | bytes 2097168 | tf_op jit(solution)/shard_map/all_gather | solution.py:74
  201.0 5.9 convolution_convert_fusion.2
  209.3 16.1 %all_to_all.72 = bf16[1,64,8,704]{3,1,0,2:T(8,128)(2,1)} all-to-all(bf16[1,64,8,704]{3,1,0,2:T(8,128)(2,1)S(1)} %copy.212), channel_id=1, replica_groups=mesh['seq'=8,'dp'=4] {'seq'}, dimensions={2} | all-to-all | bytes 1441792 | tf_op jit(solution)/shard_map/all_to_all | solution.py:67
  227.7 23.2 %all_to_all.73 = bf16[1,64,8,704]{3,1,0,2:T(8,128)(2,1)} all-to-all(bf16[1,64,8,704]{3,1,0,2:T(8,128)(2,1)S(1)} %copy.215), channel_id=1, replica_groups=mesh['seq'=8,'dp'=4] {'seq'}, dimensions={2} | all-to-all | bytes 1441792 | tf_op jit(solution)/shard_map/all_to_all | solution.py:67
  251.0 14.6 %reduce-scatter.11.cloned.1.call-done = bf16[128,2048]{1,0:T(8,128)(2,1)} async-done(((bf16[1024,2048]{1,0:T(8,128)(2,1)}), bf16[128,2048]{1,0:T(8,128)(2,1)}) %reduce-scatter.11.cloned.1.call-update) | async-done | bytes 524304 | tf_op jit(solution)/shard_map/reduce_scatter | solution.py:98
  267.9 2.3 convert_element_type.194
  271.6 59.0 %all-gather.31.cloned.1.call-done = bf16[8,4,64,1,704]{4,2,3,0,1:T(8,128)(2,1)} async-done(((bf16[8,1,64,1,704]{4,2,3,0,1:T(8,128)(2,1)}), bf16[8,4,64,1,704]{4,2,3,0,1:T(8,128)(2,1)}) %all-gather.31.cloned.1.call-update) | async-done | bytes 2883600 | tf_op jit(solution)/shard_map/all_gather | solution.py:69
  330.6 3.8 copy.214
  334.5 60.0 %all-gather.33.cloned.1.call-done = bf16[8,4,64,1,704]{4,2,3,0,1:T(8,128)(2,1)} async-done(((bf16[8,1,64,1,704]{4,2,3,0,1:T(8,128)(2,1)}), bf16[8,4,64,1,704]{4,2,3,0,1:T(8,128)(2,1)}) %all-gather.33.cloned.1.call-update) | async-done | bytes 2883600 | tf_op jit(solution)/shard_map/all_gather | solution.py:69
  394.5 3.8 copy.217
  398.3 34.2 %all-gather.21.cloned.1.call-done = bf16[1024,2048]{1,0:T(8,128)(2,1)} async-done(((bf16[128,2048]{1,0:T(8,128)(2,1)}), bf16[1024,2048]{1,0:T(8,128)(2,1)}) %all-gather.21.cloned.1.call-update) | async-done | bytes 4194320 | tf_op jit(solution)/shard_map/all_gather | solution.py:94
  432.5 8.1 fusion.69
  440.6 4.9 fusion.68
  445.4 48.5 %all-gather.23.cloned.1.call-done = bf16[704,2048]{1,0:T(8,128)(2,1)} async-done(((bf16[176,2048]{1,0:T(8,128)(2,1)}), bf16[704,2048]{1,0:T(8,128)(2,1)}) %all-gather.23.cloned.1.call-update) | async-done | bytes 2883600 | tf_op jit(solution)/shard_map/all_gather | solution.py:74
  493.9 37.9 %all-gather.25.cloned.1.call-done = bf16[1024,2048]{1,0:T(8,128)(2,1)} async-done(((bf16[128,2048]{1,0:T(8,128)(2,1)}), bf16[1024,2048]{1,0:T(8,128)(2,1)}) %all-gather.25.cloned.1.call-update) | async-done | bytes 4194320 | tf_op jit(solution)/shard_map/all_gather | solution.py:94
  531.8 10.0 multiply_convert_fusion.1
  541.9 3.7 fusion.70
  545.6 5.2 add_convert_fusion
  550.9 7.8 convolution_convert_fusion.1
  558.8 43.5 %reduce-scatter.15.cloned.1.call-done = bf16[128,2048]{1,0:T(8,128)(2,1)} async-done(((bf16[1024,2048]{1,0:T(8,128)(2,1)}), bf16[128,2048]{1,0:T(8,128)(2,1)}) %reduce-scatter.15.cloned.1.call-update) | async-done | bytes 524304 | tf_op jit(solution)/shard_map/reduce_scatter | solution.py:98
  603.7 53.2 %reduce-scatter.13.cloned.1.call-done = bf16[128,2048]{1,0:T(8,128)(2,1)} async-done(((bf16[1024,2048]{1,0:T(8,128)(2,1)}), bf16[128,2048]{1,0:T(8,128)(2,1)}) %reduce-scatter.13.cloned.1.call-update) | async-done | bytes 524304 | tf_op jit(solution)/shard_map/reduce_scatter | solution.py:98
  656.8 3.1 fusion.59
  660.3 2.6 copy.222
  663.2 33.7 %all-gather.27.cloned.1.call-done = bf16[1024,2048]{1,0:T(8,128)(2,1)} async-done(((bf16[128,2048]{1,0:T(8,128)(2,1)}), bf16[1024,2048]{1,0:T(8,128)(2,1)}) %all-gather.27.cloned.1.call-update) | async-done | bytes 4194320 | tf_op jit(solution)/shard_map/all_gather | solution.py:94
  696.9 6.0 multiply_reduce_fusion
  704.2 4.9 multiply_convert_fusion
  710.5 2.4 broadcast_multiply_fusion
  719.8 6.6 convolution_convert_fusion.3
  726.4 4.7 copy.236
  731.1 4.0 copy.237
  736.4 6.7 convolution_convert_fusion.4
  743.1 4.6 copy.232
  747.7 3.9 copy.233
  753.0 6.7 convolution_convert_fusion.5
  759.8 2.9 fusion.19
  764.3 5.9 convolution_convert_fusion.6
  776.8 4.6 convolution_convert_fusion
  781.4 45.9 %reduce-scatter.27.cloned.1.call-done = bf16[512,704]{1,0:T(8,128)(2,1)} async-done(((bf16[2048,704]{1,0:T(8,128)(2,1)}), bf16[512,704]{1,0:T(8,128)(2,1)}) %reduce-scatter.27.cloned.1.call-update) | async-done | bytes 720912 | tf_op jit(solution)/shard_map/reduce_scatter | solution.py:82
  827.3 3.7 all-to-all-start.5
  831.0 58.8 %reduce-scatter.25.cloned.1.call-done = bf16[512,704]{1,0:T(8,128)(2,1)} async-done(((bf16[2048,704]{1,0:T(8,128)(2,1)}), bf16[512,704]{1,0:T(8,128)(2,1)}) %reduce-scatter.25.cloned.1.call-update) | async-done | bytes 720912 | tf_op jit(solution)/shard_map/reduce_scatter | solution.py:82
  889.8 3.7 all-to-all-start.4
  893.5 54.7 %reduce-scatter.29.cloned.1.call-done = bf16[176,2048]{1,0:T(8,128)(2,1)} async-done(((bf16[704,2048]{1,0:T(8,128)(2,1)}), bf16[176,2048]{1,0:T(8,128)(2,1)}) %reduce-scatter.29.cloned.1.call-update) | async-done | bytes 720912 | tf_op jit(solution)/shard_map/reduce_scatter | solution.py:88
  948.2 2.4 convert_element_type.228
  954.0 24.0 %reduce-scatter.21.cloned.1.call-done = bf16[256,512]{1,0:T(8,128)(2,1)} async-done(((bf16[1024,512]{1,0:T(8,128)(2,1)}), bf16[256,512]{1,0:T(8,128)(2,1)}) %reduce-scatter.21.cloned.1.call-update) | async-done | bytes 262160 | tf_op jit(solution)/shard_map/reduce_scatter | solution.py:82
  978.0 4.3 all-to-all-start.3
  985.0 4.2 all-to-all-done.3
  991.1 31.8 %reduce-scatter.23.cloned.1.call-done = bf16[128,2048]{1,0:T(8,128)(2,1)} async-done(((bf16[512,2048]{1,0:T(8,128)(2,1)}), bf16[128,2048]{1,0:T(8,128)(2,1)}) %reduce-scatter.23.cloned.1.call-update) | async-done | bytes 524304 | tf_op jit(solution)/shard_map/reduce_scatter | solution.py:88
  1022.9 2.1 convert_element_type.216
  1025.0 5.6 fusion.43
  1033.0 39.7 %all-reduce = f32[32,168]{1,0:T(8,128)S(1)} all-reduce(f32[32,168]{1,0:T(8,128)S(1)} %pad_maximum_fusion.7), channel_id=9, replica_groups=mesh['seq'=8,'dp'=4] {'seq','dp'}, use_global_device_ids=true, to_apply=%region_22.23.clone | all-reduce | flops 5376 | bytes 43008
  1075.2 2.0 fusion.40
  1077.2 64.9 %reduce-scatter.19.cloned.1.call-done = bf16[64,1536]{1,0:T(8,128)(2,1)} async-done(((bf16[2048,1536]{1,0:T(8,128)(2,1)}), bf16[64,1536]{1,0:T(8,128)(2,1)}) %reduce-scatter.19.cloned.1.call-update) | async-done | bytes 196624 | tf_op jit(solution)/shard_map/reduce_scatter | solution.py:260
  (234 shorter events, 65.2 us)
Async XLA Ops:
  7.2 10.6 copy-start.42
  7.2 10.7 copy-start.43
  7.2 10.7 copy-start.39
  7.2 10.7 copy-start.40
  7.2 80.1 %copy-start.38 = (s32[1,4]{1,0:T(1,128)S(1)}, s32[1,4]{1,0:T(1,128)}, u32[]{:S(2)}) copy-start(s32[1,4]{1,0:T(1,128)} %param.16) | copy-start | bytes 52
  7.2 87.1 %all-gather.15.cloned.1.call-start = ((), (), s32[]{:S(2)}) async-start(), calls=%async_computation.16 | async-start | bytes 6488064 | tf_op jit(solution)/shard_map/all_gather | solution.py:149
  11.8 80.6 %copy-start = (f32[1,128,2048]{2,1,0:T(8,128)S(1)}, f32[1,128,2048]{2,1,0:T(8,128)}, u32[]{:S(2)}) copy-start(f32[1,128,2048]{2,1,0:T(8,128)} %param.15) | copy-start | bytes 3145732
  12.6 80.9 %all-to-all-start = ((bf16[1,32,8,512]{3,1,0,2:T(8,128)(2,1)}), bf16[1,32,8,512]{3,1,0,2:T(8,128)(2,1)S(1)}, u32[]{:S(2)}, u32[]{:S(2)}) async-start(bf16[1,32,8,512]{3,1,0,2:T(8,128)(2,1)} %copy.203), calls=%async_computation | async-start | bytes 524288 | tf_op jit(solution)/shard_map/all_to_all | solution.py:67
  17.8 100.9 %all-gather.29.cloned.1.call-start = ((), (), s32[]{:S(2)}) async-start(), calls=%async_computation.33 | async-start | bytes 1310720 | tf_op jit(solution)/shard_map/all_gather | solution.py:69
  92.4 12.3 %copy-start.6 = (f32[1024,256]{1,0:T(8,128)}, f32[1024,256]{1,0:T(8,128)S(1)}, u32[]{:S(2)}) copy-start(f32[1024,256]{1,0:T(8,128)S(1)} %get-tuple-element.39) | copy-start | bytes 3145732
  92.4 13.6 %copy-start.5 = (f32[1024,256]{1,0:T(8,128)}, f32[1024,256]{1,0:T(8,128)S(1)}, u32[]{:S(2)}) copy-start(f32[1024,256]{1,0:T(8,128)S(1)} %get-tuple-element.40) | copy-start | bytes 3145732
  92.8 13.4 %copy-start.28 = (f32[256]{0:T(256)}, f32[256]{0:T(256)S(1)}, u32[]{:S(2)}) copy-start(f32[256]{0:T(256)S(1)} %mul.448) | copy-start | bytes 3076
  92.9 13.4 %copy-start.26 = (f32[1024]{0:T(1024)}, f32[1024]{0:T(1024)S(1)}, u32[]{:S(2)}) copy-start(f32[1024]{0:T(1024)S(1)} %mul.442) | copy-start | bytes 12292
  93.0 13.3 %copy-start.24 = (f32[2048]{0:T(1024)}, f32[2048]{0:T(1024)S(1)}, u32[]{:S(2)}) copy-start(f32[2048]{0:T(1024)S(1)} %mul.436) | copy-start | bytes 24580
  93.5 12.8 %copy-start.30 = (f32[128]{0:T(128)}, f32[128]{0:T(128)S(1)}, u32[]{:S(2)}) copy-start(f32[128]{0:T(128)S(1)} %get-tuple-element.52) | copy-start | bytes 1540
  94.3 58.8 %all-gather.17.cloned.1.call-start = ((), (), s32[]{:S(2)}) async-start(), calls=%async_computation.17 | async-start | bytes 3538944 | tf_op jit(solution)/shard_map/all_gather | solution.py:94
  99.0 7.0 copy-start.34
  99.5 6.4 copy-start.32
  100.6 100.3 %all-gather.19.cloned.1.call-start = ((), (), s32[]{:S(2)}) async-start(), calls=%async_computation.18 | async-start | bytes 2621440 | tf_op jit(solution)/shard_map/all_gather | solution.py:74
  102.8 162.8 %reduce-scatter.11.cloned.1.call-start = ((), (), s32[]{:S(2)}) async-start(), calls=%async_computation.19 | async-start | bytes 4718592 | tf_op jit(solution)/shard_map/reduce_scatter | solution.py:98
  120.0 36.2 %copy-start.10 = (bf16[8,4,32,1,512]{4,2,1,0,3:T(8,128)(2,1)}, bf16[8,4,32,1,512]{4,2,1,0,3:T(8,128)(2,1)S(1)}, u32[]{:S(2)}) copy-start(bf16[8,4,32,1,512]{4,2,1,0,3:T(8,128)(2,1)S(1)} %copy.205) | copy-start | bytes 3145732
  158.2 8.2 copy-start.21
  171.1 1.9 copy-start.1
  176.7 30.3 %copy-start.19 = (bf16[2,1024,256]{1,2,0:T(8,128)(2,1)}, bf16[2,1024,256]{1,2,0:T(8,128)(2,1)S(1)}, u32[]{:S(2)}) copy-start(bf16[2,1024,256]{1,2,0:T(8,128)(2,1)S(1)} %get-tuple-element.61) | copy-start | bytes 3145732
  206.9 123.7 %all-gather.31.cloned.1.call-start = ((), (), s32[]{:S(2)}) async-start(), calls=%async_computation.34 | async-start | bytes 3932160 | tf_op jit(solution)/shard_map/all_gather | solution.py:69
  225.4 169.1 %all-gather.33.cloned.1.call-start = ((), (), s32[]{:S(2)}) async-start(), calls=%async_computation.35 | async-start | bytes 3932160 | tf_op jit(solution)/shard_map/all_gather | solution.py:69
  250.9 181.6 %all-gather.21.cloned.1.call-start = ((), (), s32[]{:S(2)}) async-start(), calls=%async_computation.20 | async-start | bytes 4718592 | tf_op jit(solution)/shard_map/all_gather | solution.py:94
  266.9 3.4 copy-start.8
  267.8 226.1 %all-gather.23.cloned.1.call-start = ((), (), s32[]{:S(2)}) async-start(), calls=%async_computation.21 | async-start | bytes 3604480 | tf_op jit(solution)/shard_map/all_gather | solution.py:74
  270.2 261.6 %all-gather.25.cloned.1.call-start = ((), (), s32[]{:S(2)}) async-start(), calls=%async_computation.23 | async-start | bytes 4718592 | tf_op jit(solution)/shard_map/all_gather | solution.py:94
  271.2 331.1 %reduce-scatter.15.cloned.1.call-start = ((), (), s32[]{:S(2)}) async-start(), calls=%async_computation.24 | async-start | bytes 4718592 | tf_op jit(solution)/shard_map/reduce_scatter | solution.py:98
  432.5 8.1 copy-start.14
  432.5 8.1 copy-start.41
  531.8 10.1 copy-start.15
  541.9 3.8 copy-start.44
  541.9 3.8 copy-start.47
  541.9 3.8 copy-start.16
  550.8 106.0 %reduce-scatter.13.cloned.1.call-start = ((), (), s32[]{:S(2)}) async-start(), calls=%async_computation.22 | async-start | bytes 4718592 | tf_op jit(solution)/shard_map/reduce_scatter | solution.py:98
  558.7 138.2 %all-gather.27.cloned.1.call-start = ((), (), s32[]{:S(2)}) async-start(), calls=%async_computation.25 | async-start | bytes 4718592 | tf_op jit(solution)/shard_map/all_gather | solution.py:94
  660.0 2.9 copy-start.12
  660.0 110.3 %reduce-scatter.17.cloned.1.call-start = ((), (), s32[]{:S(2)}) async-start(), calls=%async_computation.26 | async-start | bytes 3538944 | tf_op jit(solution)/shard_map/reduce_scatter | solution.py:98
  696.9 6.0 copy-start.2
  704.2 4.9 copy-start.22
  718.5 108.9 %reduce-scatter.27.cloned.1.call-start = ((), (), s32[]{:S(2)}) async-start(), calls=%async_computation.31 | async-start | bytes 3932160 | tf_op jit(solution)/shard_map/reduce_scatter | solution.py:82
  735.1 154.7 %reduce-scatter.25.cloned.1.call-start = ((), (), s32[]{:S(2)}) async-start(), calls=%async_computation.30 | async-start | bytes 3932160 | tf_op jit(solution)/shard_map/reduce_scatter | solution.py:82
  751.7 196.5 %reduce-scatter.29.cloned.1.call-start = ((), (), s32[]{:S(2)}) async-start(), calls=%async_computation.32 | async-start | bytes 3604480 | tf_op jit(solution)/shard_map/reduce_scatter | solution.py:88
  759.8 218.2 %reduce-scatter.21.cloned.1.call-start = ((), (), s32[]{:S(2)}) async-start(), calls=%async_computation.28 | async-start | bytes 1310720 | tf_op jit(solution)/shard_map/reduce_scatter | solution.py:82
  762.7 1.6 copy-start.20
  763.8 259.1 %reduce-scatter.23.cloned.1.call-start = ((), (), s32[]{:S(2)}) async-start(), calls=%async_computation.29 | async-start | bytes 2621440 | tf_op jit(solution)/shard_map/reduce_scatter | solution.py:88
  770.2 2.3 copy-start.4
  770.2 2.3 copy-start.27
  770.2 2.3 copy-start.35
  770.2 4.0 copy-start.29
  770.2 4.0 copy-start.33
  770.2 5.6 copy-start.37
  770.2 5.7 copy-start.36
  770.3 6.6 copy-start.25
  770.3 6.6 copy-start.31
  770.3 371.7 %reduce-scatter.19.cloned.1.call-start = ((), (), s32[]{:S(2)}) async-start(), calls=%async_computation.27 | async-start | bytes 6488064 | tf_op jit(solution)/shard_map/reduce_scatter | solution.py:260
  827.3 62.5 %all-to-all-start.5 = ((bf16[8,64,1,704]{3,1,2,0:T(8,128)(2,1)}), bf16[8,64,1,704]{3,1,2,0:T(8,128)(2,1)S(1)}, u32[]{:S(2)}, u32[]{:S(2)}) async-start(bf16[8,64,1,704]{3,1,2,0:T(8,128)(2,1)} %bitcast.252), calls=%async_computation.14 | async-start | bytes 1572864 | tf_op jit(solution)/shard_map/all_to_all | solution.py:83
  889.8 64.2 %all-to-all-start.4 = ((bf16[8,64,1,704]{3,1,2,0:T(8,128)(2,1)}), bf16[8,64,1,704]{3,1,2,0:T(8,128)(2,1)S(1)}, u32[]{:S(2)}, u32[]{:S(2)}) async-start(bf16[8,64,1,704]{3,1,2,0:T(8,128)(2,1)} %bitcast.251), calls=%async_computation.12 | async-start | bytes 1572864 | tf_op jit(solution)/shard_map/all_to_all | solution.py:83
  978.0 11.3 all-to-all-start.3
  983.4 41.6 %copy-start.18 = (bf16[128,1024]{1,0:T(8,128)(2,1)S(1)}, bf16[128,1024]{1,0:T(8,128)(2,1)}, u32[]{:S(2)}) copy-start(bf16[128,1024]{1,0:T(8,128)(2,1)} %copy-done.17) | copy-start | bytes 786436
  1025.0 50.2 %copy-start.7 = (f32[128,2048]{1,0:T(8,128)S(1)}, f32[128,2048]{1,0:T(8,128)}, u32[]{:S(2)}) copy-start(f32[128,2048]{1,0:T(8,128)} %get-tuple-element.26) | copy-start | bytes 3145732
  (9 other events, 10.7 us)
Sparse Core Ops, SparseCore 0:
  11.5 72.2 all-gather.14
  94.4 24.2 all-gather.28
  121.2 31.7 all-gather.16
  155.0 45.9 all-gather.18
  207.1 58.4 reduce-scatter.10
  267.1 63.4 all-gather.30
  332.3 62.1 all-gather.32
  397.1 35.3 all-gather.20
  434.7 59.1 all-gather.22
  496.4 35.3 all-gather.24
  550.9 51.3 reduce-scatter.14
  605.5 51.2 reduce-scatter.12
  660.1 36.7 all-gather.26
  718.6 46.2 reduce-scatter.16
  767.0 60.2 reduce-scatter.26
  829.5 60.2 reduce-scatter.24
  891.9 56.1 reduce-scatter.28
  950.9 26.9 reduce-scatter.20
  980.3 42.4 reduce-scatter.22
  1028.4 113.6 reduce-scatter.18

commit v2 on v1

v2 whole, which is shorter than its diff:
```python
import math

import jax
import jax.numpy as jnp
from jax import lax
from jax.experimental import pallas as pl
from jax.experimental.pallas import tpu as pltpu
from jax.sharding import PartitionSpec as P

D = 2048
H = 16
E = 256


MESH = pl.DeviceIdType.MESH
STEP = 16
VMEM_LIMIT = 48 * 1024 * 1024
COST = pl.CostEstimate(flops=0, transcendentals=0, bytes_accessed=1024)

eps_norm = 1e-06
big_negative = -1e30


def rms_scale(values, gain_vec):
    inverse = lax.rsqrt(jnp.mean(values * values, axis=-1, keepdims=True) + eps_norm)
    return values * inverse * gain_vec


def norm_back(values, gain_vec, upstream):
    inverse = lax.rsqrt(jnp.mean(values * values, axis=-1, keepdims=True) + eps_norm)
    gain_grad = jnp.sum(upstream * values * inverse, axis=0)
    scaled = upstream * gain_vec
    value_grad = inverse * scaled - values * (inverse * inverse * inverse) * jnp.mean(
        scaled * values, axis=-1, keepdims=True
    )
    return (value_grad, gain_grad)


def rotate(values, cosine, sine_tab):
    half_width = values.shape[-1] // 2
    turned = jnp.concatenate([-values[..., half_width:], values[..., :half_width]], axis=-1)
    return values * cosine + turned * sine_tab


def rotate_back(upstream, cosine, sine_tab):
    half_width = upstream.shape[-1] // 2
    weighted = upstream * sine_tab
    turned = jnp.concatenate([weighted[..., half_width:], -weighted[..., :half_width]], axis=-1)
    return upstream * cosine + turned


def layout(seq_lengths, group_tokens):
    seq_ends = jnp.cumsum(seq_lengths)
    places = jnp.arange(group_tokens, dtype=jnp.int32)
    passed = places[:, None] >= seq_ends[None, :]
    segment = jnp.sum(passed.astype(jnp.int32), axis=1)
    starts = jnp.sum(jnp.where(passed, seq_lengths[None, :], 0), axis=1)
    return (segment, places, places - starts)


def rope_tables(offsets, width):
    half_width = width // 2
    frequency = jnp.exp(
        jnp.arange(half_width, dtype=jnp.float32) * (-2.0 * math.log(10000.0) / width)
    )
    angles = offsets.astype(jnp.float32)[:, None] * frequency[None, :]
    angles = jnp.concatenate([angles, angles], axis=-1)
    return (jnp.cos(angles), jnp.sin(angles))


VMEM = pl.BlockSpec(memory_space=pltpu.VMEM)
ANY = pl.BlockSpec(memory_space=pl.ANY)
SIBLING = (1, 0)


def flip(index, bits):
    out, power = index, 1
    while power <= bits:
        if bits & power:
            out = out + power - 2 * power * ((index // power) % 2)
        power *= 2
    return out


def here():
    return lax.axis_index("seq"), lax.axis_index("dp")


def device(mask):
    me, group = here()
    return flip(me, mask[0]), flip(group, mask[1])


def copy_to(source, target, sems, seq_to, dp_to):
    return pltpu.make_async_remote_copy(
        src_ref=source,
        dst_ref=target,
        send_sem=sems.at[0],
        recv_sem=sems.at[1],
        device_id=(seq_to, dp_to),
        device_id_type=MESH,
    )


def remote(source, target, sems, mask):
    copy = copy_to(source, target, sems, *device(mask))
    copy.start()
    return copy


def keep(source, target, sem):
    copy = pltpu.make_async_copy(source, target, sem)
    copy.start()
    return copy


class Task:
    def __init__(self, inputs, outputs, scratch, masks, run):
        self.inputs, self.outputs, self.scratch = inputs, outputs, scratch
        self.masks, self.run = masks, run


def launch(name, collective_id, tasks, needs=(), passes=()):
    masks = sorted({mask for task in tasks for mask in task.masks})
    n_in = sum(len(task.inputs) for task in tasks)
    n_out = sum(len(task.outputs) for task in tasks)

    def body(*refs):
        refs = list(refs)
        ins = refs[:n_in]
        refs = refs[n_in + len(needs) + len(passes) :]
        outs, scratch = refs[:n_out], refs[n_out + len(passes) :]
        barrier = pltpu.get_barrier_semaphore()
        for mask in masks:
            pl.semaphore_signal(barrier, inc=1, device_id=device(mask), device_id_type=MESH)
        pl.semaphore_wait(barrier, len(masks))
        running = []
        for task in tasks:
            a, b, c = len(task.inputs), len(task.outputs), len(task.scratch)
            running.append(task.run(ins[:a], outs[:b], scratch[:c]))
            ins, outs, scratch = ins[a:], outs[b:], scratch[c:]
        while running:
            for step in list(running):
                if next(step, "done") == "done":
                    running.remove(step)

    inputs = [pair for task in tasks for pair in task.inputs]
    outputs = [pair for task in tasks for pair in task.outputs]
    results = pl.pallas_call(
        body,
        name=name,
        out_shape=[shape for shape, _ in outputs]
        + [jax.ShapeDtypeStruct(a.shape, a.dtype) for a in passes],
        in_specs=[spec for _, spec in inputs] + [ANY] * (len(needs) + len(passes)),
        out_specs=[spec for _, spec in outputs] + [ANY] * len(passes),
        input_output_aliases={n_in + len(needs) + i: n_out + i for i in range(len(passes))},
        scratch_shapes=[shape for task in tasks for shape in task.scratch],
        compiler_params=pltpu.CompilerParams(
            collective_id=collective_id, has_side_effects=True, vmem_limit_bytes=VMEM_LIMIT
        ),
        cost_estimate=COST,
    )(*[array for array, _ in inputs], *needs, *passes)
    results, split = list(results), []
    for task in tasks:
        split.append(results[: len(task.outputs)])
        results = results[len(task.outputs) :]
    return split + results


def rows_loop(start, stop, step):
    def one(i, carry):
        step(pl.ds(pl.multiple_of(i * STEP, STEP), STEP))
        return carry

    lax.fori_loop(start // STEP, stop // STEP, one, 0)


def axis_masks(axis):
    if axis == "chip":
        return [(2 * j, 0) for j in range(1, lax.axis_size("seq") // 2)]
    return [(0, j) for j in range(1, lax.axis_size("dp"))]


def axis_block(axis, mask=(0, 0)):
    seq_at, dp_at = device(mask)
    return seq_at if axis == "chip" else dp_at * 2 + seq_at % 2


def line_masks():
    masks, power = [], 2
    while power <= lax.axis_size("dp"):
        masks.append((0, power - 1))
        power *= 2
    return masks


def spread_masks(axis):
    if axis == "dp":
        return [SIBLING] + line_masks()
    return [SIBLING] + axis_masks(axis)


def spread(axis, low, all_ref, keep_sem, sems):
    own = all_ref.at[axis_block(axis)]
    rows = low.shape[0]
    sends = []
    if axis == "dp":
        yield from spread_line(low, all_ref, keep_sem, sems)
        return
    masks = axis_masks(axis)
    square = len(masks) == 3
    direct = [(2, 0), (4, 0)] if square else masks
    for i, mask in enumerate(direct):
        sends.append(remote(low, own, sems.at[i], mask))
    beside = [remote(low, own, sems.at[len(masks)], SIBLING)]
    kept = keep(low, own, keep_sem)
    yield
    at, halves = len(masks) + 1, []

    def block(mask):
        return all_ref.at[axis_block(axis, mask)]

    def half(mask, which):
        return all_ref.at[axis_block(axis, mask), pl.ds(which * (rows // 2), rows // 2)]

    for i, mask in enumerate(direct):
        sends[i].wait_recv()
        if square:
            halves.append(remote(half(mask, i), half(mask, i), sems.at[at], direct[1 - i]))
            at += 1
        beside.append(remote(block(mask), block(mask), sems.at[at], SIBLING))
        at += 1
        yield
    for i, copy in enumerate(halves):
        copy.wait_recv()
        part = half((6, 0), i)
        beside.append(remote(part, part, sems.at[at], SIBLING))
        at += 1
        yield
    for copy in beside:
        copy.wait_recv()
    for copy in sends + halves + beside:
        copy.wait_send()
    kept.wait()


def spread_line(low, all_ref, keep_sem, sems):
    me, group = here()
    core, groups = me % 2, lax.axis_size("dp")
    own = all_ref.at[axis_block("dp")]
    kept = keep(low, own, keep_sem)
    beside = remote(low, own, sems.at[0], SIBLING)

    def at(way, k, kind):
        return sems.at[1 + (way * (groups - 1) + k) * 2 + kind]

    def hop(way, k):
        step = 1 - 2 * way
        block = all_ref.at[(group - step * k) * 2 + core]
        return copy_to(low if k == 0 else block, block, at(way, k, 0), me, group + step)

    def landed(way, k):
        block = all_ref.at[(group - (1 - 2 * way) * (k + 1)) * 2 + core]
        return copy_to(block, block, at(way, k, 0), *device(SIBLING))

    def aside(way, k):
        block = all_ref.at[(group - (1 - 2 * way) * (k + 1)) * 2 + core]
        return copy_to(block, block, at(way, k, 1), *device(SIBLING))

    def sends(way, k):
        if way == 0:
            return (group >= k) & (group < groups - 1)
        return (group + k < groups) & (group > 0)

    def lands(way, k):
        return (group >= k + 1) if way == 0 else (group + k + 1 < groups)

    for k in range(groups - 1):
        for way in range(2):

            @pl.when(sends(way, k))
            def _(way=way, k=k):
                hop(way, k).start()

        yield
        for way in range(2):

            @pl.when(lands(way, k))
            def _(way=way, k=k):
                landed(way, k).wait_recv()
                aside(way, k).start()

    yield
    beside.wait_recv()
    for k in range(groups - 1):
        for way in range(2):

            @pl.when(lands(way, k))
            def _(way=way, k=k):
                aside(way, k).wait()

            @pl.when(sends(way, k))
            def _(way=way, k=k):
                hop(way, k).wait_send()

    beside.wait_send()
    kept.wait()


def exchange(
    partial,
    row_operands,
    vec_operands,
    row_function,
    own_widths,
    low_width,
    vec_width,
    sum_axis="chip",
    spread_axis="chip",
):
    blocks, rows, cols = partial.shape
    far = blocks // 2
    n_rows = len(row_operands)
    masks = axis_masks(sum_axis)
    square = sum_axis == "chip" and len(masks) == 3
    out_blocks = lax.axis_size("seq") if spread_axis == "chip" else 2 * lax.axis_size("dp")
    order = list(range(far - 1, 0, -1)) + [0]
    at_mask = [(0, 0)] + masks

    def run(ins, outs, scratch):
        ins, outs = list(ins), list(outs)
        partial_ref = ins.pop(0)
        row_refs, vec_refs = ins[:n_rows], ins[n_rows:]
        all_ref = outs.pop(0) if low_width else None
        vec_out = outs.pop(-1) if vec_width else None
        mine, beside, arrived, low, local_sem, sems, out_sems = scratch

        across, loads = {}, {}
        for j in order:
            block = axis_block(sum_axis, at_mask[j])
            other = axis_block(sum_axis, (at_mask[j][0] + 1, at_mask[j][1]))
            across[j] = remote(partial_ref.at[other], beside.at[j], sems.at[j], SIBLING)
            loads[j] = keep(partial_ref.at[block], mine.at[j], local_sem.at[j])
        yield
        sent = []

        def settle(j, low_row=0, high_row=rows, more=None):
            def add(at):
                total = mine[j, at, :].astype(jnp.float32) + beside[j, at, :].astype(jnp.float32)
                if more is not None:
                    total = total + arrived[more, at, :].astype(jnp.float32)
                mine[j, at, :] = total.astype(jnp.bfloat16)

            rows_loop(low_row, high_row, add)

        if square:
            middle = rows // 2
            first, second = pl.ds(0, middle), pl.ds(middle, middle)
            for j in (3, 1, 2):
                loads[j].wait()
                across[j].wait_recv()
                if j == 3:
                    settle(3)
                elif j == 1:
                    settle(1, 0, middle)
                else:
                    settle(2, middle, rows)
                base = far + 2 * (j - 1)
                if j in (3, 1):
                    sent.append(
                        remote(mine.at[j, first], arrived.at[j, first], sems.at[base], (2, 0))
                    )
                if j in (3, 2):
                    sent.append(
                        remote(mine.at[j, second], arrived.at[j, second], sems.at[base + 1], (4, 0))
                    )
            yield
            diagonal_x, diagonal_y = sent[0], sent[1]
            diagonal_x.wait_recv()
            settle(2, 0, middle, more=3)
            sent.append(
                remote(mine.at[2, first], arrived.at[2, first], sems.at[far + 2], (4, 0))
            )
            diagonal_y.wait_recv()
            settle(1, middle, rows, more=3)
            sent.append(
                remote(mine.at[1, second], arrived.at[1, second], sems.at[far + 1], (2, 0))
            )
            yield
            adds = [1, 2]
            landed = sent[2:]
        else:
            for j in order[:-1]:
                loads[j].wait()
                across[j].wait_recv()
                settle(j)
                sent.append(remote(mine.at[j], arrived.at[j], sems.at[far + j], at_mask[j]))
                yield
            adds = order[:-1]
            landed = sent
        loads[0].wait()
        across[0].wait_recv()
        for copy in landed:
            copy.wait_recv()
        if vec_width:
            vec_out[...] = jnp.zeros_like(vec_out)
        vecs = [v[...] for v in vec_refs]

        def finish(at):
            total = mine[0, at, :].astype(jnp.float32) + beside[0, at, :].astype(jnp.float32)
            for j in adds:
                total = total + arrived[j, at, :].astype(jnp.float32)
            low_now, own_now, vec_now = row_function(total, [r[at, :] for r in row_refs], vecs)
            if low_width:
                low[at, :] = low_now.astype(jnp.bfloat16)
            for ref, value in zip(outs, own_now, strict=True):
                ref[at, :] = value
            if vec_width:
                vec_out[...] += vec_now

        rows_loop(0, rows, finish)
        if low_width:
            yield from spread(spread_axis, low, all_ref, local_sem.at[0], out_sems)
        for copy in list(across.values()) + sent:
            copy.wait_send()

    outputs = []
    if low_width:
        outputs.append((jax.ShapeDtypeStruct((out_blocks, rows, low_width), jnp.bfloat16), ANY))
    outputs += [(jax.ShapeDtypeStruct((rows, width), jnp.float32), VMEM) for width in own_widths]
    if vec_width:
        outputs.append((jax.ShapeDtypeStruct((STEP, vec_width), jnp.float32), VMEM))
    return Task(
        [(partial, ANY)] + [(a, VMEM) for a in list(row_operands) + list(vec_operands)],
        outputs,
        [
            pltpu.VMEM((far, rows, cols), jnp.bfloat16),
            pltpu.VMEM((far, rows, cols), jnp.bfloat16),
            pltpu.VMEM((far, rows, cols), jnp.bfloat16),
            pltpu.VMEM((rows, max(low_width, 128)), jnp.bfloat16),
            pltpu.SemaphoreType.DMA((far,)),
            pltpu.SemaphoreType.DMA((far + max(6, far), 2)),
            pltpu.SemaphoreType.DMA((spread_sems(spread_axis), 2)),
        ],
        [SIBLING] + masks + (spread_masks(spread_axis) if low_width else []),
        run,
    )


def spread_sems(axis):
    if axis == "dp":
        return 1 + 4 * (lax.axis_size("dp") - 1)
    return 2 * lax.axis_size("seq")


def gather(low, axis):
    rows, cols = low.shape
    blocks = lax.axis_size("seq") if axis == "chip" else 2 * lax.axis_size("dp")

    def run(ins, outs, scratch):
        yield from spread(axis, ins[0], outs[0], scratch[0].at[0], scratch[1])

    return Task(
        [(low, ANY)],
        [(jax.ShapeDtypeStruct((blocks, rows, cols), low.dtype), ANY)],
        [pltpu.SemaphoreType.DMA((1,)), pltpu.SemaphoreType.DMA((spread_sems(axis), 2))],
        spread_masks(axis),
        run,
    )


def family(kind):
    parts, groups = lax.axis_size("seq"), lax.axis_size("dp")
    if kind == "seq":
        return [(m, 0) for m in range(1, parts)], lambda s, d: s
    if kind == "dp":
        return [(0, m) for m in range(1, groups)], lambda s, d: d
    return [(m % 2, m // 2) for m in range(1, 2 * groups)], lambda s, d: d * 2 + s % 2


def swap(array, kind, repeat=False):
    masks, index = family(kind)

    def run(ins, outs, scratch):
        own = index(*here())
        copies = [keep(ins[0] if repeat else ins[0].at[own], outs[0].at[own], scratch[0].at[0])]
        for i, mask in enumerate(masks):
            source = ins[0] if repeat else ins[0].at[index(*device(mask))]
            copies.append(remote(source, outs[0].at[own], scratch[1].at[i], mask))
        yield
        for copy in copies:
            copy.wait()

    shape = (len(masks) + 1,) + array.shape if repeat else array.shape
    return Task(
        [(array, ANY)],
        [(jax.ShapeDtypeStruct(shape, array.dtype), ANY)],
        [pltpu.SemaphoreType.DMA((1,)), pltpu.SemaphoreType.DMA((len(masks), 2))],
        masks,
        run,
    )


def gather_both(array):
    seq_masks, dp_masks = family("seq")[0], family("dp")[0]
    parts, groups = lax.axis_size("seq"), lax.axis_size("dp")

    def run(ins, outs, scratch):
        me, group = here()
        (small,), (everything, line) = ins, outs
        copies = [keep(small, line.at[group], scratch[0].at[0])]
        for i, mask in enumerate(dp_masks):
            copies.append(remote(small, line.at[group], scratch[1].at[i], mask))
        yield
        for copy in copies:
            copy.wait()
        copies = [keep(line, everything.at[me], scratch[0].at[1])]
        for i, mask in enumerate(seq_masks):
            at = scratch[1].at[len(dp_masks) + i]
            copies.append(remote(line, everything.at[me], at, mask))
        yield
        for copy in copies:
            copy.wait()

    return Task(
        [(array, VMEM)],
        [
            (jax.ShapeDtypeStruct((parts, groups) + array.shape, array.dtype), VMEM),
            (jax.ShapeDtypeStruct((groups,) + array.shape, array.dtype), VMEM),
        ],
        [
            pltpu.SemaphoreType.DMA((2,)),
            pltpu.SemaphoreType.DMA((len(seq_masks) + len(dp_masks), 2)),
        ],
        seq_masks + dp_masks,
        run,
    )


def sum_both(array):
    seq_masks, dp_masks = family("seq")[0], family("dp")[0]

    def run(ins, outs, scratch):
        me, group = here()
        stage_one, line, stage_two, local_sem, sems = scratch
        copies = [keep(ins[0].at[me], stage_one.at[me], local_sem.at[0])]
        for i, mask in enumerate(seq_masks):
            source = ins[0].at[flip(me, mask[0])]
            copies.append(remote(source, stage_one.at[me], sems.at[i], mask))
        yield
        for copy in copies:
            copy.wait()
        line[...] = jnp.sum(stage_one[...], axis=0)
        copies = [keep(line.at[group], stage_two.at[group], local_sem.at[1])]
        for i, mask in enumerate(dp_masks):
            at = sems.at[len(seq_masks) + i]
            copies.append(remote(line.at[flip(group, mask[1])], stage_two.at[group], at, mask))
        yield
        for copy in copies:
            copy.wait()
        outs[0][...] = jnp.sum(stage_two[...], axis=0)

    return Task(
        [(array, VMEM)],
        [(jax.ShapeDtypeStruct(array.shape[2:], array.dtype), VMEM)],
        [
            pltpu.VMEM(array.shape, array.dtype),
            pltpu.VMEM(array.shape[1:], array.dtype),
            pltpu.VMEM(array.shape[1:], array.dtype),
            pltpu.SemaphoreType.DMA((2,)),
            pltpu.SemaphoreType.DMA((len(seq_masks) + len(dp_masks), 2)),
        ],
        seq_masks + dp_masks,
        run,
    )


def tie(value, needs):
    def body(*refs):
        pass

    return pl.pallas_call(
        body,
        name="tie",
        out_shape=jax.ShapeDtypeStruct(value.shape, value.dtype),
        in_specs=[ANY] * (1 + len(needs)),
        out_specs=ANY,
        input_output_aliases={0: 0},
        cost_estimate=COST,
    )(value, *needs)


def dot(left, right):
    return jnp.dot(left, right, preferred_element_type=jnp.float32)


def back_rows(values, gain, upstream):
    inverse = lax.rsqrt(jnp.mean(values * values, axis=-1, keepdims=True) + eps_norm)
    scaled = upstream * gain
    value_grad = inverse * scaled - values * (inverse * inverse * inverse) * jnp.mean(
        scaled * values, axis=-1, keepdims=True
    )
    return value_grad, upstream * values * inverse


def columns(weight, parts):
    rows, cols = weight.shape
    low = weight.astype(jnp.bfloat16).reshape(rows, parts, cols // parts)
    return jnp.transpose(low, (1, 0, 2))


def join(pieces):
    parts, rows, cols = pieces.shape
    full = lax.all_gather(pieces.reshape(parts * rows, cols), "dp", axis=0, tiled=True)
    full = full.reshape(-1, parts, rows, cols)
    return jnp.transpose(full, (1, 0, 2, 3)).reshape(-1, cols)


def scatter_columns(grad, parts, groups):
    rows, cols = grad.shape
    piece = rows // (parts * groups)
    low = grad.astype(jnp.bfloat16).reshape(parts, groups, piece, cols)
    low = jnp.transpose(low, (1, 0, 2, 3)).reshape(rows, cols)
    own = lax.psum_scatter(low, "dp", scatter_dimension=0, tiled=True)
    return own.reshape(parts, piece, cols), low


def scatter_rows(grad):
    low = grad.astype(jnp.bfloat16)
    return lax.psum_scatter(low, "dp", scatter_dimension=0, tiled=True), low


def unfold(pieces):
    parts, rows, cols = pieces.shape
    return jnp.transpose(pieces, (1, 0, 2)).reshape(rows, parts * cols).astype(jnp.float32)


def line_columns(weight, chips, groups):
    rows, cols = weight.shape
    low = weight.astype(jnp.bfloat16).reshape(rows, chips, 2, groups, -1)
    return jnp.transpose(low, (3, 2, 0, 1, 4)).reshape(2 * groups, rows, -1)


def line_unfold(pieces, chips, groups):
    rows = pieces.shape[1]
    full = pieces.reshape(groups, 2, rows, chips, -1)
    return jnp.transpose(full, (2, 3, 1, 0, 4)).reshape(rows, -1).astype(jnp.float32)


def chip_groups(parts):
    return [[chip * 2 + core for chip in range(parts // 2)] for core in range(2)]


def chip_gather(rows, parts):
    return lax.all_gather(rows, "seq", axis=0, tiled=True, axis_index_groups=chip_groups(parts))


def chip_scatter(rows, parts):
    return lax.psum_scatter(
        rows, "seq", scatter_dimension=0, tiled=True, axis_index_groups=chip_groups(parts)
    )


def local(
    block_input,
    lengths,
    cotangent,
    attn_gain,
    w_qa,
    q_gain,
    w_qb,
    w_k,
    k_gain,
    w_v,
    w_o,
    mlp_gain,
    w_gate,
    w_up,
    w_down,
):
    tok_rows = block_input.shape[1]
    parts = lax.axis_size("seq")
    groups = lax.axis_size("dp")
    me = lax.axis_index("seq")
    heads = H // parts
    group_tokens = tok_rows * parts
    first_row = me * tok_rows
    segment, places, offsets = layout(lengths[0], group_tokens)
    cos_all, sin_all = rope_tables(offsets, E)
    cosine = lax.dynamic_slice_in_dim(cos_all, first_row, tok_rows, 0)
    sine_tab = lax.dynamic_slice_in_dim(sin_all, first_row, tok_rows, 0)
    score_scale = 1.0 / math.sqrt(E)
    flat_rows = block_input.reshape(tok_rows, D)
    out_grad = cotangent.reshape(tok_rows, D)
    rank = w_qa.shape[1]
    inner = rank + 2 * E
    width = D // parts

    own_gains = [attn_gain, q_gain, k_gain, mlp_gain]
    spans = [g.shape[0] for g in own_gains]
    gain_block = jnp.concatenate(
        [jnp.pad(g, (0, 128 - g.shape[0]))[None] for g in own_gains]
        + [jnp.zeros((4, 128), jnp.float32)],
        axis=0,
    )
    gain_block = lax.reduce_precision(gain_block, 8, 7)
    inverse_one = lax.rsqrt(jnp.mean(flat_rows * flat_rows, axis=-1, keepdims=True) + eps_norm)
    scaled_cols = jnp.transpose(
        (flat_rows * inverse_one).reshape(tok_rows, parts, width), (1, 0, 2)
    )
    w_in = jnp.concatenate([w_qa, w_k, w_v], axis=1).astype(jnp.bfloat16)
    (gains, gains_line), (scaled_cols,), (in_rows,), (qb_cols,), o_low = launch(
        "start",
        0,
        [
            gather_both(gain_block),
            swap(scaled_cols, "seq"),
            swap(w_in, "dp", repeat=True),
            swap(columns(w_qb, parts), "seq"),
        ],
        passes=[w_o.astype(jnp.bfloat16)],
    )
    gain_one = gains[:, :, 0, : spans[0]].reshape(1, -1)
    gain_latent = gains[:, :, 1, : spans[1]].reshape(1, -1)
    gain_key = gains[:, :, 2, : spans[2]].reshape(1, -1)
    gain_two = gains[:, :, 3, : spans[3]].reshape(1, -1)
    gain_mine = gains_line[:, 0, : spans[0]].reshape(1, -1)

    o_rows = lax.all_gather(o_low, "dp", axis=0, tiled=True)
    qb_cols = join(qb_cols)

    in_rows = in_rows.reshape(width, inner)
    normed = (scaled_cols.reshape(group_tokens, width) * gain_mine).astype(jnp.bfloat16)
    partial = dot(normed, in_rows).astype(jnp.bfloat16).reshape(parts, tok_rows, inner)

    def latent_rows(total, row, vec):
        latent, key, value = total[:, :rank], total[:, rank : rank + E], total[:, rank + E :]
        low = jnp.concatenate(
            [rms_scale(latent, vec[0]), rotate(rms_scale(key, vec[1]), row[0], row[1]), value],
            axis=1,
        )
        return low, [total], None

    (gathered, inner_own), (grad_all,), down_low = launch(
        "latent",
        1,
        [
            exchange(
                partial,
                [cosine, sine_tab],
                [gain_latent, gain_key],
                latent_rows,
                [inner],
                inner,
                0,
            ),
            gather(out_grad.astype(jnp.bfloat16), "dp"),
        ],
        passes=[w_down.astype(jnp.bfloat16)],
    )
    grad_all = grad_all.reshape(-1, D)
    down_rows = chip_gather(down_low, parts)
    chips = parts // 2
    both_cols = jnp.concatenate(
        [line_columns(w_gate, chips, groups), line_columns(w_up, chips, groups)], axis=2
    )
    ((both_cols,),) = launch("gate_up", 2, [swap(both_cols, "line")], needs=[gathered])
    gathered = gathered.reshape(group_tokens, inner)
    units = both_cols.shape[2] // 2
    latent_all = gathered[:, :rank]
    keys_all = gathered[:, rank : rank + E]
    values_all = gathered[:, rank + E :]

    query = dot(latent_all, qb_cols).reshape(group_tokens, heads, E)
    query = jnp.transpose(query, (1, 0, 2))
    q_rot = rotate(query, cos_all[None], sin_all[None]).astype(jnp.bfloat16)
    allowed = (segment[:, None] == segment[None, :]) & (places[None, :] <= places[:, None])
    scores = (
        jnp.einsum("htd,kd->htk", q_rot, keys_all, preferred_element_type=jnp.float32)
        * score_scale
    )
    scores = jnp.where(allowed[None], scores, big_negative)
    shifted = jnp.exp(scores - jnp.max(scores, axis=-1, keepdims=True))
    probs = shifted / jnp.sum(shifted, axis=-1, keepdims=True)
    probs_low = probs.astype(jnp.bfloat16)
    attended = jnp.einsum("htk,kd->htd", probs_low, values_all, preferred_element_type=jnp.float32)
    attended_low = jnp.transpose(attended.astype(jnp.bfloat16), (1, 0, 2)).reshape(
        group_tokens, heads * E
    )
    partial = dot(attended_low, o_rows).astype(jnp.bfloat16).reshape(parts, tok_rows, D)

    def mixed_function(total, row, vec):
        mixed = row[0] + total
        return rms_scale(mixed, vec[0]), [mixed], None

    ((two_all, mixed_rows),) = launch(
        "mixed",
        3,
        [
            exchange(
                partial,
                [flat_rows],
                [gain_two],
                mixed_function,
                [D],
                D,
                0,
                spread_axis="dp",
            )
        ],
        needs=[down_rows],
    )
    two_all = two_all.reshape(-1, D)
    wide = both_cols.shape[2]
    piece = both_cols.shape[1]
    both_cols = chip_gather(both_cols.reshape(-1, wide), parts)
    both_cols = both_cols.reshape(chips, groups, 2, piece, wide)
    both_cols = jnp.transpose(both_cols, (0, 2, 1, 3, 4)).reshape(D, wide)

    both_act = dot(two_all, both_cols)
    gate_act, up_act = both_act[:, :units], both_act[:, units:]
    sigmoid_gate = jax.nn.sigmoid(gate_act)
    hidden = (gate_act * sigmoid_gate * up_act).astype(jnp.bfloat16)
    hidden_grad = jnp.einsum("td,fd->tf", grad_all, down_rows, preferred_element_type=jnp.float32)
    gate_grad = (
        hidden_grad * up_act * (sigmoid_gate * (1.0 + gate_act * (1.0 - sigmoid_gate)))
    ).astype(jnp.bfloat16)
    up_grad = (hidden_grad * (gate_act * sigmoid_gate)).astype(jnp.bfloat16)
    down_low = jnp.einsum("tf,td->fd", hidden, grad_all, preferred_element_type=jnp.float32)
    down_low = down_low.astype(jnp.bfloat16)
    down_shard = chip_scatter(down_low, parts)
    both_grad = jnp.concatenate([gate_grad, up_grad], axis=1)
    both_low = jnp.einsum("td,tf->df", two_all, both_grad, preferred_element_type=jnp.float32)
    both_low = both_low.astype(jnp.bfloat16).reshape(chips, 2, groups, piece, wide)
    both_low = jnp.transpose(both_low, (0, 2, 1, 3, 4)).reshape(D, wide)
    both_shard = chip_scatter(both_low, parts).reshape(2 * groups, piece, wide)
    two_part = jnp.einsum(
        "tf,df->td", both_grad, both_cols, preferred_element_type=jnp.float32
    ).astype(jnp.bfloat16)

    def two_function(total, row, vec):
        value_grad, gain_grad = back_rows(row[0], vec[0], total)
        mixed_grad = row[1] + value_grad
        return mixed_grad, [mixed_grad], gain_grad

    ((mixed_all, mixed_grad, gain_two_grad),) = launch(
        "two_grad",
        4,
        [
            exchange(
                two_part.reshape(2 * groups, tok_rows, D),
                [mixed_rows, out_grad],
                [gain_two],
                two_function,
                [D],
                D,
                D,
                sum_axis="dp",
            )
        ],
        needs=[down_low, both_low],
    )
    mixed_all = tie(mixed_all, [down_shard]).reshape(group_tokens, D)
    o_shard, o_low = scatter_rows(
        jnp.einsum("tf,td->fd", attended_low, mixed_all, preferred_element_type=jnp.float32)
    )
    att_grad = jnp.einsum("td,fd->tf", mixed_all, o_rows, preferred_element_type=jnp.float32)
    att_grad = jnp.transpose(
        att_grad.astype(jnp.bfloat16).reshape(group_tokens, heads, E), (1, 0, 2)
    )
    delta_rows = jnp.sum(att_grad.astype(jnp.float32) * attended, axis=-1)
    value_grads = jnp.einsum(
        "htk,htd->kd", probs_low, att_grad, preferred_element_type=jnp.float32
    )
    prob_grad = jnp.einsum("htd,kd->htk", att_grad, values_all, preferred_element_type=jnp.float32)
    score_grad = (probs * (prob_grad - delta_rows[..., None])).astype(jnp.bfloat16)
    query_grad = (
        jnp.einsum("htk,kd->htd", score_grad, keys_all, preferred_element_type=jnp.float32)
        * score_scale
    )
    key_grads = (
        jnp.einsum("htk,htd->kd", score_grad, q_rot, preferred_element_type=jnp.float32)
        * score_scale
    )
    query_grad = rotate_back(query_grad, cos_all[None], sin_all[None]).astype(jnp.bfloat16)
    query_grad = jnp.transpose(query_grad, (1, 0, 2)).reshape(group_tokens, heads * E)
    qb_shard, qb_low = scatter_columns(
        jnp.einsum("tr,tf->rf", latent_all, query_grad, preferred_element_type=jnp.float32),
        parts,
        groups,
    )
    latent_part = jnp.einsum("tf,rf->tr", query_grad, qb_cols, preferred_element_type=jnp.float32)
    partial = jnp.concatenate([latent_part, key_grads, value_grads], axis=1).astype(jnp.bfloat16)

    def inner_function(total, row, vec):
        latent_grad, latent_gain = back_rows(row[0][:, :rank], vec[0], total[:, :rank])
        key_back = rotate_back(total[:, rank : rank + E], row[1], row[2])
        key_grad, key_gain = back_rows(row[0][:, rank : rank + E], vec[1], key_back)
        low = jnp.concatenate([latent_grad, key_grad, total[:, rank + E :]], axis=1)
        return low, [], jnp.concatenate([latent_gain, key_gain], axis=1)

    out_part = dot(hidden, down_rows).astype(jnp.bfloat16).reshape(2 * groups, tok_rows, D)

    def out_function(total, row, vec):
        return None, [row[0] + total], None

    (in_grad, inner_gain_grad), (output_rows,) = launch(
        "inner_grad",
        5,
        [
            exchange(
                partial.reshape(parts, tok_rows, inner),
                [inner_own, cosine, sine_tab],
                [gain_latent, gain_key],
                inner_function,
                [],
                inner,
                rank + E,
            ),
            exchange(out_part, [mixed_rows], [], out_function, [D], 0, 0, sum_axis="dp"),
        ],
        needs=[o_low, qb_low],
    )
    in_grad = in_grad.reshape(group_tokens, inner)
    in_low = jnp.einsum("td,tr->dr", normed, in_grad, preferred_element_type=jnp.float32)
    in_low = in_low.astype(jnp.bfloat16).reshape(groups, -1, inner)
    normed_part = jnp.einsum("tr,dr->td", in_grad, in_rows, preferred_element_type=jnp.float32)
    normed_part = normed_part.astype(jnp.bfloat16).reshape(parts, tok_rows, width)

    (normed_grad,), (in_shard,), (both_shard,) = launch(
        "normed_grad",
        6,
        [swap(normed_part, "seq"), swap(in_low, "dp"), swap(both_shard, "line")],
    )
    in_shard = jnp.sum(in_shard.astype(jnp.float32), axis=0)
    normed_grad = jnp.transpose(normed_grad.astype(jnp.float32), (1, 0, 2)).reshape(tok_rows, D)
    input_part, gain_one_grad = back_rows(flat_rows, gain_one, normed_grad)
    input_grad = mixed_grad + input_part

    gain_grads = [
        jnp.sum(gain_one_grad, axis=0),
        jnp.sum(inner_gain_grad[:, :rank], axis=0),
        jnp.sum(inner_gain_grad[:, rank:], axis=0),
        jnp.sum(gain_two_grad, axis=0),
    ]
    gain_grads = jnp.stack(
        [
            jnp.pad(g.reshape(parts, groups, n), ((0, 0), (0, 0), (0, 128 - n)))
            for g, n in zip(gain_grads, spans, strict=True)
        ]
        + [jnp.zeros((parts, groups, 128), jnp.float32)] * 4,
        axis=2,
    )
    (gain_own,), (qb_shard,) = launch("end", 7, [sum_both(gain_grads), swap(qb_shard, "seq")])
    return (
        output_rows.reshape(1, tok_rows, D),
        input_grad.reshape(1, tok_rows, D),
        gain_own[0, : spans[0]],
        in_shard[:, :rank],
        gain_own[1, : spans[1]],
        unfold(qb_shard),
        in_shard[:, rank : rank + E],
        gain_own[2, : spans[2]],
        in_shard[:, rank + E :],
        o_shard.astype(jnp.float32),
        gain_own[3, : spans[3]],
        line_unfold(both_shard[:, :, :units], chips, groups),
        line_unfold(both_shard[:, :, units:], chips, groups),
        down_shard.astype(jnp.float32),
    )


def solution(mesh):
    return jax.shard_map(
        local,
        mesh=mesh,
        in_specs=(
            P("dp", "seq", None),
            P("dp", None),
            P("dp", "seq", None),
            P(("seq", "dp")),
            P(("seq", "dp"), None),
            P(("seq", "dp")),
            P(("seq", "dp"), None),
            P(("seq", "dp"), None),
            P(("seq", "dp")),
            P(("seq", "dp"), None),
            P(("seq", "dp"), None),
            P(("seq", "dp")),
            P(("seq", "dp"), None),
            P(("seq", "dp"), None),
            P(("seq", "dp"), None),
        ),
        out_specs=(
            P("dp", "seq", None),
            P("dp", "seq", None),
            P(("seq", "dp")),
            P(("seq", "dp"), None),
            P(("seq", "dp")),
            P(("seq", "dp"), None),
            P(("seq", "dp"), None),
            P(("seq", "dp")),
            P(("seq", "dp"), None),
            P(("seq", "dp"), None),
            P(("seq", "dp")),
            P(("seq", "dp"), None),
            P(("seq", "dp"), None),
            P(("seq", "dp"), None),
        ),
        check_vma=False,
    )
```

time: 1160 us -> 731 us (0.63)
  waiting for transfers between devices: 738 us -> 12.6 us
  Pallas kernels: 0 us -> 446 us
  blocking collectives: 148 us -> 0 us
  local copies, waits for them, and re-layouts: 60.4 us -> 99.3 us
  starting transfers between devices: 18.7 us -> 1.02 us
  matrix products: 121 us -> 104 us
    pallas_call x0 -> x9, Pallas kernels: none -> 446 us  [the longest x8 446 us: launch(): pl.pallas_call(body, name=name, out_shape=[shape for shape, _ in outputs]...]
    reduce_scatter x10 -> x4, waiting for transfers between devices: 391 us -> 11.1 us  [the longest x2 11.1 us: chip_scatter(): lax.psum_scatter(rows, 'seq', scatter_dimension=0, tiled=True, axis_index...]
    all_gather x10 -> x4, waiting for transfers between devices: 342 us -> 0.03 us  [the longest x2 0.02 us: chip_gather(): lax.all_gather(rows, 'seq', axis=0, tiled=True, axis_index_groups=chip_gr...]
    all_gather x1 -> x0, blocking collectives: 69.3 us -> none  [local(): gains = lax.all_gather(gains, both, axis=0, tiled=False).astype(jnp.float32)]
    unnamed x1 -> x0, blocking collectives: 39.7 us -> none
    all_to_all x2 -> x0, blocking collectives: 39.3 us -> none  [gather_columns(): mine = lax.all_to_all(low, 'seq', split_axis=1, concat_axis=0, tiled=False)]
    reshape x4 -> x15, local copies, waits for them, and re-layouts: 2.26 us -> 30.8 us  [the longest x4 15.4 us: line_columns(): low = weight.astype(jnp.bfloat16).reshape(rows, chips, 2, groups, -1)]
    all_to_all x4 -> x0, starting transfers between devices: 16.8 us -> none  [the longest x3 11.7 us: scatter_columns(): back = lax.all_to_all(own, 'seq', split_axis=0, concat_axis=1, tiled=False)]
  transfers between devices with their start and end apart: 24 -> 8, of which waited for: 19 -> 1; matrix products, arithmetic and copies ran while one was open for 15% -> 22% of each run, Pallas kernels for 0% -> 56%
where the time goes in v2:
time: 731 us; the launch traced here: 725 us
  Pallas kernels  446 us (61%)
  matrix products  104 us (14%)
  local copies, waits for them, and re-layouts  99.3 us (14%)
  other arithmetic  46.6 us (6%)
  between operations  15.2 us (2%)
  waiting for transfers between devices  12.6 us (2%)
    pallas_call x8, Pallas kernels, launch(): pl.pallas_call(body, name=name, out_shape=[shape for shape, _ in outputs]...  446 us
    dot_general x5, matrix products, dot(): return jnp.dot(left, right, preferred_element_type=jnp.float32)  28.2 us
    unnamed x125, local copies, waits for them, and re-layouts  21.9 us
    convert_element_type x6, local copies, waits for them, and re-layouts, line_unfold(): jnp.transpose(full, (2, 3, 1, 0, 4)).reshape(rows, -1).astype(jnp.float32)  21.5 us
    reshape x4, local copies, waits for them, and re-layouts, line_columns(): low = weight.astype(jnp.bfloat16).reshape(rows, chips, 2, groups, -1)  15.4 us
  transfers between devices with their start and end apart: 8, of which 1 were waited for; matrix products, arithmetic and copies ran while one was open for 22% of the time, Pallas kernels for 56%

profile of v2, /device:TPU:0, one launch (start us, length us, event | category | flops | bytes accessed | tf_op | source)
XLA Modules:
  0.0 725.3 jit_solution(11399097181590650147)
XLA Ops:
  7.3 1.6 copy.122
  13.8 24.0 %start.1 = (f32[8,4,8,128]{3,2,1,0:T(8,128)S(1)}, f32[4,8,128]{2,1,0:T(8,128)S(1)}, f32[8,128,256]{2,1,0:T(8,128)S(1)}, bf16[4,64,1536]{2,1,0:T(8,128)(2,1)S(1)}...) custom-call(f32[8,128]{1,0:T(8,128)S(1)} %reduce_precision.3.refs_0_, ...), custom_call_target="tpu_custom_call", output_to_operand_aliasing={{5}: (4, {})} | custom-call | bytes 1024 | tf_op jit(solution)/shard_map/start/pallas_call | solution.py:149
  39.2 2.3 convert_element_type.167.refs_6_
  42.4 4.6 broadcast_multiply_fusion.2
  48.1 2.6 convolution_convert_fusion.1
  50.8 91.3 %latent.1 = (bf16[8,128,1536]{2,1,0:T(8,128)(2,1)S(1)}, f32[128,1536]{1,0:T(8,128)S(1)}, bf16[8,128,2048]{2,1,0:T(8,128)(2,1)}, bf16[176,2048]{1,0:T(8,128)(2,1)}) custom-call(bf16[8,128,1536]{2,1,0:T(8,128)(2,1)} %bitcast.212, f32[128,256]{1,0:T(8,128)S(1)} %get-tuple-element.95.refs_1_.refs_2_, ...), custom_call_target="tpu_custom_call", output_to_operand_aliasing={{3}: (6, {})} | custom-call | bytes 1024 | tf_op jit(solution)/shard_map/latent/pallas_call | solution.py:149
  143.6 2.8 convert_element_type.174
  146.4 5.1 reshape.376
  151.4 2.7 copy.176
  154.1 3.0 reshape.377
  157.2 2.3 convert_element_type.173
  159.4 5.1 reshape.374
  164.5 2.6 copy.177
  167.1 3.0 reshape.375
  170.2 1.8 pad_maximum_fusion.4.refs_0_
  172.0 28.3 %gate_up.1 = bf16[8,64,1408]{2,1,0:T(8,128)(2,1)} custom-call(bf16[8,64,1408]{2,1,0:T(8,128)(2,1)S(1)} %pad_maximum_fusion.4.refs_0_, bf16[8,128,1536]{2,1,0:T(8,128)(2,1)S(1)} %get-tuple-element.41.refs_1_), custom_call_target="tpu_custom_call" | custom-call | bytes 1024 | tf_op jit(solution)/shard_map/gate_up/pallas_call | solution.py:149
  200.4 2.5 copy.128
  202.9 2.5 copy.127
  207.0 2.3 fusion.4
  209.3 2.3 copy.125
  211.6 2.4 copy.126
  214.0 2.7 fusion.17
  218.5 1.7 fusion.10
  220.3 8.0 %fusion.40 = (f32[2,1024]{1,0:T(2,128)S(1)}, f32[2,1024,1024]{1,2,0:T(8,128)}) fusion(pred[1024,1024]{0,1:T(8,128)(4,1)} %fusion.4, bf16[2,1024,256]{1,2,0:T(8,128)(2,1)} %fusion.10, bf16[1024,1536]{1,0:T(8,128)(2,1)S(1)} %bitcast.196), kind=kOutput, calls=%fused_computation.113 | convolution fusion | flops 1082131456 | bytes 11018240 | tf_op jit(solution)/shard_map/sub | solution.py:783
  228.3 6.6 fusion.6
  234.9 5.1 fusion.41
  240.0 6.8 convolution_convert_fusion.4
  246.8 1.8 copy-done.7
  248.6 84.4 %mixed.1 = (bf16[8,128,2048]{2,1,0:T(8,128)(2,1)}, f32[128,2048]{1,0:T(8,128)S(1)}) custom-call(bf16[8,128,2048]{2,1,0:T(8,128)(2,1)} %bitcast.220, f32[128,2048]{1,0:T(8,128)S(1)} %bitcast.192, f32[1,2048]{1,0:T(1,128)S(1)} %reshape_squeeze.13.refs_2_.refs_3_, bf16[704,2048]{1,0:T(8,128)(2,1)S(1)} %copy-done.7), custom_call_target="tpu_custom_call" | custom-call | bytes 1024 | tf_op jit(solution)/shard_map/mixed/pallas_call | solution.py:149
  333.1 3.3 copy.134
  337.0 8.3 %fusion.42 = f32[1024,1408]{0,1:T(8,128)} fusion(bf16[1024,2048]{1,0:T(8,128)(2,1)S(1)} %bitcast.253, bf16[2048,1408]{1,0:T(8,128)(2,1)S(1)} %bitcast.216), kind=kOutput, calls=%fused_computation.115 | convolution fusion | flops 5905580032 | bytes 15728640 | tf_op jit(solution)/shard_map/dot_general | solution.py:594
  345.3 7.5 %multiply_convert_fusion.3 = (bf16[1024,704]{0,1:T(8,128)(2,1)}, bf16[1024,704]{0,1:T(8,128)(2,1)}, bf16[1024,704]{0,1:T(8,128)(2,1)S(1)}) fusion(f32[1024,1408]{0,1:T(8,128)} %fusion.42, bf16[1024,2048]{1,0:T(8,128)(2,1)S(1)} %bitcast.250, bf16[704,2048]{1,0:T(8,128)(2,1)S(1)} %copy-done.8), kind=kOutput, calls=%fused_computation.23 | convolution fusion | flops 2963603456 | bytes 17170432 | tf_op jit(solution)/shard_map/td,fd->tf/dot_general | solution.py:824
  353.8 4.5 convolution_convert_fusion.5.refs_4_
  358.4 9.8 %convolution_convert_fusion = bf16[2048,1408]{1,0:T(8,128)(2,1)S(1)} fusion(bf16[1024,2048]{1,0:T(8,128)(2,1)} %bitcast.252, bf16[1024,704]{0,1:T(8,128)(2,1)} %get-tuple-element.65, bf16[1024,704]{0,1:T(8,128)(2,1)} %get-tuple-element.64), kind=kOutput, calls=%fused_computation.4 | convolution fusion | flops 5914230784 | bytes 12845056 | tf_op jit(solution)/shard_map/td,tf->df/dot_general | solution.py:833
  368.3 3.1 copy.137
  371.4 11.3 %convolution_convert_fusion.3 = bf16[1024,2048]{1,0:T(8,128)(2,1)} fusion(bf16[2048,1408]{1,0:T(8,128)(2,1)} %bitcast.217, bf16[1024,704]{0,1:T(8,128)(2,1)S(1)} %copy-done.60, bf16[1024,704]{0,1:T(8,128)(2,1)S(1)} %copy-done.59), kind=kOutput, calls=%fused_computation.14 | convolution fusion | flops 5913444352 | bytes 12845056 | tf_op jit(solution)/shard_map/tf,df->td/dot_general | solution.py:837
  382.7 1.8 copy-done.1
  384.5 74.8 %two_grad.1 = (bf16[8,128,2048]{2,1,0:T(8,128)(2,1)}, f32[128,2048]{1,0:T(8,128)S(1)}, f32[16,2048]{1,0:T(8,128)S(1)}) custom-call(bf16[8,128,2048]{2,1,0:T(8,128)(2,1)} %bitcast.219, f32[128,2048]{1,0:T(8,128)S(1)} %get-tuple-element.47.refs_1_.refs_7_, f32[128,2048]{1,0:T(8,128)S(1)} %bitcast.201, f32[1,2048]{1,0:T(1,128)S(1)} %reshape_squeeze.13.refs_2_.refs_3_, ...), custom_call_target="tpu_custom_call" | custom-call | bytes 1024 | tf_op jit(solution)/shard_map/two_grad/pallas_call | solution.py:149
  461.5 5.8 convolution_convert_fusion.6.refs_8_
  468.3 1.6 copy.143
  469.9 2.5 copy.142
  474.6 7.8 %convolution_convert_fusion.2 = bf16[1024,2048]{1,0:T(8,128)(2,1)} fusion(bf16[1024,704]{0,1:T(8,128)(2,1)} %copy-done.58, bf16[704,2048]{1,0:T(8,128)(2,1)} %all-gather.7.cloned.1.call-done.refs_3_), kind=kOutput, calls=%fused_computation.13 | convolution fusion | flops 2954887168 | bytes 8519680 | tf_op jit(solution)/shard_map/dot_general | solution.py:594
  482.5 2.4 multiply_reduce_fusion
  485.0 5.1 multiply_convert_fusion
  495.9 2.9 convolution_convert_fusion.7
  500.1 4.0 fusion.25
  504.1 1.8 pad_maximum_fusion.refs_0_
  506.5 64.6 %inner_grad.1 = (bf16[8,128,1536]{2,1,0:T(8,128)(2,1)}, f32[16,1280]{1,0:T(8,128)S(1)}, f32[128,2048]{1,0:T(8,128)S(1)}) custom-call(bf16[8,128,1536]{2,1,0:T(8,128)(2,1)} %pad_maximum_fusion.refs_0_, f32[128,1536]{1,0:T(8,128)S(1)} %copy-done.17, f32[128,256]{1,0:T(8,128)S(1)} %get-tuple-element.95.refs_1_.refs_2_, ...), custom_call_target="tpu_custom_call" | custom-call | bytes 1024 | tf_op jit(solution)/shard_map/inner_grad/pallas_call | solution.py:149
  572.3 2.4 convert_element_type.203
  574.7 4.2 fusion.8
  578.9 1.8 convolution_convert_fusion.9
  580.7 2.1 convert_element_type.194
  582.8 11.1 %reduce-scatter.7.cloned.1.call-done = bf16[512,1408]{1,0:T(8,128)(2,1)} async-done(((bf16[2048,1408]{1,0:T(8,128)(2,1)}), bf16[512,1408]{1,0:T(8,128)(2,1)}) %reduce-scatter.7.cloned.1.call-update) | async-done | bytes 1441808 | tf_op jit(solution)/shard_map/reduce_scatter | solution.py:659
  597.4 62.0 %normed_grad.1 = (bf16[8,128,256]{2,1,0:T(8,128)(2,1)S(1)}, bf16[4,64,1536]{2,1,0:T(8,128)(2,1)S(1)}, bf16[8,64,1408]{2,1,0:T(8,128)(2,1)S(1)}) custom-call(bf16[8,128,256]{2,1,0:T(8,128)(2,1)S(1)} %bitcast.208, bf16[4,64,1536]{2,1,0:T(8,128)(2,1)S(1)} %bitcast.207, bf16[8,64,1408]{2,1,0:T(8,128)(2,1)S(1)} %bitcast.202), custom_call_target="tpu_custom_call" | custom-call | bytes 1024 | tf_op jit(solution)/shard_map/normed_grad/pallas_call | solution.py:149
  664.0 16.7 %end.1 = (f32[8,128]{1,0:T(8,128)S(1)}, bf16[8,32,512]{2,1,0:T(8,128)(2,1)S(1)}) custom-call(f32[8,4,8,128]{3,2,1,0:T(8,128)S(1)} %stack.23.refs_0_, bf16[8,32,512]{2,1,0:T(8,128)(2,1)S(1)} %bitcast.209), custom_call_target="tpu_custom_call" | custom-call | bytes 1024 | tf_op jit(solution)/shard_map/end/pallas_call | solution.py:149
  684.9 2.5 copy.149
  687.5 2.5 copy.150
  692.3 2.1 slice_convert_fusion
  694.5 3.0 reshape.405
  697.5 2.7 copy.153
  700.2 4.4 reshape.403
  704.6 2.9 reshape.406
  707.5 4.4 copy.154
  711.9 4.0 reshape.404
  (212 shorter events, 45.9 us)
Async XLA Ops:
  7.2 3.2 copy-start.49
  7.2 3.2 copy-start.50
  7.2 3.2 copy-start.51
  7.2 3.2 copy-start.52
  7.2 4.3 copy-start.41
  7.2 4.3 copy-start.42
  7.2 4.3 copy-start.40
  7.3 202.0 %all-gather.5.cloned.1.call-start = ((), (), s32[]{:S(2)}) async-start(), calls=%async_computation.4 | async-start | bytes 1310720 | tf_op jit(solution)/shard_map/all_gather | solution.py:614
  8.9 3.7 copy-start.39
  10.9 2.9 copy-start.22
  11.5 2.3 copy-start.45
  13.6 25.1 %copy-start.48 = (s32[1,4]{1,0:T(1,128)S(1)}, s32[1,4]{1,0:T(1,128)}, u32[]{:S(2)}) copy-start(s32[1,4]{1,0:T(1,128)} %param.16) | copy-start | bytes 52
  37.7 10.3 %copy-start.14 = (bf16[4,64,1536]{2,1,0:T(8,128)(2,1)}, bf16[4,64,1536]{2,1,0:T(8,128)(2,1)S(1)}, u32[]{:S(2)}) copy-start(bf16[4,64,1536]{2,1,0:T(8,128)(2,1)S(1)} %get-tuple-element.39) | copy-start | bytes 2359300
  37.8 202.3 %all-gather.9.cloned.1.call-start = ((), (), s32[]{:S(2)}) async-start(), calls=%async_computation.6 | async-start | bytes 2621440 | tf_op jit(solution)/shard_map/all_gather | solution.py:729
  38.5 208.3 %all-gather.7.cloned.1.call-start = ((), (), s32[]{:S(2)}) async-start(), calls=%async_computation.5 | async-start | bytes 3604480 | tf_op jit(solution)/shard_map/all_gather | solution.py:655
  46.9 3.8 copy-start.26
  48.0 2.7 copy-start.33
  48.1 2.6 copy-start.5
  143.0 91.9 %copy-start.3 = (bf16[8,128,1536]{2,1,0:T(8,128)(2,1)}, bf16[8,128,1536]{2,1,0:T(8,128)(2,1)S(1)}, u32[]{:S(2)}) copy-start(bf16[8,128,1536]{2,1,0:T(8,128)(2,1)S(1)} %get-tuple-element.41.refs_1_) | copy-start | bytes 9437188
  143.0 190.1 %all-gather.11.cloned.1.call-start = ((), (), s32[]{:S(2)}) async-start(), calls=%async_computation.7 | async-start | bytes 7208960 | tf_op jit(solution)/shard_map/all_gather | solution.py:655
  200.3 259.9 %reduce-scatter.5.cloned.1.call-start = ((), (), s32[]{:S(2)}) async-start(), calls=%async_computation.8 | async-start | bytes 3604480 | tf_op jit(solution)/shard_map/reduce_scatter | solution.py:659
  216.7 1.4 copy-start.28
  216.7 1.8 copy-start.29
  228.3 6.6 copy-start.43
  240.0 6.8 copy-start
  246.8 1.8 copy-start.7
  333.1 3.9 copy-start.54
  336.4 8.8 %copy-start.25 = (bf16[4,2,4,64,1408]{4,3,2,1,0:T(8,128)(2,1)}, bf16[4,2,4,64,1408]{4,3,2,1,0:T(8,128)(2,1)S(1)}, u32[]{:S(2)}) copy-start(bf16[4,2,4,64,1408]{4,3,2,1,0:T(8,128)(2,1)S(1)} %copy.134) | copy-start | bytes 17301508
  337.0 8.3 %copy-start.8 = (bf16[704,2048]{1,0:T(8,128)(2,1)S(1)}, bf16[704,2048]{1,0:T(8,128)(2,1)}, u32[]{:S(2)}) copy-start(bf16[704,2048]{1,0:T(8,128)(2,1)} %all-gather.7.cloned.1.call-done.refs_3_) | copy-start | bytes 8650756
  337.0 8.3 %copy-start.53 = (bf16[8,128,2048]{2,1,0:T(8,128)(2,1)S(1)}, bf16[8,128,2048]{2,1,0:T(8,128)(2,1)}, u32[]{:S(2)}) copy-start(bf16[8,128,2048]{2,1,0:T(8,128)(2,1)} %get-tuple-element.43) | copy-start | bytes 12582916
  352.7 1.1 copy-start.58
  358.4 222.3 %reduce-scatter.11.cloned.1.call-start = ((), (), s32[]{:S(2)}) async-start(), calls=%async_computation.11 | async-start | bytes 2621440 | tf_op jit(solution)/shard_map/reduce_scatter | solution.py:630
  368.3 3.1 copy-start.59
  368.3 3.1 copy-start.60
  371.4 11.3 %copy-start.6 = (f32[1,128,2048]{2,1,0:T(8,128)S(1)}, f32[1,128,2048]{2,1,0:T(8,128)}, u32[]{:S(2)}) copy-start(f32[1,128,2048]{2,1,0:T(8,128)} %param.17) | copy-start | bytes 3145732
  382.6 1.8 copy-start.1
  459.3 1.0 copy-start.10
  460.3 1.2 copy-start.38
  467.3 126.6 %reduce-scatter.7.cloned.1.call-start = ((), (), s32[]{:S(2)}) async-start(), calls=%async_computation.9 | async-start | bytes 7208960 | tf_op jit(solution)/shard_map/reduce_scatter | solution.py:659
  468.1 195.0 %reduce-scatter.9.cloned.1.call-start = ((), (), s32[]{:S(2)}) async-start(), calls=%async_computation.10 | async-start | bytes 1310720 | tf_op jit(solution)/shard_map/reduce_scatter | solution.py:624
  474.6 7.9 %copy-start.30 = (bf16[8,128,2048]{2,1,0:T(8,128)(2,1)S(1)}, bf16[8,128,2048]{2,1,0:T(8,128)(2,1)}, u32[]{:S(2)}) copy-start(bf16[8,128,2048]{2,1,0:T(8,128)(2,1)} %tie.1) | copy-start | bytes 12582916
  474.6 7.9 %copy-start.36 = (f32[2,1024,256]{1,2,0:T(8,128)S(1)}, f32[2,1024,256]{1,2,0:T(8,128)}, u32[]{:S(2)}) copy-start(f32[2,1024,256]{1,2,0:T(8,128)} %get-tuple-element.86) | copy-start | bytes 6291460
  474.6 7.9 %copy-start.56 = (bf16[512,2048]{1,0:T(8,128)(2,1)S(1)}, bf16[512,2048]{1,0:T(8,128)(2,1)}, u32[]{:S(2)}) copy-start(bf16[512,2048]{1,0:T(8,128)(2,1)} %all-gather.9.cloned.1.call-done) | copy-start | bytes 6291460
  482.5 2.4 copy-start.4
  482.5 2.4 copy-start.44
  484.9 5.1 copy-start.57
  491.4 1.2 copy-start.32
  493.5 2.4 copy-start.31
  495.9 2.9 copy-start.37
  500.1 4.0 copy-start.35
  504.1 1.9 copy-start.2
  504.1 2.4 copy-start.17
  506.5 68.2 %copy-start.34 = (bf16[8,128,256]{2,1,0:T(8,128)(2,1)S(1)}, bf16[8,128,256]{2,1,0:T(8,128)(2,1)}, u32[]{:S(2)}) copy-start(bf16[8,128,256]{2,1,0:T(8,128)(2,1)} %copy-done.33) | copy-start | bytes 1572868
  574.7 4.2 copy-start.15
  574.7 4.2 copy-start.55
  580.7 79.7 %copy-start.46 = (f32[128]{0:T(128)S(1)}, f32[128]{0:T(128)}, u32[]{:S(2)}) copy-start(f32[128]{0:T(128)} %copy-done.45) | copy-start | bytes 1540
  593.9 1.4 copy-start.9
  595.3 1.1 copy-start.19
  596.4 1.0 copy-start.20
  700.2 4.4 copy-start.24
  707.5 8.4 %copy-start.11 = (f32[128,2048]{1,0:T(8,128)S(1)}, f32[128,2048]{1,0:T(8,128)}, u32[]{:S(2)}) copy-start(f32[128,2048]{1,0:T(8,128)} %copy-done.10) | copy-start | bytes 3145732
  707.5 8.4 %copy-start.23 = (f32[128,2048]{1,0:T(8,128)S(1)}, f32[128,2048]{1,0:T(8,128)}, u32[]{:S(2)}) copy-start(f32[128,2048]{1,0:T(8,128)} %copy.150) | copy-start | bytes 3145732
  707.5 8.4 %copy-start.47 = (f32[128]{0:T(128)S(1)}, f32[128]{0:T(128)}, u32[]{:S(2)}) copy-start(f32[128]{0:T(128)} %get-tuple-element.81) | copy-start | bytes 1540
  716.0 1.3 copy-start.13
  (5 other events, 4.7 us)
Sparse Core Ops, SparseCore 0:
  37.9 33.2 all-gather.4
  72.7 61.9 all-gather.8
  143.1 42.9 all-gather.6
  200.4 84.2 all-gather.10
  358.5 39.9 reduce-scatter.4
  467.5 42.1 reduce-scatter.10
  512.9 80.9 reduce-scatter.6
  596.9 45.1 reduce-scatter.8

commit v3 on v2

--- a/solution.py
+++ b/solution.py
@@ -14,7 +14,8 @@
 
 MESH = pl.DeviceIdType.MESH
 STEP = 16
-VMEM_LIMIT = 48 * 1024 * 1024
+QUERIES = 256
+VMEM_LIMIT = 60 * 1024 * 1024
 COST = pl.CostEstimate(flops=0, transcendentals=0, bytes_accessed=1024)
 
 eps_norm = 1e-06
@@ -130,10 +131,11 @@
         ins = refs[:n_in]
         refs = refs[n_in + len(needs) + len(passes) :]
         outs, scratch = refs[:n_out], refs[n_out + len(passes) :]
-        barrier = pltpu.get_barrier_semaphore()
-        for mask in masks:
-            pl.semaphore_signal(barrier, inc=1, device_id=device(mask), device_id_type=MESH)
-        pl.semaphore_wait(barrier, len(masks))
+        if masks:
+            barrier = pltpu.get_barrier_semaphore()
+            for mask in masks:
+                pl.semaphore_signal(barrier, inc=1, device_id=device(mask), device_id_type=MESH)
+            pl.semaphore_wait(barrier, len(masks))
         running = []
         for task in tasks:
             a, b, c = len(task.inputs), len(task.outputs), len(task.scratch)
@@ -156,7 +158,9 @@
         input_output_aliases={n_in + len(needs) + i: n_out + i for i in range(len(passes))},
         scratch_shapes=[shape for task in tasks for shape in task.scratch],
         compiler_params=pltpu.CompilerParams(
-            collective_id=collective_id, has_side_effects=True, vmem_limit_bytes=VMEM_LIMIT
+            collective_id=collective_id if masks else None,
+            has_side_effects=bool(masks),
+            vmem_limit_bytes=VMEM_LIMIT,
         ),
         cost_estimate=COST,
     )(*[array for array, _ in inputs], *needs, *passes)
@@ -165,6 +169,34 @@
         split.append(results[: len(task.outputs)])
         results = results[len(task.outputs) :]
     return split + results
+
+
+def chain(first, second, links):
+    inputs = [pair for i, pair in enumerate(second.inputs) if i not in links]
+    a, b, c = len(first.inputs), len(first.outputs), len(first.scratch)
+
+    def run(ins, outs, scratch):
+        yield from first.run(ins[:a], outs[:b], scratch[:c])
+        rest = list(ins[a:])
+        joined = [outs[links[i]] if i in links else rest.pop(0) for i in range(len(second.inputs))]
+        yield from second.run(joined, outs[b:], scratch[c:])
+
+    return Task(
+        first.inputs + inputs,
+        first.outputs + second.outputs,
+        first.scratch + second.scratch,
+        first.masks + second.masks,
+        run,
+    )
+
+
+def paused(task, pauses):
+    def run(ins, outs, scratch):
+        for _ in range(pauses):
+            yield
+        yield from task.run(ins, outs, scratch)
+
+    return Task(task.inputs, task.outputs, task.scratch, task.masks, run)
 
 
 def rows_loop(start, stop, step):
@@ -317,6 +349,7 @@
     vec_width,
     sum_axis="chip",
     spread_axis="chip",
+    all_space=ANY,
 ):
     blocks, rows, cols = partial.shape
     far = blocks // 2
@@ -395,7 +428,7 @@
                 across[j].wait_recv()
                 settle(j)
                 sent.append(remote(mine.at[j], arrived.at[j], sems.at[far + j], at_mask[j]))
-                yield
+            yield
             adds = order[:-1]
             landed = sent
         loads[0].wait()
@@ -426,7 +459,8 @@
 
     outputs = []
     if low_width:
-        outputs.append((jax.ShapeDtypeStruct((out_blocks, rows, low_width), jnp.bfloat16), ANY))
+        shape = jax.ShapeDtypeStruct((out_blocks, rows, low_width), jnp.bfloat16)
+        outputs.append((shape, all_space))
     outputs += [(jax.ShapeDtypeStruct((rows, width), jnp.float32), VMEM) for width in own_widths]
     if vec_width:
         outputs.append((jax.ShapeDtypeStruct((STEP, vec_width), jnp.float32), VMEM))
@@ -453,7 +487,7 @@
     return 2 * lax.axis_size("seq")
 
 
-def gather(low, axis):
+def gather(low, axis, all_space=ANY):
     rows, cols = low.shape
     blocks = lax.axis_size("seq") if axis == "chip" else 2 * lax.axis_size("dp")
 
@@ -462,7 +496,7 @@
 
     return Task(
         [(low, ANY)],
-        [(jax.ShapeDtypeStruct((blocks, rows, cols), low.dtype), ANY)],
+        [(jax.ShapeDtypeStruct((blocks, rows, cols), low.dtype), all_space)],
         [pltpu.SemaphoreType.DMA((1,)), pltpu.SemaphoreType.DMA((spread_sems(axis), 2))],
         spread_masks(axis),
         run,
@@ -590,6 +624,491 @@
     )(value, *needs)
 
 
+def gather_chips(low):
+    rows, cols = low.shape
+    masks = axis_masks("chip")
+    square = len(masks) == 3
+
+    def run(ins, outs, scratch):
+        me, _ = here()
+        low_ref, all_ref, (local_sem, sems) = ins[0], outs[0], scratch
+
+        def block(mask):
+            return all_ref.at[device(mask)[0] // 2]
+
+        def half(mask, which):
+            middle = rows // 2 // STEP * STEP
+            part = pl.ds(middle, rows - middle) if which else pl.ds(0, middle)
+            return all_ref.at[device(mask)[0] // 2, part]
+
+        kept = keep(low_ref, block((0, 0)), local_sem.at[0])
+        direct = [(2, 0), (4, 0)] if square else masks
+        copies = [
+            remote(low_ref, block((0, 0)), sems.at[i], mask) for i, mask in enumerate(direct)
+        ]
+        yield
+        if square:
+            for i, mask in enumerate(direct):
+                copies[i].wait_recv()
+                part = half(mask, i)
+                copies.append(remote(part, part, sems.at[2 + i], direct[1 - i]))
+            yield
+            copies[0].wait_send()
+            copies[1].wait_send()
+            copies = copies[2:]
+        for copy in copies:
+            copy.wait()
+        kept.wait()
+
+    return Task(
+        [(low, ANY)],
+        [(jax.ShapeDtypeStruct((len(masks) + 1, rows, cols), low.dtype), ANY)],
+        [pltpu.SemaphoreType.DMA((1,)), pltpu.SemaphoreType.DMA((max(4, len(masks)), 2))],
+        masks,
+        run,
+    )
+
+
+def lanes_of(sources, segments, tile, rows):
+    lane = lax.broadcasted_iota(jnp.int32, (rows, 128), 1)
+    out = jnp.zeros((rows, 128), jnp.float32)
+    low = tile * 128
+    for source, from_col, to_col, length in segments:
+        first, last = max(low, to_col), min(low + 128, to_col + length)
+        if first >= last:
+            continue
+        begin = from_col + first - to_col
+        window = begin // 128 * 128
+        wide = 128 if begin - window + last - first <= 128 else 256
+        held = min(wide, sources[source].shape[1] - window)
+        wide = pl.cdiv(held, 128) * 128
+        piece = sources[source][:, window : window + held].astype(jnp.float32)
+        if held < wide:
+            blank = jnp.zeros((rows, wide - held), jnp.float32)
+            piece = jnp.concatenate([piece, blank], axis=1)
+        shift = (first - low - (begin - window)) % wide
+        if shift:
+            piece = pltpu.roll(piece, shift, axis=1)
+        out = jnp.where((lane >= first - low) & (lane < last - low), piece[:, :128], out)
+    return out
+
+
+def fold(weights, chips, groups):
+    rows, cols = weights[0].shape
+    units = cols // (2 * chips * groups)
+    width = 2 * chips * units
+
+    def body(first_ref, second_ref, out_ref):
+        sources = [first_ref, second_ref]
+        for group in range(groups):
+            for core in range(2):
+                segments = [
+                    (
+                        which,
+                        ((chip * 2 + core) * groups + group) * units,
+                        (which * chips + chip) * units,
+                        units,
+                    )
+                    for which in range(2)
+                    for chip in range(chips)
+                ]
+                for tile in range(pl.cdiv(width, 128)):
+                    value = lanes_of(sources, segments, tile, rows).astype(jnp.bfloat16)
+                    stop = min(width, tile * 128 + 128)
+                    out_ref[group * 2 + core, :, tile * 128 : stop] = value[:, : stop - tile * 128]
+
+    return pl.pallas_call(
+        body,
+        name="fold",
+        out_shape=jax.ShapeDtypeStruct((2 * groups, rows, width), jnp.bfloat16),
+        in_specs=[VMEM, VMEM],
+        out_specs=VMEM,
+        compiler_params=pltpu.CompilerParams(vmem_limit_bytes=VMEM_LIMIT),
+        cost_estimate=COST,
+    )(*weights)
+
+
+def unfold_pair(pieces, chips, groups):
+    _, rows, width = pieces.shape
+    units = width // (2 * chips)
+    cols = units * 2 * chips * groups
+
+    def body(in_ref, first_ref, second_ref):
+        sources = [in_ref.at[i] for i in range(2 * groups)]
+        for which, out_ref in enumerate([first_ref, second_ref]):
+            segments = [
+                (
+                    group * 2 + core,
+                    (which * chips + chip) * units,
+                    ((chip * 2 + core) * groups + group) * units,
+                    units,
+                )
+                for chip in range(chips)
+                for core in range(2)
+                for group in range(groups)
+            ]
+            for tile in range(cols // 128):
+                out_ref[:, tile * 128 : tile * 128 + 128] = lanes_of(sources, segments, tile, rows)
+
+    shape = jax.ShapeDtypeStruct((rows, cols), jnp.float32)
+    return pl.pallas_call(
+        body,
+        name="unfold",
+        out_shape=[shape, shape],
+        in_specs=[VMEM],
+        out_specs=[VMEM, VMEM],
+        compiler_params=pltpu.CompilerParams(vmem_limit_bytes=VMEM_LIMIT),
+        cost_estimate=COST,
+    )(pieces)
+
+
+def nt(left, right):
+    return lax.dot_general(
+        left, right, (((1,), (1,)), ((), ())), preferred_element_type=jnp.float32
+    )
+
+
+def tn(left, right):
+    return lax.dot_general(
+        left, right, (((0,), (0,)), ((), ())), preferred_element_type=jnp.float32
+    )
+
+
+def window_of(i, tokens):
+    wide = tokens // 2 + QUERIES
+    start = jnp.clip(i * QUERIES - tokens // 2, 0, tokens - wide)
+    return pl.multiple_of(start, QUERIES), wide
+
+
+def probabilities(queries, keys, i, start, seg_col, seg_row):
+    scores = nt(queries, keys) * (1.0 / math.sqrt(E))
+    row = i * QUERIES + lax.broadcasted_iota(jnp.int32, scores.shape, 0)
+    col = start + lax.broadcasted_iota(jnp.int32, scores.shape, 1)
+    scores = jnp.where((seg_col == seg_row) & (col <= row), scores, big_negative)
+    shifted = jnp.exp(scores - jnp.max(scores, axis=-1, keepdims=True))
+    return shifted / jnp.sum(shifted, axis=-1, keepdims=True)
+
+
+def attend(gathered, qb_cols, cosine, sine_tab, seg_col, seg_rows):
+    tokens, inner = gathered.shape
+    rank, width = qb_cols.shape
+
+    def run(ins, outs, scratch):
+        in_ref, qb_ref, cos_ref, sin_ref, seg_ref, segs_ref = ins
+        q_ref, out_ref = outs
+
+        def block(i, carry):
+            at = pl.ds(pl.multiple_of(i * QUERIES, QUERIES), QUERIES)
+            start, wide = window_of(i, tokens)
+            span = pl.ds(start, wide)
+            query = dot(in_ref[at, :rank], qb_ref[...])
+            keys, values = in_ref[span, rank : rank + E], in_ref[span, rank + E :]
+            for head in range(width // E):
+                lanes = slice(head * E, head * E + E)
+                rotated = rotate(query[:, lanes], cos_ref[at, :], sin_ref[at, :])
+                rotated = rotated.astype(jnp.bfloat16)
+                q_ref[at, lanes] = rotated
+                probs = probabilities(rotated, keys, i, start, seg_ref[at, :], segs_ref[i])
+                out_ref[at, lanes] = dot(probs.astype(jnp.bfloat16), values).astype(jnp.bfloat16)
+            return carry
+
+        lax.fori_loop(0, tokens // QUERIES, block, 0)
+        yield
+
+    shape = jax.ShapeDtypeStruct((tokens, width), jnp.bfloat16)
+    return Task(
+        [(a, VMEM) for a in (gathered, qb_cols, cosine, sine_tab, seg_col, seg_rows)],
+        [(shape, VMEM), (shape, VMEM)],
+        [],
+        [],
+        run,
+    )
+
+
+def attend_back(
+    gathered, queries, out_grad, o_rows, qb_cols, cosine, sine_tab, seg_col, seg_rows
+):
+    tokens, inner = gathered.shape
+    rank, width = qb_cols.shape
+    scale = 1.0 / math.sqrt(E)
+
+    def run(ins, outs, scratch):
+        in_ref, q_ref, grad_ref, o_ref, qb_ref, cos_ref, sin_ref, seg_ref, segs_ref = ins
+        dq_ref, part_ref = outs
+        key_sum, value_sum = scratch
+        key_sum[...] = jnp.zeros_like(key_sum)
+        value_sum[...] = jnp.zeros_like(value_sum)
+
+        def block(i, carry):
+            at = pl.ds(pl.multiple_of(i * QUERIES, QUERIES), QUERIES)
+            start, wide = window_of(i, tokens)
+            span = pl.ds(start, wide)
+            per = QUERIES // grad_ref.shape[1]
+            upstream = grad_ref[pl.ds(i * per, per)].reshape(QUERIES, grad_ref.shape[2])
+            attended_grad = nt(upstream, o_ref[...]).astype(jnp.bfloat16)
+            keys, values = in_ref[span, rank : rank + E], in_ref[span, rank + E :]
+            for head in range(width // E):
+                lanes = slice(head * E, head * E + E)
+                query, upstream = q_ref[at, lanes], attended_grad[:, lanes]
+                probs = probabilities(query, keys, i, start, seg_ref[at, :], segs_ref[i])
+                value_sum[span, :] += tn(probs.astype(jnp.bfloat16), upstream)
+                prob_grad = nt(upstream, values)
+                delta = jnp.sum(probs * prob_grad, axis=-1, keepdims=True)
+                score_grad = (probs * (prob_grad - delta)).astype(jnp.bfloat16)
+                key_sum[span, :] += tn(score_grad, query)
+                query_grad = dot(score_grad, keys) * scale
+                query_grad = rotate_back(query_grad, cos_ref[at, :], sin_ref[at, :])
+                dq_ref[at, lanes] = query_grad.astype(jnp.bfloat16)
+            part_ref[at, :rank] = nt(dq_ref[at, :], qb_ref[...]).astype(jnp.bfloat16)
+            return carry
+
+        lax.fori_loop(0, tokens // QUERIES, block, 0)
+        part_ref[:, rank : rank + E] = (key_sum[...] * scale).astype(jnp.bfloat16)
+        part_ref[:, rank + E :] = value_sum[...].astype(jnp.bfloat16)
+        yield
+
+    return Task(
+        [
+            (a, VMEM)
+            for a in (
+                gathered,
+                queries,
+                out_grad,
+                o_rows,
+                qb_cols,
+                cosine,
+                sine_tab,
+                seg_col,
+                seg_rows,
+            )
+        ],
+        [
+            (jax.ShapeDtypeStruct((tokens, width), jnp.bfloat16), VMEM),
+            (jax.ShapeDtypeStruct((tokens, inner), jnp.bfloat16), VMEM),
+        ],
+        [pltpu.VMEM((tokens, E), jnp.float32), pltpu.VMEM((tokens, E), jnp.float32)],
+        [],
+        run,
+    )
+
+
+def feed_forward(two_all, grad_all, both_cols, down_rows, mixed_rows, out_grad, gain_two):
+    line, rows, cols = two_all.shape
+    units = down_rows.shape[0]
+    far = line // 2
+    chips, groups = lax.axis_size("seq") // 2, lax.axis_size("dp")
+    masks = axis_masks("dp")
+    at_mask = [(0, 0)] + masks
+    order = list(range(far - 1, 0, -1)) + [0]
+    slab = cols // (2 * chips)
+    piece = slab // groups
+
+    def run(ins, outs, scratch):
+        two_ref, grad_ref, both_ref, down_ref, mixed_ref, dy_ref, gain_ref = ins
+        mixed_out, low_out, vec_out, y_out, down_out, both_out = outs
+        mine, give, beside, arrived, hidden, pair_grad, stage, sems, stage_sem = scratch
+        core = here()[0] % 2
+
+        def produce(j):
+            block = device(at_mask[j])[1] * 2
+            both = pl.ds(block, 2)
+            x = two_ref[both].reshape(2 * rows, cols)
+            dy = grad_ref[both].reshape(2 * rows, cols)
+            act = dot(x, both_ref[...])
+            gate, up = act[:, :units], act[:, units:]
+            sigmoid = jax.nn.sigmoid(gate)
+            silu = gate * sigmoid
+            hid = (silu * up).astype(jnp.bfloat16)
+            hidden[both] = hid.reshape(2, rows, units)
+            y_out[both] = dot(hid, down_ref[...]).astype(jnp.bfloat16).reshape(2, rows, cols)
+            hid_grad = nt(dy, down_ref[...])
+            gate_grad = hid_grad * up * (sigmoid * (1.0 + gate * (1.0 - sigmoid)))
+            up_grad = hid_grad * silu
+            pair = jnp.concatenate([gate_grad, up_grad], axis=1).astype(jnp.bfloat16)
+            pair_grad[both] = pair.reshape(2, rows, 2 * units)
+            part = nt(pair, both_ref[...]).astype(jnp.bfloat16)
+
+            @pl.when(core == 0)
+            def _():
+                mine[j], give[j] = part[:rows], part[rows:]
+
+            @pl.when(core == 1)
+            def _():
+                mine[j], give[j] = part[rows:], part[:rows]
+
+        across, sent = {}, {}
+
+        def settle(j):
+            across[j].wait_recv()
+
+            def add(at):
+                total = mine[j, at, :].astype(jnp.float32) + beside[j, at, :].astype(jnp.float32)
+                mine[j, at, :] = total.astype(jnp.bfloat16)
+
+            rows_loop(0, rows, add)
+            sent[j] = remote(mine.at[j], arrived.at[j], sems.at[far + j], at_mask[j])
+
+        last = None
+        for j in order:
+            produce(j)
+            across[j] = remote(give.at[j], beside.at[j], sems.at[j], SIBLING)
+            if last is not None:
+                settle(last)
+            last = j
+        yield
+
+        down_out[...] = tn(
+            hidden[...].reshape(line * rows, units), grad_ref[...].reshape(line * rows, cols)
+        ).astype(jnp.bfloat16)
+        moves = []
+        for index in range(2 * chips):
+            slot = index % 2
+            if index >= 2:
+                for move in moves[(index - 2) * groups : (index - 1) * groups]:
+                    move.wait()
+            x = two_ref[:, :, index * slab : (index + 1) * slab].reshape(line * rows, slab)
+            value = tn(x, pair_grad[...].reshape(line * rows, 2 * units))
+            stage[slot] = value.astype(jnp.bfloat16).reshape(groups, piece, 2 * units)
+            for group in range(groups):
+                place = ((index // 2) * groups + group) * 2 + index % 2
+                moves.append(
+                    keep(stage.at[slot, group], both_out.at[place], stage_sem.at[slot, group])
+                )
+        for move in moves[-2 * groups :]:
+            move.wait()
+
+        across[0].wait_recv()
+        for j in order[:-1]:
+            sent[j].wait_recv()
+        vec_out[...] = jnp.zeros_like(vec_out)
+        gain = gain_ref[...]
+
+        def finish(at):
+            total = mine[0, at, :].astype(jnp.float32) + beside[0, at, :].astype(jnp.float32)
+            for j in order[:-1]:
+                total = total + arrived[j, at, :].astype(jnp.float32)
+            value_grad, gain_grad = back_rows(mixed_ref[at, :], gain, total)
+            mixed_grad = dy_ref[at, :] + value_grad
+            mixed_out[at, :] = mixed_grad
+            low_out[at, :] = mixed_grad.astype(jnp.bfloat16)
+            vec_out[...] += gain_grad
+
+        rows_loop(0, rows, finish)
+        for copy in list(across.values()) + list(sent.values()):
+            copy.wait_send()
+
+    def low(*shape):
+        return jax.ShapeDtypeStruct(shape, jnp.bfloat16)
+
+    blocks = pltpu.VMEM((far, rows, cols), jnp.bfloat16)
+    return Task(
+        [
+            (a, VMEM)
+            for a in (two_all, grad_all, both_cols, down_rows, mixed_rows, out_grad, gain_two)
+        ],
+        [
+            (jax.ShapeDtypeStruct((rows, cols), jnp.float32), VMEM),
+            (low(rows, cols), VMEM),
+            (jax.ShapeDtypeStruct((STEP, cols), jnp.float32), VMEM),
+            (low(line, rows, cols), VMEM),
+            (low(units, cols), VMEM),
+            (low(2 * chips * groups, piece, 2 * units), ANY),
+        ],
+        [
+            blocks,
+            blocks,
+            blocks,
+            blocks,
+            pltpu.VMEM((line, rows, units), jnp.bfloat16),
+            pltpu.VMEM((line, rows, 2 * units), jnp.bfloat16),
+            pltpu.VMEM((2, groups, piece, 2 * units), jnp.bfloat16),
+            pltpu.SemaphoreType.DMA((2 * far, 2)),
+            pltpu.SemaphoreType.DMA((2, groups)),
+        ],
+        [SIBLING] + masks,
+        run,
+    )
+
+
+def chip_sum(partial):
+    chips, rows, cols = partial.shape
+    masks = axis_masks("chip")
+    square = chips == 4
+    middle = rows // 2 // STEP * STEP
+
+    def run(ins, outs, scratch):
+        (in_ref,), (out_ref,) = ins, outs
+        arrived, held, local_sem, sems = scratch
+
+        def block(j):
+            return device(([(0, 0)] + masks)[j])[0] // 2
+
+        def add(target, start, stop, *terms):
+            def one(at):
+                total = terms[0][at, :].astype(jnp.float32)
+                for term in terms[1:]:
+                    total = total + term[at, :].astype(jnp.float32)
+                target[at, :] = total.astype(jnp.bfloat16)
+
+            rows_loop(start, stop, one)
+
+        own = keep(in_ref.at[block(0)], held.at[0], local_sem.at[0])
+        if not square:
+            copies = [
+                remote(in_ref.at[block(j)], arrived.at[j - 1], sems.at[j - 1], masks[j - 1])
+                for j in range(1, chips)
+            ]
+            yield
+            own.wait()
+            for copy in copies:
+                copy.wait_recv()
+            add(out_ref, 0, rows, held.at[0], *[arrived.at[j] for j in range(chips - 1)])
+            for copy in copies:
+                copy.wait_send()
+            return
+        first, second = pl.ds(0, middle), pl.ds(middle, rows - middle)
+        over_x, over_y = (2, 0), (4, 0)
+        copies = [
+            remote(in_ref.at[block(3), first], arrived.at[2, first], sems.at[0], over_x),
+            remote(in_ref.at[block(3), second], arrived.at[2, second], sems.at[1], over_y),
+            remote(in_ref.at[block(1), first], arrived.at[0, first], sems.at[2], over_x),
+            remote(in_ref.at[block(2), second], arrived.at[1, second], sems.at[3], over_y),
+        ]
+        loads = [
+            keep(in_ref.at[block(2), first], held.at[1, first], local_sem.at[1]),
+            keep(in_ref.at[block(1), second], held.at[1, second], local_sem.at[2]),
+        ]
+        yield
+        loads[0].wait()
+        copies[0].wait_recv()
+        add(held.at[1], 0, middle, held.at[1], arrived.at[2])
+        copies.append(remote(held.at[1, first], arrived.at[1, first], sems.at[4], over_y))
+        loads[1].wait()
+        copies[1].wait_recv()
+        add(held.at[1], middle, rows, held.at[1], arrived.at[2])
+        copies.append(remote(held.at[1, second], arrived.at[0, second], sems.at[5], over_x))
+        yield
+        own.wait()
+        for copy in copies[2:]:
+            copy.wait_recv()
+        add(out_ref, 0, rows, held.at[0], arrived.at[0], arrived.at[1])
+        for copy in copies:
+            copy.wait_send()
+
+    return Task(
+        [(partial, ANY)],
+        [(jax.ShapeDtypeStruct((rows, cols), jnp.bfloat16), VMEM)],
+        [
+            pltpu.VMEM((chips - 1, rows, cols), jnp.bfloat16),
+            pltpu.VMEM((2, rows, cols), jnp.bfloat16),
+            pltpu.SemaphoreType.DMA((3,)),
+            pltpu.SemaphoreType.DMA((max(6, chips), 2)),
+        ],
+        masks,
+        run,
+    )
+
+
 def dot(left, right):
     return jnp.dot(left, right, preferred_element_type=jnp.float32)
 
@@ -633,18 +1152,6 @@
 def unfold(pieces):
     parts, rows, cols = pieces.shape
     return jnp.transpose(pieces, (1, 0, 2)).reshape(rows, parts * cols).astype(jnp.float32)
-
-
-def line_columns(weight, chips, groups):
-    rows, cols = weight.shape
-    low = weight.astype(jnp.bfloat16).reshape(rows, chips, 2, groups, -1)
-    return jnp.transpose(low, (3, 2, 0, 1, 4)).reshape(2 * groups, rows, -1)
-
-
-def line_unfold(pieces, chips, groups):
-    rows = pieces.shape[1]
-    full = pieces.reshape(groups, 2, rows, chips, -1)
-    return jnp.transpose(full, (2, 3, 1, 0, 4)).reshape(rows, -1).astype(jnp.float32)
 
 
 def chip_groups(parts):
@@ -741,7 +1248,9 @@
         )
         return low, [total], None
 
-    (gathered, inner_own), (grad_all,), down_low = launch(
+    chips = parts // 2
+    both_cols = fold(list(lax.optimization_barrier((w_gate, w_up))), chips, groups)
+    (gathered, inner_own), (both_cols,), (down_rows,) = launch(
         "latent",
         1,
         [
@@ -754,46 +1263,32 @@
                 inner,
                 0,
             ),
-            gather(out_grad.astype(jnp.bfloat16), "dp"),
-        ],
-        passes=[w_down.astype(jnp.bfloat16)],
-    )
-    grad_all = grad_all.reshape(-1, D)
-    down_rows = chip_gather(down_low, parts)
-    chips = parts // 2
-    both_cols = jnp.concatenate(
-        [line_columns(w_gate, chips, groups), line_columns(w_up, chips, groups)], axis=2
-    )
-    ((both_cols,),) = launch("gate_up", 2, [swap(both_cols, "line")], needs=[gathered])
+            swap(both_cols, "line"),
+            gather_chips(w_down.astype(jnp.bfloat16)),
+        ],
+    )
     gathered = gathered.reshape(group_tokens, inner)
-    units = both_cols.shape[2] // 2
-    latent_all = gathered[:, :rank]
-    keys_all = gathered[:, rank : rank + E]
-    values_all = gathered[:, rank + E :]
-
-    query = dot(latent_all, qb_cols).reshape(group_tokens, heads, E)
-    query = jnp.transpose(query, (1, 0, 2))
-    q_rot = rotate(query, cos_all[None], sin_all[None]).astype(jnp.bfloat16)
-    allowed = (segment[:, None] == segment[None, :]) & (places[None, :] <= places[:, None])
-    scores = (
-        jnp.einsum("htd,kd->htk", q_rot, keys_all, preferred_element_type=jnp.float32)
-        * score_scale
-    )
-    scores = jnp.where(allowed[None], scores, big_negative)
-    shifted = jnp.exp(scores - jnp.max(scores, axis=-1, keepdims=True))
-    probs = shifted / jnp.sum(shifted, axis=-1, keepdims=True)
-    probs_low = probs.astype(jnp.bfloat16)
-    attended = jnp.einsum("htk,kd->htd", probs_low, values_all, preferred_element_type=jnp.float32)
-    attended_low = jnp.transpose(attended.astype(jnp.bfloat16), (1, 0, 2)).reshape(
-        group_tokens, heads * E
-    )
+    seg_col = segment[:, None]
+    seg_rows = jnp.stack(
+        [
+            lax.slice_in_dim(segment, start, start + group_tokens // 2 + QUERIES)
+            for start in [
+                min(max(0, first - group_tokens // 2), group_tokens // 2 - QUERIES)
+                for first in range(0, group_tokens, QUERIES)
+            ]
+        ]
+    )[:, None, :]
+    ((q_rot, attended_low),) = launch(
+        "attend", 2, [attend(gathered, qb_cols, cos_all, sin_all, seg_col, seg_rows)]
+    )
+    down_rows = down_rows.reshape(-1, D)
     partial = dot(attended_low, o_rows).astype(jnp.bfloat16).reshape(parts, tok_rows, D)
 
     def mixed_function(total, row, vec):
         mixed = row[0] + total
         return rms_scale(mixed, vec[0]), [mixed], None
 
-    ((two_all, mixed_rows),) = launch(
+    (two_all, mixed_rows), (grad_all,) = launch(
         "mixed",
         3,
         [
@@ -806,91 +1301,59 @@
                 D,
                 0,
                 spread_axis="dp",
-            )
-        ],
-        needs=[down_rows],
-    )
-    two_all = two_all.reshape(-1, D)
+            ),
+            gather(out_grad.astype(jnp.bfloat16), "dp"),
+        ],
+    )
     wide = both_cols.shape[2]
     piece = both_cols.shape[1]
     both_cols = chip_gather(both_cols.reshape(-1, wide), parts)
     both_cols = both_cols.reshape(chips, groups, 2, piece, wide)
     both_cols = jnp.transpose(both_cols, (0, 2, 1, 3, 4)).reshape(D, wide)
 
-    both_act = dot(two_all, both_cols)
-    gate_act, up_act = both_act[:, :units], both_act[:, units:]
-    sigmoid_gate = jax.nn.sigmoid(gate_act)
-    hidden = (gate_act * sigmoid_gate * up_act).astype(jnp.bfloat16)
-    hidden_grad = jnp.einsum("td,fd->tf", grad_all, down_rows, preferred_element_type=jnp.float32)
-    gate_grad = (
-        hidden_grad * up_act * (sigmoid_gate * (1.0 + gate_act * (1.0 - sigmoid_gate)))
-    ).astype(jnp.bfloat16)
-    up_grad = (hidden_grad * (gate_act * sigmoid_gate)).astype(jnp.bfloat16)
-    down_low = jnp.einsum("tf,td->fd", hidden, grad_all, preferred_element_type=jnp.float32)
-    down_low = down_low.astype(jnp.bfloat16)
-    down_shard = chip_scatter(down_low, parts)
-    both_grad = jnp.concatenate([gate_grad, up_grad], axis=1)
-    both_low = jnp.einsum("td,tf->df", two_all, both_grad, preferred_element_type=jnp.float32)
-    both_low = both_low.astype(jnp.bfloat16).reshape(chips, 2, groups, piece, wide)
-    both_low = jnp.transpose(both_low, (0, 2, 1, 3, 4)).reshape(D, wide)
-    both_shard = chip_scatter(both_low, parts).reshape(2 * groups, piece, wide)
-    two_part = jnp.einsum(
-        "tf,df->td", both_grad, both_cols, preferred_element_type=jnp.float32
-    ).astype(jnp.bfloat16)
-
-    def two_function(total, row, vec):
-        value_grad, gain_grad = back_rows(row[0], vec[0], total)
-        mixed_grad = row[1] + value_grad
-        return mixed_grad, [mixed_grad], gain_grad
-
-    ((mixed_all, mixed_grad, gain_two_grad),) = launch(
-        "two_grad",
+    ((mixed_grad, mixed_low, gain_two_grad, out_part, down_low, both_low),) = launch(
+        "feed_forward",
+        9,
+        [
+            feed_forward(
+                two_all, grad_all, both_cols, down_rows, mixed_rows, out_grad, gain_two
+            )
+        ],
+    )
+    both_shard = chip_scatter(both_low.reshape(D, wide), parts).reshape(2 * groups, piece, wide)
+
+    def out_function(total, row, vec):
+        return None, [row[0] + total], None
+
+    mixed_task = gather(mixed_low, "chip", VMEM)
+    back_task = attend_back(
+        gathered,
+        q_rot,
+        jax.ShapeDtypeStruct((parts, tok_rows, D), jnp.bfloat16),
+        o_rows,
+        qb_cols,
+        cos_all,
+        sin_all,
+        seg_col,
+        seg_rows,
+    )
+    (output_rows,), (mixed_all, query_grad, partial) = launch(
+        "attend_back",
         4,
         [
-            exchange(
-                two_part.reshape(2 * groups, tok_rows, D),
-                [mixed_rows, out_grad],
-                [gain_two],
-                two_function,
-                [D],
-                D,
-                D,
-                sum_axis="dp",
-            )
-        ],
-        needs=[down_low, both_low],
-    )
-    mixed_all = tie(mixed_all, [down_shard]).reshape(group_tokens, D)
+            exchange(out_part, [mixed_rows], [], out_function, [D], 0, 0, sum_axis="dp"),
+            chain(mixed_task, back_task, {2: 0}),
+        ],
+    )
+    mixed_all = tie(mixed_all, [both_shard]).reshape(group_tokens, D)
     o_shard, o_low = scatter_rows(
         jnp.einsum("tf,td->fd", attended_low, mixed_all, preferred_element_type=jnp.float32)
     )
-    att_grad = jnp.einsum("td,fd->tf", mixed_all, o_rows, preferred_element_type=jnp.float32)
-    att_grad = jnp.transpose(
-        att_grad.astype(jnp.bfloat16).reshape(group_tokens, heads, E), (1, 0, 2)
-    )
-    delta_rows = jnp.sum(att_grad.astype(jnp.float32) * attended, axis=-1)
-    value_grads = jnp.einsum(
-        "htk,htd->kd", probs_low, att_grad, preferred_element_type=jnp.float32
-    )
-    prob_grad = jnp.einsum("htd,kd->htk", att_grad, values_all, preferred_element_type=jnp.float32)
-    score_grad = (probs * (prob_grad - delta_rows[..., None])).astype(jnp.bfloat16)
-    query_grad = (
-        jnp.einsum("htk,kd->htd", score_grad, keys_all, preferred_element_type=jnp.float32)
-        * score_scale
-    )
-    key_grads = (
-        jnp.einsum("htk,htd->kd", score_grad, q_rot, preferred_element_type=jnp.float32)
-        * score_scale
-    )
-    query_grad = rotate_back(query_grad, cos_all[None], sin_all[None]).astype(jnp.bfloat16)
-    query_grad = jnp.transpose(query_grad, (1, 0, 2)).reshape(group_tokens, heads * E)
     qb_shard, qb_low = scatter_columns(
-        jnp.einsum("tr,tf->rf", latent_all, query_grad, preferred_element_type=jnp.float32),
+        jnp.einsum("tr,tf->rf", gathered[:, :rank], query_grad, preferred_element_type=jnp.float32),
         parts,
         groups,
     )
-    latent_part = jnp.einsum("tf,rf->tr", query_grad, qb_cols, preferred_element_type=jnp.float32)
-    partial = jnp.concatenate([latent_part, key_grads, value_grads], axis=1).astype(jnp.bfloat16)
 
     def inner_function(total, row, vec):
         latent_grad, latent_gain = back_rows(row[0][:, :rank], vec[0], total[:, :rank])
@@ -899,12 +1362,7 @@
         low = jnp.concatenate([latent_grad, key_grad, total[:, rank + E :]], axis=1)
         return low, [], jnp.concatenate([latent_gain, key_gain], axis=1)
 
-    out_part = dot(hidden, down_rows).astype(jnp.bfloat16).reshape(2 * groups, tok_rows, D)
-
-    def out_function(total, row, vec):
-        return None, [row[0] + total], None
-
-    (in_grad, inner_gain_grad), (output_rows,) = launch(
+    (in_grad, inner_gain_grad), (both_shard,), (down_shard,) = launch(
         "inner_grad",
         5,
         [
@@ -917,7 +1375,8 @@
                 inner,
                 rank + E,
             ),
-            exchange(out_part, [mixed_rows], [], out_function, [D], 0, 0, sum_axis="dp"),
+            swap(both_shard, "line"),
+            paused(chip_sum(down_low.reshape(chips, -1, D)), 2),
         ],
         needs=[o_low, qb_low],
     )
@@ -927,10 +1386,10 @@
     normed_part = jnp.einsum("tr,dr->td", in_grad, in_rows, preferred_element_type=jnp.float32)
     normed_part = normed_part.astype(jnp.bfloat16).reshape(parts, tok_rows, width)
 
-    (normed_grad,), (in_shard,), (both_shard,) = launch(
+    (normed_grad,), (in_shard,) = launch(
         "normed_grad",
         6,
-        [swap(normed_part, "seq"), swap(in_low, "dp"), swap(both_shard, "line")],
+        [swap(normed_part, "seq"), swap(in_low, "dp")],
     )
     in_shard = jnp.sum(in_shard.astype(jnp.float32), axis=0)
     normed_grad = jnp.transpose(normed_grad.astype(jnp.float32), (1, 0, 2)).reshape(tok_rows, D)
@@ -952,6 +1411,7 @@
         axis=2,
     )
     (gain_own,), (qb_shard,) = launch("end", 7, [sum_both(gain_grads), swap(qb_shard, "seq")])
+    gate_grad, up_grad = unfold_pair(both_shard, chips, groups)
     return (
         output_rows.reshape(1, tok_rows, D),
         input_grad.reshape(1, tok_rows, D),
@@ -964,8 +1424,8 @@
         in_shard[:, rank + E :],
         o_shard.astype(jnp.float32),
         gain_own[3, : spans[3]],
-        line_unfold(both_shard[:, :, :units], chips, groups),
-        line_unfold(both_shard[:, :, units:], chips, groups),
+        gate_grad,
+        up_grad,
         down_shard.astype(jnp.float32),
     )
 

time: 731 us -> 599 us (0.82)
  matrix products: 104 us -> 23 us
  local copies, waits for them, and re-layouts: 99.3 us -> 30.4 us
  Pallas kernels: 446 us -> 503 us
  other arithmetic: 46.6 us -> 20.5 us
  waiting for transfers between devices: 12.6 us -> 0.82 us
    dot_general x12 -> x1, matrix products: 56.4 us -> 2.52 us  [local(): jnp.einsum('tr,tf->rf', gathered[:, :rank], query_grad, preferred_element...]
    pallas_call x8 -> x9, Pallas kernels: 446 us -> 495 us  [launch(): pl.pallas_call(body, name=name, out_shape=[shape for shape, _ in outputs]...]
    reshape x8 -> x0, local copies, waits for them, and re-layouts: 26.9 us -> none  [the longest x4 15.4 us: line_columns(): low = weight.astype(jnp.bfloat16).reshape(rows, chips, 2, groups, -1)]
    convert_element_type x6 -> x0, local copies, waits for them, and re-layouts: 21.5 us -> none  [line_unfold(): jnp.transpose(full, (2, 3, 1, 0, 4)).reshape(rows, -1).astype(jnp.float32)]
    dot_general x5 -> x2, matrix products: 28.2 us -> 8.88 us  [dot(): return jnp.dot(left, right, preferred_element_type=jnp.float32)]
    unnamed x125 -> x54, local copies, waits for them, and re-layouts: 21.9 us -> 5.56 us
    convert_element_type x6 -> x0, other arithmetic: 16.2 us -> none  [the longest x1 6.61 us: local(): probs_low = probs.astype(jnp.bfloat16)]
    reduce_scatter x2 -> x1, waiting for transfers between devices: 11.1 us -> 0.02 us  [chip_scatter(): lax.psum_scatter(rows, 'seq', scatter_dimension=0, tiled=True, axis_index...]
  transfers between devices with their start and end apart: 8 -> 6, of which waited for: 1 -> 0; matrix products, arithmetic and copies ran while one was open for 22% -> 9% of each run, Pallas kernels for 56% -> 68%
where the time goes in v3:
time: 599 us; the launch traced here: 594 us
  Pallas kernels  503 us (84%)
  local copies, waits for them, and re-layouts  30.4 us (5%)
  matrix products  23 us (4%)
  other arithmetic  20.5 us (3%)
  between operations  15.1 us (3%)
    pallas_call x9, Pallas kernels, launch(): pl.pallas_call(body, name=name, out_shape=[shape for shape, _ in outputs]...  495 us
  transfers between devices with their start and end apart: 6, of which 0 were waited for; matrix products, arithmetic and copies ran while one was open for 9% of the time, Pallas kernels for 68%

profile of v3, /device:TPU:0, one launch (start us, length us, event | category | flops | bytes accessed | tf_op | source)
XLA Modules:
  0.0 593.6 jit_solution(5650149854957167808)
XLA Ops:
  7.3 1.5 multiply_reduce_fusion.2
  8.7 1.6 copy.46
  10.4 0.3 copy.47
  10.7 0.8 pad_bitcast_fusion.2
  11.5 0.6 reduce_precision.3.refs_0_
  12.1 1.1 convert_element_type.81
  13.2 0.7 copy.63
  13.9 0.9 convert_element_type.82.refs_4_
  14.9 1.1 multiply_bitcast_fusion.refs_1_
  16.0 0.7 pad_maximum_fusion.1.refs_2_
  16.7 25.3 %start.1 = (f32[8,4,8,128]{3,2,1,0:T(8,128)}, f32[4,8,128]{2,1,0:T(8,128)}, f32[8,128,256]{2,1,0:T(8,128)}, bf16[4,64,1536]{2,1,0:T(8,128)(2,1)}, bf16[8,32,512]...) custom-call(f32[8,128]{1,0:T(8,128)} %reduce_precision.3.refs_0_, ...), custom_call_target="tpu_custom_call", output_to_operand_aliasing={{5}: (4, {})} | custom-call | bytes 1024 | tf_op jit(solution)/shard_map/start/pallas_call | solution.py:151
  42.1 0.7 all-gather.6.cloned.1.call-update
  42.8 0.7 slice_reduce_fusion.6
  43.6 1.0 slice_reduce_fusion.5
  44.6 0.7 reshape_squeeze.11.refs_3_.refs_4_
  45.3 1.0 slice_reduce_fusion.4
  46.3 0.6 reshape_squeeze.12.refs_4_.refs_5_
  47.1 1.0 convert_element_type.87.refs_6_
  48.0 4.0 fold.1.refs_5_
  52.1 0.2 broadcast_multiply_fusion
  52.3 3.7 fusion.6
  56.0 0.8 constant_dynamic-slice_fusion
  57.0 2.6 convolution_convert_fusion
  59.6 70.0 %latent.1 = (bf16[8,128,1536]{2,1,0:T(8,128)(2,1)}, f32[128,1536]{1,0:T(8,128)}, bf16[8,64,1408]{2,1,0:T(8,128)(2,1)}, bf16[4,176,2048]{2,1,0:T(8,128)(2,1)}) custom-call(bf16[8,128,1536]{2,1,0:T(8,128)(2,1)} %bitcast.97, f32[128,256]{1,0:T(8,128)} %get-tuple-element.107.refs_1_.refs_2_, f32[128,256]{1,0:T(8,128)} %get-tuple-element.106.refs_2_.refs_3_, ...), custom_call_target="tpu_custom_call" | custom-call | bytes 1024 | tf_op jit(solution)/shard_map/latent/pallas_call | solution.py:151
  129.6 0.5 reduce-scatter.4.cloned.1.call-start
  130.2 0.6 broadcast_in_dim.51.refs_5_.refs_10_
  130.8 1.0 copy.50.refs_4_.refs_9_
  131.8 1.1 slice_reduce_fusion.2
  132.9 0.7 reshape_squeeze.13.refs_2_.refs_6_
  133.6 0.9 bitcast_convert_fusion.refs_3_
  134.5 2.3 copy.49
  136.8 10.1 %attend.1 = (bf16[1024,512]{1,0:T(8,128)(2,1)}, bf16[1024,512]{1,0:T(8,128)(2,1)}) custom-call(bf16[1024,1536]{1,0:T(8,128)(2,1)} %bitcast.99, bf16[1024,512]{1,0:T(8,128)(2,1)} %bitcast.102, f32[1024,256]{1,0:T(8,128)} %copy-done.3, f32[1024,256]{1,0:T(8,128)} %copy-done.2, s32[1024,1]{1,0:T(8,128)} %copy.50.refs_4_.refs_9_, ...), custom_call_target="tpu_custom_call" | custom-call | bytes 1024 | tf_op jit(solution)/shard_map/attend/pallas_call | solution.py:151
  146.8 6.3 %convolution_convert_fusion.1 = bf16[1024,2048]{1,0:T(8,128)(2,1)} fusion(bf16[1024,512]{1,0:T(8,128)(2,1)} %get-tuple-element.59, bf16[512,2048]{1,0:T(8,128)(2,1)} %all-gather.6.cloned.1.call-done.refs_5_), kind=kOutput, calls=%fused_computation.1 | convolution fusion | flops 2149580800 | bytes 7340032 | tf_op jit(solution)/shard_map/dot_general | solution.py:1113
  153.1 108.1 %mixed.1 = (bf16[8,128,2048]{2,1,0:T(8,128)(2,1)}, f32[128,2048]{1,0:T(8,128)}, bf16[8,128,2048]{2,1,0:T(8,128)(2,1)}) custom-call(bf16[8,128,2048]{2,1,0:T(8,128)(2,1)} %bitcast.112, f32[128,2048]{1,0:T(8,128)} %bitcast.96, f32[1,2048]{1,0:T(1,128)} %reshape_squeeze.13.refs_2_.refs_6_, bf16[128,2048]{1,0:T(8,128)(2,1)} %bitcast_convert_fusion.refs_3_), custom_call_target="tpu_custom_call" | custom-call | bytes 1024 | tf_op jit(solution)/shard_map/mixed/pallas_call | solution.py:151
  261.2 5.7 copy.51
  267.0 72.7 %feed_forward.1 = (f32[128,2048]{1,0:T(8,128)}, bf16[128,2048]{1,0:T(8,128)(2,1)}, f32[16,2048]{1,0:T(8,128)}, bf16[8,128,2048]{2,1,0:T(8,128)(2,1)}, bf16[704,2...) custom-call(bf16[8,128,2048]{2,1,0:T(8,128)(2,1)} %get-tuple-element.61.refs_0_, ...), custom_call_target="tpu_custom_call" | custom-call | bytes 1024 | tf_op jit(solution)/shard_map/feed_forward/pallas_call | solution.py:151
  339.7 0.3 reduce-scatter.6.cloned.1.call-start
  340.0 79.3 %attend_back.1 = (f32[128,2048]{1,0:T(8,128)}, bf16[8,128,2048]{2,1,0:T(8,128)(2,1)}, bf16[1024,512]{1,0:T(8,128)(2,1)}, bf16[1024,1536]{1,0:T(8,128)(2,1)}) custom-call(bf16[8,128,2048]{2,1,0:T(8,128)(2,1)} %get-tuple-element.66.refs_0_, f32[128,2048]{1,0:T(8,128)} %get-tuple-element.65.refs_4_.refs_1_, bf16[128,2048]{1,0:T(8,128)(2,1)} %get-tuple-element.67.refs_2_, ...), custom_call_target="tpu_custom_call" | custom-call | bytes 1024 | tf_op jit(solution)/shard_map/attend_back/pallas_call | solution.py:151
  419.4 2.5 fusion.3
  421.9 1.0 copy.53
  423.0 1.2 copy-done.25
  424.2 5.9 convolution_convert_fusion.2.refs_8_
  430.4 91.7 %inner_grad.1 = (bf16[8,128,1536]{2,1,0:T(8,128)(2,1)}, f32[16,1280]{1,0:T(8,128)}, bf16[8,64,1408]{2,1,0:T(8,128)(2,1)}, bf16[176,2048]{1,0:T(8,128)(2,1)}) custom-call(bf16[8,128,1536]{2,1,0:T(8,128)(2,1)} %bitcast.116, f32[128,1536]{1,0:T(8,128)} %get-tuple-element.72.refs_1_, f32[128,256]{1,0:T(8,128)} %get-tuple-element.107.refs_1_.refs_2_, ...), custom_call_target="tpu_custom_call" | custom-call | bytes 1024 | tf_op jit(solution)/shard_map/inner_grad/pallas_call | solution.py:151
  522.1 3.9 fusion
  526.0 1.8 convolution_convert_fusion.3
  527.9 24.0 %normed_grad.1 = (bf16[8,128,256]{2,1,0:T(8,128)(2,1)}, bf16[4,64,1536]{2,1,0:T(8,128)(2,1)}) custom-call(bf16[8,128,256]{2,1,0:T(8,128)(2,1)} %bitcast.129, bf16[4,64,1536]{2,1,0:T(8,128)(2,1)} %bitcast.127), custom_call_target="tpu_custom_call" | custom-call | bytes 1024 | tf_op jit(solution)/shard_map/normed_grad/pallas_call | solution.py:151
  551.9 1.3 multiply_reduce_fusion
  553.6 0.8 stack.37.refs_0_
  554.3 13.9 %end.1 = (f32[8,128]{1,0:T(8,128)}, bf16[8,32,512]{2,1,0:T(8,128)(2,1)}) custom-call(f32[8,4,8,128]{3,2,1,0:T(8,128)} %stack.37.refs_0_, bf16[8,32,512]{2,1,0:T(8,128)(2,1)} %bitcast.130), custom_call_target="tpu_custom_call" | custom-call | bytes 1024 | tf_op jit(solution)/shard_map/end/pallas_call | solution.py:151
  568.2 1.0 convert_bitcast_fusion.1
  569.2 0.8 copy.61
  570.2 0.3 copy.55
  570.5 0.3 copy.56
  570.9 0.3 copy-done.14
  571.4 0.7 slice.71
  572.1 3.8 unfold.1
  575.8 2.4 convert_element_type.100
  578.4 0.5 slice_bitcast_fusion.1
  578.9 0.5 slice_bitcast_fusion.2
  579.4 0.5 slice_bitcast_fusion
  580.0 0.7 fusion.8
  580.6 1.3 add_bitcast_fusion
  581.9 2.1 convert_element_type.99
  584.0 2.3 copy.67
  (100 shorter events, 1.9 us)
Async XLA Ops:
  7.2 3.5 copy-start.22
  7.2 3.5 copy-start.21
  7.2 6.7 %copy-start.10 = (f32[128,2048]{1,0:T(8,128)S(1)}, f32[128,2048]{1,0:T(8,128)}, u32[]{:S(2)}) copy-start(f32[128,2048]{1,0:T(8,128)} %param.25) | copy-start | bytes 3145732
  7.2 127.3 %all-gather.4.cloned.1.call-start = ((), (), s32[]{:S(2)}) async-start(), calls=%async_computation.3 | async-start | bytes 1310720 | tf_op jit(solution)/shard_map/all_gather | solution.py:1133
  8.7 6.1 %copy-start.15 = (f32[64,1024]{1,0:T(8,128)S(1)}, f32[64,1024]{1,0:T(8,128)}, u32[]{:S(2)}) copy-start(f32[64,1024]{1,0:T(8,128)} %param.19) | copy-start | bytes 786436
  10.3 4.5 copy-start.18
  10.3 4.5 copy-start.19
  10.7 31.3 %copy-start.4 = (f32[128,8,256]{2,0,1:T(8,128)}, f32[128,8,256]{2,0,1:T(8,128)S(1)}, u32[]{:S(2)}) copy-start(f32[128,8,256]{2,0,1:T(8,128)S(1)} %copy.47) | copy-start | bytes 3145732
  14.8 32.1 %copy-start.20 = (s32[1,4]{1,0:T(1,128)S(1)}, s32[1,4]{1,0:T(1,128)}, u32[]{:S(2)}) copy-start(s32[1,4]{1,0:T(1,128)} %param.16) | copy-start | bytes 52
  14.8 32.2 %copy-start.8 = (f32[176,2048]{1,0:T(8,128)S(1)}, f32[176,2048]{1,0:T(8,128)}, u32[]{:S(2)}) copy-start(f32[176,2048]{1,0:T(8,128)} %param.29) | copy-start | bytes 4325380
  42.0 104.8 %all-gather.6.cloned.1.call-start = ((), (), s32[]{:S(2)}) async-start(), calls=%async_computation.4 | async-start | bytes 2621440 | tf_op jit(solution)/shard_map/all_gather | solution.py:1236
  42.8 218.4 %all-gather.8.cloned.1.call-start = ((), (), s32[]{:S(2)}) async-start(), calls=%async_computation.5 | async-start | bytes 7208960 | tf_op jit(solution)/shard_map/all_gather | solution.py:1162
  48.0 8.8 %copy-start.11 = (f32[8,128,256]{2,1,0:T(8,128)S(1)}, f32[8,128,256]{2,1,0:T(8,128)}, u32[]{:S(2)}) copy-start(f32[8,128,256]{2,1,0:T(8,128)} %get-tuple-element.51) | copy-start | bytes 3145732
  52.0 5.0 copy-start.12
  56.0 3.6 copy-start.2
  56.0 3.6 copy-start.3
  59.6 74.0 %copy-start.6 = (f32[1,128,2048]{2,1,0:T(8,128)S(1)}, f32[1,128,2048]{2,1,0:T(8,128)}, u32[]{:S(2)}) copy-start(f32[1,128,2048]{2,1,0:T(8,128)} %param.17) | copy-start | bytes 3145732
  129.6 293.4 %reduce-scatter.4.cloned.1.call-start = ((), (), s32[]{:S(2)}) async-start(), calls=%async_computation.6 | async-start | bytes 7208960 | tf_op jit(solution)/shard_map/reduce_scatter | solution.py:1166
  339.7 214.6 %reduce-scatter.6.cloned.1.call-start = ((), (), s32[]{:S(2)}) async-start(), calls=%async_computation.7 | async-start | bytes 1310720 | tf_op jit(solution)/shard_map/reduce_scatter | solution.py:1143
  340.0 79.3 %copy-start.1 = (bf16[8,128,1536]{2,1,0:T(8,128)(2,1)S(1)}, bf16[8,128,1536]{2,1,0:T(8,128)(2,1)}, u32[]{:S(2)}) copy-start(bf16[8,128,1536]{2,1,0:T(8,128)(2,1)} %get-tuple-element.57) | copy-start | bytes 9437188
  422.9 159.0 %reduce-scatter.8.cloned.1.call-start = ((), (), s32[]{:S(2)}) async-start(), calls=%async_computation.8 | async-start | bytes 2621440 | tf_op jit(solution)/shard_map/reduce_scatter | solution.py:1149
  423.0 1.2 copy-start.25
  424.2 6.0 %copy-start.16 = (f32[16,2048]{1,0:T(8,128)S(1)}, f32[16,2048]{1,0:T(8,128)}, u32[]{:S(2)}) copy-start(f32[16,2048]{1,0:T(8,128)} %get-tuple-element.80) | copy-start | bytes 393220
  522.1 3.9 copy-start.13
  522.1 3.9 copy-start.24
  526.0 25.9 %copy-start.5 = (f32[128,8,256]{2,0,1:T(8,128)S(1)}, f32[128,8,256]{2,0,1:T(8,128)}, u32[]{:S(2)}) copy-start(f32[128,8,256]{2,0,1:T(8,128)} %copy-done.4) | copy-start | bytes 3145732
  526.0 27.3 %copy-start.17 = (f32[16,1280]{1,0:T(8,128)S(1)}, f32[16,1280]{1,0:T(8,128)}, u32[]{:S(2)}) copy-start(f32[16,1280]{1,0:T(8,128)} %get-tuple-element.79) | copy-start | bytes 245764
  551.9 18.2 %copy-start.7 = (bf16[8,128,256]{2,1,0:T(8,128)(2,1)S(1)}, bf16[8,128,256]{2,1,0:T(8,128)(2,1)}, u32[]{:S(2)}) copy-start(bf16[8,128,256]{2,1,0:T(8,128)(2,1)} %get-tuple-element.78) | copy-start | bytes 1572868
  570.1 1.1 copy-start.14
  570.9 7.4 %copy-start = (f32[1,128,2048]{2,1,0:T(8,128)S(1)}, f32[1,128,2048]{2,1,0:T(8,128)}, u32[]{:S(2)}) copy-start(f32[1,128,2048]{2,1,0:T(8,128)} %param.15) | copy-start | bytes 3145732
  571.3 7.1 %copy-start.23 = (f32[8,128]{1,0:T(8,128)S(1)}, f32[8,128]{1,0:T(8,128)}, u32[]{:S(2)}) copy-start(f32[8,128]{1,0:T(8,128)} %get-tuple-element.81) | copy-start | bytes 12292
  571.3 9.3 %copy-start.9 = (f32[128,2048]{1,0:T(8,128)S(1)}, f32[128,2048]{1,0:T(8,128)}, u32[]{:S(2)}) copy-start(f32[128,2048]{1,0:T(8,128)} %get-tuple-element.70) | copy-start | bytes 3145732
Sparse Core Ops, SparseCore 0:
  42.1 36.1 all-gather.3
  79.9 54.5 all-gather.5
  136.3 98.1 all-gather.7
  339.8 80.7 reduce-scatter.3
  423.4 39.8 reduce-scatter.5
  465.5 53.0 reduce-scatter.7

commit v4 on v3

--- a/solution.py
+++ b/solution.py
@@ -121,7 +121,7 @@
         self.masks, self.run = masks, run
 
 
-def launch(name, collective_id, tasks, needs=(), passes=()):
+def launch(name, collective_id, tasks, needs=(), passes=(), turns=()):
     masks = sorted({mask for task in tasks for mask in task.masks})
     n_in = sum(len(task.inputs) for task in tasks)
     n_out = sum(len(task.outputs) for task in tasks)
@@ -141,6 +141,8 @@
             a, b, c = len(task.inputs), len(task.outputs), len(task.scratch)
             running.append(task.run(ins[:a], outs[:b], scratch[:c]))
             ins, outs, scratch = ins[a:], outs[b:], scratch[c:]
+        for turn in turns:
+            next(running[turn], None)
         while running:
             for step in list(running):
                 if next(step, "done") == "done":
@@ -625,7 +627,8 @@
 
 
 def gather_chips(low):
-    rows, cols = low.shape
+    rows = low.shape[0]
+    middle = rows // 2 // STEP * STEP if len(low.shape) == 2 else rows // 2
     masks = axis_masks("chip")
     square = len(masks) == 3
 
@@ -637,7 +640,6 @@
             return all_ref.at[device(mask)[0] // 2]
 
         def half(mask, which):
-            middle = rows // 2 // STEP * STEP
             part = pl.ds(middle, rows - middle) if which else pl.ds(0, middle)
             return all_ref.at[device(mask)[0] // 2, part]
 
@@ -662,7 +664,7 @@
 
     return Task(
         [(low, ANY)],
-        [(jax.ShapeDtypeStruct((len(masks) + 1, rows, cols), low.dtype), ANY)],
+        [(jax.ShapeDtypeStruct((len(masks) + 1,) + low.shape, low.dtype), ANY)],
         [pltpu.SemaphoreType.DMA((1,)), pltpu.SemaphoreType.DMA((max(4, len(masks)), 2))],
         masks,
         run,
@@ -789,13 +791,15 @@
     return shifted / jnp.sum(shifted, axis=-1, keepdims=True)
 
 
-def attend(gathered, qb_cols, cosine, sine_tab, seg_col, seg_rows):
+def attend(gathered, qb_cols, o_rows, cosine, sine_tab, seg_col, seg_rows, parts):
     tokens, inner = gathered.shape
     rank, width = qb_cols.shape
+    rows, cols = tokens // parts, o_rows.shape[1]
+    per = QUERIES // rows
 
     def run(ins, outs, scratch):
-        in_ref, qb_ref, cos_ref, sin_ref, seg_ref, segs_ref = ins
-        q_ref, out_ref = outs
+        in_ref, qb_ref, o_ref, cos_ref, sin_ref, seg_ref, segs_ref = ins
+        part_ref, q_ref, out_ref = outs
 
         def block(i, carry):
             at = pl.ds(pl.multiple_of(i * QUERIES, QUERIES), QUERIES)
@@ -810,6 +814,8 @@
                 q_ref[at, lanes] = rotated
                 probs = probabilities(rotated, keys, i, start, seg_ref[at, :], segs_ref[i])
                 out_ref[at, lanes] = dot(probs.astype(jnp.bfloat16), values).astype(jnp.bfloat16)
+            part = dot(out_ref[at, :], o_ref[...]).astype(jnp.bfloat16)
+            part_ref[pl.ds(i * per, per)] = part.reshape(per, rows, cols)
             return carry
 
         lax.fori_loop(0, tokens // QUERIES, block, 0)
@@ -817,8 +823,12 @@
 
     shape = jax.ShapeDtypeStruct((tokens, width), jnp.bfloat16)
     return Task(
-        [(a, VMEM) for a in (gathered, qb_cols, cosine, sine_tab, seg_col, seg_rows)],
-        [(shape, VMEM), (shape, VMEM)],
+        [(a, VMEM) for a in (gathered, qb_cols, o_rows, cosine, sine_tab, seg_col, seg_rows)],
+        [
+            (jax.ShapeDtypeStruct((parts, rows, cols), jnp.bfloat16), VMEM),
+            (shape, VMEM),
+            (shape, VMEM),
+        ],
         [],
         [],
         run,
@@ -1250,7 +1260,7 @@
 
     chips = parts // 2
     both_cols = fold(list(lax.optimization_barrier((w_gate, w_up))), chips, groups)
-    (gathered, inner_own), (both_cols,), (down_rows,) = launch(
+    (gathered, inner_own), (down_rows,) = launch(
         "latent",
         1,
         [
@@ -1263,9 +1273,9 @@
                 inner,
                 0,
             ),
-            swap(both_cols, "line"),
             gather_chips(w_down.astype(jnp.bfloat16)),
         ],
+        turns=[0, 0, 1, 0, 0, 0, 0, 1, 0, 0, 0],
     )
     gathered = gathered.reshape(group_tokens, inner)
     seg_col = segment[:, None]
@@ -1278,39 +1288,37 @@
             ]
         ]
     )[:, None, :]
-    ((q_rot, attended_low),) = launch(
-        "attend", 2, [attend(gathered, qb_cols, cos_all, sin_all, seg_col, seg_rows)]
-    )
-    down_rows = down_rows.reshape(-1, D)
-    partial = dot(attended_low, o_rows).astype(jnp.bfloat16).reshape(parts, tok_rows, D)
-
     def mixed_function(total, row, vec):
         mixed = row[0] + total
         return rms_scale(mixed, vec[0]), [mixed], None
 
-    (two_all, mixed_rows), (grad_all,) = launch(
+    down_rows = down_rows.reshape(-1, D)
+    piece, wide = both_cols.shape[1:]
+    attend_task = attend(
+        gathered, qb_cols, o_rows, cos_all, sin_all, seg_col, seg_rows, parts
+    )
+    mixed_task = exchange(
+        jax.ShapeDtypeStruct((parts, tok_rows, D), jnp.bfloat16),
+        [flat_rows],
+        [gain_two],
+        mixed_function,
+        [D],
+        D,
+        0,
+        spread_axis="dp",
+    )
+    (_, q_rot, attended_low, two_all, mixed_rows), (grad_all,), (_, both_cols) = launch(
         "mixed",
         3,
         [
-            exchange(
-                partial,
-                [flat_rows],
-                [gain_two],
-                mixed_function,
-                [D],
-                D,
-                0,
-                spread_axis="dp",
-            ),
+            chain(attend_task, mixed_task, {0: 0}),
             gather(out_grad.astype(jnp.bfloat16), "dp"),
-        ],
-    )
-    wide = both_cols.shape[2]
-    piece = both_cols.shape[1]
-    both_cols = chip_gather(both_cols.reshape(-1, wide), parts)
+            chain(swap(both_cols, "line"), gather_chips(both_cols), {0: 0}),
+        ],
+        turns=[2, 0, 0, 0, 0, 2, 1, 0, 1, 0, 2, 1, 0],
+    )
     both_cols = both_cols.reshape(chips, groups, 2, piece, wide)
     both_cols = jnp.transpose(both_cols, (0, 2, 1, 3, 4)).reshape(D, wide)
-
     ((mixed_grad, mixed_low, gain_two_grad, out_part, down_low, both_low),) = launch(
         "feed_forward",
         9,
@@ -1344,6 +1352,7 @@
             exchange(out_part, [mixed_rows], [], out_function, [D], 0, 0, sum_axis="dp"),
             chain(mixed_task, back_task, {2: 0}),
         ],
+        turns=[1, 0, 0, 1, 1, 1, 1, 1],
     )
     mixed_all = tie(mixed_all, [both_shard]).reshape(group_tokens, D)
     o_shard, o_low = scatter_rows(
@@ -1362,7 +1371,7 @@
         low = jnp.concatenate([latent_grad, key_grad, total[:, rank + E :]], axis=1)
         return low, [], jnp.concatenate([latent_gain, key_gain], axis=1)
 
-    (in_grad, inner_gain_grad), (both_shard,), (down_shard,) = launch(
+    (in_grad, inner_gain_grad), (both_shard,) = launch(
         "inner_grad",
         5,
         [
@@ -1376,8 +1385,8 @@
                 rank + E,
             ),
             swap(both_shard, "line"),
-            paused(chip_sum(down_low.reshape(chips, -1, D)), 2),
-        ],
+        ],
+        turns=[1, 0, 0, 0, 0, 0, 0, 0, 0, 0],
         needs=[o_low, qb_low],
     )
     in_grad = in_grad.reshape(group_tokens, inner)
@@ -1386,10 +1395,15 @@
     normed_part = jnp.einsum("tr,dr->td", in_grad, in_rows, preferred_element_type=jnp.float32)
     normed_part = normed_part.astype(jnp.bfloat16).reshape(parts, tok_rows, width)
 
-    (normed_grad,), (in_shard,) = launch(
+    (normed_grad,), (in_shard,), (down_shard,) = launch(
         "normed_grad",
         6,
-        [swap(normed_part, "seq"), swap(in_low, "dp")],
+        [
+            swap(normed_part, "seq"),
+            swap(in_low, "dp"),
+            chip_sum(down_low.reshape(chips, -1, D)),
+        ],
+        turns=[0, 1, 2, 2],
     )
     in_shard = jnp.sum(in_shard.astype(jnp.float32), axis=0)
     normed_grad = jnp.transpose(normed_grad.astype(jnp.float32), (1, 0, 2)).reshape(tok_rows, D)

time: 599 us -> 556 us (0.928)
  Pallas kernels: 503 us -> 453 us
  waiting for transfers between devices: 0.82 us -> 16 us
  matrix products: 23 us -> 16.8 us
    pallas_call x9 -> x8, Pallas kernels: 495 us -> 445 us  [launch(): pl.pallas_call(body, name=name, out_shape=[shape for shape, _ in outputs]...]
    reduce_scatter x1, waiting for transfers between devices: 0.02 us -> 15.3 us  [chip_scatter(): lax.psum_scatter(rows, 'seq', scatter_dimension=0, tiled=True, axis_index...]
    dot_general x2 -> x1, matrix products: 8.88 us -> 2.63 us  [dot(): return jnp.dot(left, right, preferred_element_type=jnp.float32)]
  transfers between devices with their start and end apart: 6 -> 5, of which waited for: 0 -> 1; matrix products, arithmetic and copies ran while one was open for 9% -> 9% of each run, Pallas kernels for 68% -> 43%
where the time goes in v4:
time: 556 us; the launch traced here: 552 us
  Pallas kernels  453 us (81%)
  local copies, waits for them, and re-layouts  30.4 us (5%)
  other arithmetic  21.1 us (4%)
  matrix products  16.8 us (3%)
  waiting for transfers between devices  16 us (3%)
  between operations  14.7 us (3%)
    pallas_call x8, Pallas kernels, launch(): pl.pallas_call(body, name=name, out_shape=[shape for shape, _ in outputs]...  445 us
    reduce_scatter x1, waiting for transfers between devices, chip_scatter(): lax.psum_scatter(rows, 'seq', scatter_dimension=0, tiled=True, axis_index...  15.3 us
  transfers between devices with their start and end apart: 5, of which 1 were waited for; matrix products, arithmetic and copies ran while one was open for 9% of the time, Pallas kernels for 43%

profile of v4, /device:TPU:0, one launch (start us, length us, event | category | flops | bytes accessed | tf_op | source)
XLA Modules:
  0.0 552.4 jit_solution(4867585790653732114)
XLA Ops:
  7.3 1.5 multiply_reduce_fusion.2
  8.7 1.6 copy.47
  10.4 0.3 copy.48
  10.7 0.8 pad_bitcast_fusion.2
  11.5 0.6 reduce_precision.3.refs_0_
  12.1 1.1 convert_element_type.78
  13.2 0.7 copy.64
  13.9 0.9 convert_element_type.79.refs_4_
  14.9 1.1 multiply_bitcast_fusion.refs_1_
  16.0 0.7 pad_maximum_fusion.1.refs_2_
  16.7 25.3 %start.1 = (f32[8,4,8,128]{3,2,1,0:T(8,128)}, f32[4,8,128]{2,1,0:T(8,128)}, f32[8,128,256]{2,1,0:T(8,128)}, bf16[4,64,1536]{2,1,0:T(8,128)(2,1)}, bf16[8,32,512]...) custom-call(f32[8,128]{1,0:T(8,128)} %reduce_precision.3.refs_0_, ...), custom_call_target="tpu_custom_call", output_to_operand_aliasing={{5}: (4, {})} | custom-call | bytes 1024 | tf_op jit(solution)/shard_map/start/pallas_call | solution.py:153
  42.1 0.7 all-gather.5.cloned.1.call-update
  42.8 0.7 slice_reduce_fusion.6
  43.7 1.0 slice_reduce_fusion.5
  44.6 0.7 reshape_squeeze.11.refs_3_.refs_4_
  45.3 1.0 slice_reduce_fusion.4
  46.3 0.6 reshape_squeeze.12.refs_4_.refs_5_
  47.1 1.0 convert_element_type.84.refs_5_
  48.0 1.1 slice_reduce_fusion.2
  49.1 0.7 reshape_squeeze.13.refs_8_.refs_6_
  50.0 0.6 broadcast_in_dim.51.refs_6_.refs_10_
  50.6 1.0 copy.51.refs_5_.refs_9_
  51.6 3.9 fold.1.refs_10_
  55.5 0.2 broadcast_multiply_fusion
  55.7 4.2 fusion.6
  59.9 0.8 constant_dynamic-slice_fusion
  60.8 2.6 convolution_convert_fusion
  63.5 61.6 %latent.1 = (bf16[8,128,1536]{2,1,0:T(8,128)(2,1)}, f32[128,1536]{1,0:T(8,128)}, bf16[4,176,2048]{2,1,0:T(8,128)(2,1)}) custom-call(bf16[8,128,1536]{2,1,0:T(8,128)(2,1)} %bitcast.93, f32[128,256]{1,0:T(8,128)} %get-tuple-element.107.refs_1_.refs_2_, f32[128,256]{1,0:T(8,128)} %get-tuple-element.106.refs_2_.refs_3_, ...), custom_call_target="tpu_custom_call" | custom-call | bytes 1024 | tf_op jit(solution)/shard_map/latent/pallas_call | solution.py:153
  125.1 0.9 bitcast_convert_fusion.refs_9_
  126.0 2.3 copy.50
  128.3 115.0 %mixed.1 = (bf16[8,128,2048]{2,1,0:T(8,128)(2,1)}, bf16[1024,512]{1,0:T(8,128)(2,1)}, bf16[1024,512]{1,0:T(8,128)(2,1)}, bf16[8,128,2048]{2,1,0:T(8,128)(2,1)}, ...) custom-call(bf16[1024,1536]{1,0:T(8,128)(2,1)} %bitcast.95, ...), custom_call_target="tpu_custom_call" | custom-call | bytes 1024 | tf_op jit(solution)/shard_map/mixed/pallas_call | solution.py:153
  243.3 5.8 %copy.52 = bf16[4,4,2,64,1408]{4,3,1,2,0:T(8,128)(2,1)} copy(bf16[4,4,2,64,1408]{4,3,2,1,0:T(8,128)(2,1)} %bitcast.105) | data formatting | bytes 11534336 | tf_op jit(solution)/shard_map/reshape | solution.py:1320
  249.0 72.6 %feed_forward.1 = (f32[128,2048]{1,0:T(8,128)}, bf16[128,2048]{1,0:T(8,128)(2,1)}, f32[16,2048]{1,0:T(8,128)}, bf16[8,128,2048]{2,1,0:T(8,128)(2,1)}, bf16[704,2...) custom-call(bf16[8,128,2048]{2,1,0:T(8,128)(2,1)} %get-tuple-element.60.refs_0_, ...), custom_call_target="tpu_custom_call" | custom-call | bytes 1024 | tf_op jit(solution)/shard_map/feed_forward/pallas_call | solution.py:153
  321.7 0.3 reduce-scatter.6.cloned.1.call-start
  322.0 62.2 %attend_back.1 = (f32[128,2048]{1,0:T(8,128)}, bf16[8,128,2048]{2,1,0:T(8,128)(2,1)}, bf16[1024,512]{1,0:T(8,128)(2,1)}, bf16[1024,1536]{1,0:T(8,128)(2,1)}) custom-call(bf16[8,128,2048]{2,1,0:T(8,128)(2,1)} %get-tuple-element.65.refs_0_, f32[128,2048]{1,0:T(8,128)} %get-tuple-element.64.refs_4_.refs_1_, bf16[128,2048]{1,0:T(8,128)(2,1)} %get-tuple-element.66.refs_2_, ...), custom_call_target="tpu_custom_call" | custom-call | bytes 1024 | tf_op jit(solution)/shard_map/attend_back/pallas_call | solution.py:153
  384.2 2.5 fusion.3
  386.7 1.0 copy.54
  387.8 15.3 %reduce-scatter.4.cloned.1.call-done = bf16[512,1408]{1,0:T(8,128)(2,1)} async-done(((bf16[2048,1408]{1,0:T(8,128)(2,1)}), bf16[512,1408]{1,0:T(8,128)(2,1)}) %reduce-scatter.4.cloned.1.call-update) | async-done | bytes 1441808 | tf_op jit(solution)/shard_map/reduce_scatter | solution.py:1176
  403.1 1.2 copy-done.25
  404.3 5.9 %convolution_convert_fusion.1.refs_7_ = bf16[512,2048]{1,0:T(8,128)(2,1)} fusion(bf16[1024,512]{1,0:T(8,128)(2,1)S(1)} %copy-done.25, bf16[1024,2048]{1,0:T(8,128)(2,1)} %bitcast.106), kind=kOutput, calls=%fused_computation.1 | convolution fusion | flops 2148532224 | bytes 7340032 | tf_op jit(solution)/shard_map/tf,td->fd/dot_general | solution.py:1359
  410.5 46.2 %inner_grad.1 = (bf16[8,128,1536]{2,1,0:T(8,128)(2,1)}, f32[16,1280]{1,0:T(8,128)}, bf16[8,64,1408]{2,1,0:T(8,128)(2,1)}) custom-call(bf16[8,128,1536]{2,1,0:T(8,128)(2,1)} %bitcast.111, f32[128,1536]{1,0:T(8,128)} %get-tuple-element.71.refs_1_, f32[128,256]{1,0:T(8,128)} %get-tuple-element.107.refs_1_.refs_2_, ...), custom_call_target="tpu_custom_call" | custom-call | bytes 1024 | tf_op jit(solution)/shard_map/inner_grad/pallas_call | solution.py:153
  456.7 3.9 fusion
  460.6 1.8 convolution_convert_fusion.2
  462.4 41.3 %normed_grad.1 = (bf16[8,128,256]{2,1,0:T(8,128)(2,1)}, bf16[4,64,1536]{2,1,0:T(8,128)(2,1)}, bf16[176,2048]{1,0:T(8,128)(2,1)}) custom-call(bf16[8,128,256]{2,1,0:T(8,128)(2,1)} %bitcast.123, bf16[4,64,1536]{2,1,0:T(8,128)(2,1)} %bitcast.121, bf16[4,176,2048]{2,1,0:T(8,128)(2,1)} %bitcast.112), custom_call_target="tpu_custom_call" | custom-call | bytes 1024 | tf_op jit(solution)/shard_map/normed_grad/pallas_call | solution.py:153
  503.8 1.3 multiply_reduce_fusion
  505.4 0.8 stack.37.refs_0_
  506.2 21.0 %end.1 = (f32[8,128]{1,0:T(8,128)}, bf16[8,32,512]{2,1,0:T(8,128)(2,1)}) custom-call(f32[8,4,8,128]{3,2,1,0:T(8,128)} %stack.37.refs_0_, bf16[8,32,512]{2,1,0:T(8,128)(2,1)} %bitcast.124), custom_call_target="tpu_custom_call" | custom-call | bytes 1024 | tf_op jit(solution)/shard_map/end/pallas_call | solution.py:153
  527.2 1.0 convert_bitcast_fusion.1
  528.2 0.8 copy.62
  529.2 0.3 copy.56
  529.5 0.3 copy.57
  529.9 0.3 copy-done.14
  530.2 1.3 convert_element_type.96
  531.5 1.4 convert_reduce_fusion
  532.8 0.7 slice.71
  533.5 3.8 unfold.1
  537.3 0.2 multiply_reduce_fusion.1
  537.5 0.5 slice_bitcast_fusion.1
  538.0 0.5 slice_bitcast_fusion.2
  538.6 0.5 slice_bitcast_fusion
  539.1 0.7 fusion.8
  539.7 1.3 add_bitcast_fusion
  541.0 2.1 convert_element_type.95
  543.1 2.3 copy.68
  (95 shorter events, 1.5 us)
Async XLA Ops:
  7.2 3.5 copy-start.22
  7.2 3.5 copy-start.21
  7.2 6.7 %copy-start.10 = (f32[128,2048]{1,0:T(8,128)S(1)}, f32[128,2048]{1,0:T(8,128)}, u32[]{:S(2)}) copy-start(f32[128,2048]{1,0:T(8,128)} %param.25) | copy-start | bytes 3145732
  7.2 118.8 %all-gather.3.cloned.1.call-start = ((), (), s32[]{:S(2)}) async-start(), calls=%async_computation.3 | async-start | bytes 1310720 | tf_op jit(solution)/shard_map/all_gather | solution.py:1143
  8.7 6.1 %copy-start.15 = (f32[64,1024]{1,0:T(8,128)S(1)}, f32[64,1024]{1,0:T(8,128)}, u32[]{:S(2)}) copy-start(f32[64,1024]{1,0:T(8,128)} %param.19) | copy-start | bytes 786436
  10.3 4.5 copy-start.18
  10.3 4.5 copy-start.19
  10.7 31.3 %copy-start.4 = (f32[128,8,256]{2,0,1:T(8,128)}, f32[128,8,256]{2,0,1:T(8,128)S(1)}, u32[]{:S(2)}) copy-start(f32[128,8,256]{2,0,1:T(8,128)S(1)} %copy.48) | copy-start | bytes 3145732
  14.8 32.1 %copy-start.20 = (s32[1,4]{1,0:T(1,128)S(1)}, s32[1,4]{1,0:T(1,128)}, u32[]{:S(2)}) copy-start(s32[1,4]{1,0:T(1,128)} %param.16) | copy-start | bytes 52
  14.8 32.3 %copy-start.8 = (f32[176,2048]{1,0:T(8,128)S(1)}, f32[176,2048]{1,0:T(8,128)}, u32[]{:S(2)}) copy-start(f32[176,2048]{1,0:T(8,128)} %param.29) | copy-start | bytes 4325380
  42.0 86.2 %all-gather.5.cloned.1.call-start = ((), (), s32[]{:S(2)}) async-start(), calls=%async_computation.4 | async-start | bytes 2621440 | tf_op jit(solution)/shard_map/all_gather | solution.py:1246
  42.8 360.3 %reduce-scatter.4.cloned.1.call-start = ((), (), s32[]{:S(2)}) async-start(), calls=%async_computation.5 | async-start | bytes 7208960 | tf_op jit(solution)/shard_map/reduce_scatter | solution.py:1176
  51.6 9.1 %copy-start.11 = (f32[8,128,256]{2,1,0:T(8,128)S(1)}, f32[8,128,256]{2,1,0:T(8,128)}, u32[]{:S(2)}) copy-start(f32[8,128,256]{2,1,0:T(8,128)} %get-tuple-element.51) | copy-start | bytes 3145732
  55.5 5.3 copy-start.12
  59.9 3.6 copy-start.2
  59.9 3.6 copy-start.3
  63.5 61.6 %copy-start.6 = (f32[1,128,2048]{2,1,0:T(8,128)S(1)}, f32[1,128,2048]{2,1,0:T(8,128)}, u32[]{:S(2)}) copy-start(f32[1,128,2048]{2,1,0:T(8,128)} %param.17) | copy-start | bytes 3145732
  321.7 184.5 %reduce-scatter.6.cloned.1.call-start = ((), (), s32[]{:S(2)}) async-start(), calls=%async_computation.6 | async-start | bytes 1310720 | tf_op jit(solution)/shard_map/reduce_scatter | solution.py:1153
  322.0 62.2 %copy-start.1 = (bf16[8,128,1536]{2,1,0:T(8,128)(2,1)S(1)}, bf16[8,128,1536]{2,1,0:T(8,128)(2,1)}, u32[]{:S(2)}) copy-start(bf16[8,128,1536]{2,1,0:T(8,128)(2,1)} %get-tuple-element.55) | copy-start | bytes 9437188
  387.8 153.3 %reduce-scatter.8.cloned.1.call-start = ((), (), s32[]{:S(2)}) async-start(), calls=%async_computation.7 | async-start | bytes 2621440 | tf_op jit(solution)/shard_map/reduce_scatter | solution.py:1159
  403.1 1.2 copy-start.25
  404.3 6.0 %copy-start.16 = (f32[16,2048]{1,0:T(8,128)S(1)}, f32[16,2048]{1,0:T(8,128)}, u32[]{:S(2)}) copy-start(f32[16,2048]{1,0:T(8,128)} %get-tuple-element.80) | copy-start | bytes 393220
  456.7 3.9 copy-start.13
  456.7 3.9 copy-start.24
  462.4 41.3 %copy-start.5 = (f32[128,8,256]{2,0,1:T(8,128)S(1)}, f32[128,8,256]{2,0,1:T(8,128)}, u32[]{:S(2)}) copy-start(f32[128,8,256]{2,0,1:T(8,128)} %copy-done.4) | copy-start | bytes 3145732
  462.4 42.7 %copy-start.17 = (f32[16,1280]{1,0:T(8,128)S(1)}, f32[16,1280]{1,0:T(8,128)}, u32[]{:S(2)}) copy-start(f32[16,1280]{1,0:T(8,128)} %get-tuple-element.79) | copy-start | bytes 245764
  503.8 25.3 %copy-start.7 = (bf16[8,128,256]{2,1,0:T(8,128)(2,1)S(1)}, bf16[8,128,256]{2,1,0:T(8,128)(2,1)}, u32[]{:S(2)}) copy-start(bf16[8,128,256]{2,1,0:T(8,128)(2,1)} %get-tuple-element.78) | copy-start | bytes 1572868
  529.1 1.1 copy-start.14
  529.9 7.5 %copy-start = (f32[1,128,2048]{2,1,0:T(8,128)S(1)}, f32[1,128,2048]{2,1,0:T(8,128)}, u32[]{:S(2)}) copy-start(f32[1,128,2048]{2,1,0:T(8,128)} %param.15) | copy-start | bytes 3145732
  531.5 6.1 %copy-start.23 = (f32[8,128]{1,0:T(8,128)S(1)}, f32[8,128]{1,0:T(8,128)}, u32[]{:S(2)}) copy-start(f32[8,128]{1,0:T(8,128)} %get-tuple-element.81) | copy-start | bytes 12292
  531.5 8.3 %copy-start.9 = (f32[128,2048]{1,0:T(8,128)S(1)}, f32[128,2048]{1,0:T(8,128)}, u32[]{:S(2)}) copy-start(f32[128,2048]{1,0:T(8,128)} %get-tuple-element.69) | copy-start | bytes 3145732
Sparse Core Ops, SparseCore 0:
  42.2 27.1 all-gather.2
  70.9 45.3 all-gather.4
  321.8 81.2 reduce-scatter.3
  405.8 41.7 reduce-scatter.5
  449.9 64.3 reduce-scatter.7

commit v5 on v4

--- a/solution.py
+++ b/solution.py
@@ -511,7 +511,7 @@
         return [(m, 0) for m in range(1, parts)], lambda s, d: s
     if kind == "dp":
         return [(0, m) for m in range(1, groups)], lambda s, d: d
-    return [(m % 2, m // 2) for m in range(1, 2 * groups)], lambda s, d: d * 2 + s % 2
+    return [(m % 2, m // 2) for m in range(1, 2 * groups)], lambda s, d: s % 2 * groups + d
 
 
 def swap(array, kind, repeat=False):
@@ -717,7 +717,7 @@
                 for tile in range(pl.cdiv(width, 128)):
                     value = lanes_of(sources, segments, tile, rows).astype(jnp.bfloat16)
                     stop = min(width, tile * 128 + 128)
-                    out_ref[group * 2 + core, :, tile * 128 : stop] = value[:, : stop - tile * 128]
+                    out_ref[core * groups + group, :, tile * 128 : stop] = value[:, : stop - tile * 128]
 
     return pl.pallas_call(
         body,
@@ -740,7 +740,7 @@
         for which, out_ref in enumerate([first_ref, second_ref]):
             segments = [
                 (
-                    group * 2 + core,
+                    core * groups + group,
                     (which * chips + chip) * units,
                     ((chip * 2 + core) * groups + group) * units,
                     units,
@@ -980,7 +980,7 @@
             value = tn(x, pair_grad[...].reshape(line * rows, 2 * units))
             stage[slot] = value.astype(jnp.bfloat16).reshape(groups, piece, 2 * units)
             for group in range(groups):
-                place = ((index // 2) * groups + group) * 2 + index % 2
+                place = index * groups + group
                 moves.append(
                     keep(stage.at[slot, group], both_out.at[place], stage_sem.at[slot, group])
                 )
@@ -1154,11 +1154,6 @@
     return own.reshape(parts, piece, cols), low
 
 
-def scatter_rows(grad):
-    low = grad.astype(jnp.bfloat16)
-    return lax.psum_scatter(low, "dp", scatter_dimension=0, tiled=True), low
-
-
 def unfold(pieces):
     parts, rows, cols = pieces.shape
     return jnp.transpose(pieces, (1, 0, 2)).reshape(rows, parts * cols).astype(jnp.float32)
@@ -1317,8 +1312,7 @@
         ],
         turns=[2, 0, 0, 0, 0, 2, 1, 0, 1, 0, 2, 1, 0],
     )
-    both_cols = both_cols.reshape(chips, groups, 2, piece, wide)
-    both_cols = jnp.transpose(both_cols, (0, 2, 1, 3, 4)).reshape(D, wide)
+    both_cols = both_cols.reshape(D, wide)
     ((mixed_grad, mixed_low, gain_two_grad, out_part, down_low, both_low),) = launch(
         "feed_forward",
         9,
@@ -1354,10 +1348,14 @@
         ],
         turns=[1, 0, 0, 1, 1, 1, 1, 1],
     )
-    mixed_all = tie(mixed_all, [both_shard]).reshape(group_tokens, D)
-    o_shard, o_low = scatter_rows(
-        jnp.einsum("tf,td->fd", attended_low, mixed_all, preferred_element_type=jnp.float32)
-    )
+    o_low = jnp.einsum(
+        "tf,td->fd",
+        attended_low,
+        mixed_all.reshape(group_tokens, D),
+        preferred_element_type=jnp.float32,
+    ).astype(jnp.bfloat16)
+    o_low = tie(o_low, [both_shard])
+    o_shard = lax.psum_scatter(o_low, "dp", scatter_dimension=0, tiled=True)
     qb_shard, qb_low = scatter_columns(
         jnp.einsum("tr,tf->rf", gathered[:, :rank], query_grad, preferred_element_type=jnp.float32),
         parts,

time: 556 us -> 548 us (0.986)
  local copies, waits for them, and re-layouts: 30.4 us -> 23.7 us
  waiting for transfers between devices: 16 us -> 9.67 us
    reduce_scatter x1, waiting for transfers between devices: 15.3 us -> 8.9 us  [chip_scatter(): lax.psum_scatter(rows, 'seq', scatter_dimension=0, tiled=True, axis_index...]
    reshape x1 -> x0, local copies, waits for them, and re-layouts: 5.76 us -> none  [local(): both_cols = both_cols.reshape(chips, groups, 2, piece, wide)]
  transfers between devices with their start and end apart: 5 -> 5, of which waited for: 1 -> 1; matrix products, arithmetic and copies ran while one was open for 9% -> 9% of each run, Pallas kernels for 43% -> 44%
where the time goes in v5:
time: 548 us; the launch traced here: 544 us
  Pallas kernels  453 us (83%)
  other arithmetic  25.1 us (5%)
  local copies, waits for them, and re-layouts  23.7 us (4%)
  matrix products  16.8 us (3%)
  between operations  14.8 us (3%)
  waiting for transfers between devices  9.67 us (2%)
    pallas_call x8, Pallas kernels, launch(): pl.pallas_call(body, name=name, out_shape=[shape for shape, _ in outputs]...  446 us
  transfers between devices with their start and end apart: 5, of which 1 were waited for; matrix products, arithmetic and copies ran while one was open for 9% of the time, Pallas kernels for 44%

profile of v5, /device:TPU:0, one launch (start us, length us, event | category | flops | bytes accessed | tf_op | source)
XLA Modules:
  0.0 543.9 jit_solution(7780657557932769951)
XLA Ops:
  7.3 1.5 multiply_reduce_fusion.2
  8.7 1.5 copy.45
  10.3 0.3 copy.46
  10.8 0.7 reduce_precision.3.refs_0_
  11.5 1.1 convert_element_type.78
  12.6 0.7 copy.61
  13.3 0.9 convert_element_type.79.refs_4_
  14.1 1.1 convert.12
  15.2 0.8 convert.13
  16.1 0.8 convert.14
  16.9 1.1 multiply_bitcast_fusion.refs_1_
  18.0 0.7 pad_maximum_fusion.1.refs_2_
  18.7 25.3 %start.1 = (f32[8,4,8,128]{3,2,1,0:T(8,128)}, f32[4,8,128]{2,1,0:T(8,128)}, f32[8,128,256]{2,1,0:T(8,128)}, bf16[4,64,1536]{2,1,0:T(8,128)(2,1)}, bf16[8,32,512]...) custom-call(f32[8,128]{1,0:T(8,128)} %reduce_precision.3.refs_0_, ...), custom_call_target="tpu_custom_call", output_to_operand_aliasing={{5}: (4, {})} | custom-call | bytes 1024 | tf_op jit(solution)/shard_map/start/pallas_call | solution.py:153
  44.1 0.7 all-gather.5.cloned.1.call-update
  44.9 0.7 slice_reduce_fusion.6
  45.7 1.0 slice_reduce_fusion.5
  46.7 0.7 reshape_squeeze.11.refs_3_.refs_4_
  47.3 1.0 slice_reduce_fusion.4
  48.3 0.7 reshape_squeeze.12.refs_4_.refs_5_
  49.2 1.0 convert_element_type.84.refs_5_
  50.1 1.1 slice_reduce_fusion.2
  51.2 0.7 reshape_squeeze.13.refs_8_.refs_6_
  52.1 0.6 broadcast_in_dim.51.refs_6_.refs_10_
  52.7 1.0 copy.49.refs_5_.refs_9_
  53.7 3.9 fold.1.refs_10_
  57.6 0.2 broadcast_multiply_fusion
  57.8 4.2 fusion.6
  62.0 0.8 constant_dynamic-slice_fusion
  63.0 2.6 convolution_convert_fusion
  65.6 61.6 %latent.1 = (bf16[8,128,1536]{2,1,0:T(8,128)(2,1)}, f32[128,1536]{1,0:T(8,128)}, bf16[4,176,2048]{2,1,0:T(8,128)(2,1)}) custom-call(bf16[8,128,1536]{2,1,0:T(8,128)(2,1)} %bitcast.90, f32[128,256]{1,0:T(8,128)} %get-tuple-element.107.refs_1_.refs_2_, f32[128,256]{1,0:T(8,128)} %get-tuple-element.106.refs_2_.refs_3_, ...), custom_call_target="tpu_custom_call" | custom-call | bytes 1024 | tf_op jit(solution)/shard_map/latent/pallas_call | solution.py:153
  127.3 0.9 bitcast_convert_fusion.refs_9_
  128.1 2.3 copy.48
  130.4 114.9 %mixed.1 = (bf16[8,128,2048]{2,1,0:T(8,128)(2,1)}, bf16[1024,512]{1,0:T(8,128)(2,1)}, bf16[1024,512]{1,0:T(8,128)(2,1)}, bf16[8,128,2048]{2,1,0:T(8,128)(2,1)}, ...) custom-call(bf16[1024,1536]{1,0:T(8,128)(2,1)} %bitcast.91, ...), custom_call_target="tpu_custom_call" | custom-call | bytes 1024 | tf_op jit(solution)/shard_map/mixed/pallas_call | solution.py:153
  245.3 72.6 %feed_forward.1 = (f32[128,2048]{1,0:T(8,128)}, bf16[128,2048]{1,0:T(8,128)(2,1)}, f32[16,2048]{1,0:T(8,128)}, bf16[8,128,2048]{2,1,0:T(8,128)(2,1)}, bf16[704,2...) custom-call(bf16[8,128,2048]{2,1,0:T(8,128)(2,1)} %get-tuple-element.60.refs_0_, ...), custom_call_target="tpu_custom_call" | custom-call | bytes 1024 | tf_op jit(solution)/shard_map/feed_forward/pallas_call | solution.py:153
  317.9 0.3 reduce-scatter.6.cloned.1.call-start
  318.2 62.1 %attend_back.1 = (f32[128,2048]{1,0:T(8,128)}, bf16[8,128,2048]{2,1,0:T(8,128)(2,1)}, bf16[1024,512]{1,0:T(8,128)(2,1)}, bf16[1024,1536]{1,0:T(8,128)(2,1)}) custom-call(bf16[8,128,2048]{2,1,0:T(8,128)(2,1)} %get-tuple-element.65.refs_0_, f32[128,2048]{1,0:T(8,128)} %get-tuple-element.64.refs_4_.refs_1_, bf16[128,2048]{1,0:T(8,128)(2,1)} %get-tuple-element.66.refs_2_, ...), custom_call_target="tpu_custom_call" | custom-call | bytes 1024 | tf_op jit(solution)/shard_map/attend_back/pallas_call | solution.py:153
  380.4 2.5 fusion.3
  383.0 1.0 copy.51
  384.1 0.5 copy-done.24
  384.6 5.9 %convolution_convert_fusion.1.refs_0_ = bf16[512,2048]{1,0:T(8,128)(2,1)} fusion(bf16[1024,512]{1,0:T(8,128)(2,1)S(1)} %copy-done.24, bf16[1024,2048]{1,0:T(8,128)(2,1)} %bitcast.129), kind=kOutput, calls=%fused_computation.1 | convolution fusion | flops 2148532224 | bytes 7340032 | tf_op jit(solution)/shard_map/tf,td->fd/dot_general | solution.py:1351
  390.4 8.9 %reduce-scatter.4.cloned.1.call-done = bf16[512,1408]{1,0:T(8,128)(2,1)} async-done(((bf16[2048,1408]{1,0:T(8,128)(2,1)}), bf16[512,1408]{1,0:T(8,128)(2,1)}) %reduce-scatter.4.cloned.1.call-update) | async-done | bytes 1441808 | tf_op jit(solution)/shard_map/reduce_scatter | solution.py:1171
  399.4 0.8 copy-done.15
  400.4 47.0 %inner_grad.1 = (bf16[8,128,1536]{2,1,0:T(8,128)(2,1)}, f32[16,1280]{1,0:T(8,128)}, bf16[8,64,1408]{2,1,0:T(8,128)(2,1)}) custom-call(bf16[8,128,1536]{2,1,0:T(8,128)(2,1)} %bitcast.106, f32[128,1536]{1,0:T(8,128)} %get-tuple-element.71.refs_1_, f32[128,256]{1,0:T(8,128)} %get-tuple-element.107.refs_1_.refs_2_, ...), custom_call_target="tpu_custom_call" | custom-call | bytes 1024 | tf_op jit(solution)/shard_map/inner_grad/pallas_call | solution.py:153
  447.4 3.9 fusion
  451.3 1.8 convolution_convert_fusion.2
  453.1 43.0 %normed_grad.1 = (bf16[8,128,256]{2,1,0:T(8,128)(2,1)}, bf16[4,64,1536]{2,1,0:T(8,128)(2,1)}, bf16[176,2048]{1,0:T(8,128)(2,1)}) custom-call(bf16[8,128,256]{2,1,0:T(8,128)(2,1)} %bitcast.118, bf16[4,64,1536]{2,1,0:T(8,128)(2,1)} %bitcast.116, bf16[4,176,2048]{2,1,0:T(8,128)(2,1)} %bitcast.107), custom_call_target="tpu_custom_call" | custom-call | bytes 1024 | tf_op jit(solution)/shard_map/normed_grad/pallas_call | solution.py:153
  496.2 1.3 multiply_reduce_fusion
  497.8 0.8 stack.37.refs_0_
  498.6 19.3 %end.1 = (f32[8,128]{1,0:T(8,128)}, bf16[8,32,512]{2,1,0:T(8,128)(2,1)}) custom-call(f32[8,4,8,128]{3,2,1,0:T(8,128)} %stack.37.refs_0_, bf16[8,32,512]{2,1,0:T(8,128)(2,1)} %bitcast.119), custom_call_target="tpu_custom_call" | custom-call | bytes 1024 | tf_op jit(solution)/shard_map/end/pallas_call | solution.py:153
  517.9 1.0 convert_bitcast_fusion.1
  518.9 0.8 copy.59
  519.8 0.3 copy.53
  520.1 0.3 copy.54
  520.5 2.5 convert_element_type.96
  523.0 1.4 convert_reduce_fusion
  524.3 0.7 slice.71
  525.0 3.8 unfold.1
  529.0 0.5 slice_bitcast_fusion.1
  529.5 0.5 slice_bitcast_fusion.2
  530.1 0.5 slice_bitcast_fusion
  530.6 0.7 fusion.8
  531.2 1.3 add_bitcast_fusion
  532.5 2.1 convert_element_type.95
  534.6 2.3 copy.65
  (92 shorter events, 1.7 us)
Async XLA Ops:
  7.2 3.5 copy-start.19
  7.2 3.5 copy-start.18
  7.2 3.5 copy-start.21
  7.2 3.5 copy-start.20
  7.2 6.1 %copy-start.12 = (f32[128,2048]{1,0:T(8,128)S(1)}, f32[128,2048]{1,0:T(8,128)}, u32[]{:S(2)}) copy-start(f32[128,2048]{1,0:T(8,128)} %param.25) | copy-start | bytes 3145732
  7.2 120.9 %all-gather.3.cloned.1.call-start = ((), (), s32[]{:S(2)}) async-start(), calls=%async_computation.3 | async-start | bytes 1310720 | tf_op jit(solution)/shard_map/all_gather | solution.py:1143
  10.7 33.4 %copy-start.4 = (f32[128,8,256]{2,0,1:T(8,128)}, f32[128,8,256]{2,0,1:T(8,128)S(1)}, u32[]{:S(2)}) copy-start(f32[128,8,256]{2,0,1:T(8,128)S(1)} %copy.46) | copy-start | bytes 3145732
  14.1 34.8 %copy-start.17 = (s32[1,4]{1,0:T(1,128)S(1)}, s32[1,4]{1,0:T(1,128)}, u32[]{:S(2)}) copy-start(s32[1,4]{1,0:T(1,128)} %param.16) | copy-start | bytes 52
  14.1 35.0 %copy-start.10 = (f32[176,2048]{1,0:T(8,128)S(1)}, f32[176,2048]{1,0:T(8,128)}, u32[]{:S(2)}) copy-start(f32[176,2048]{1,0:T(8,128)} %param.29) | copy-start | bytes 4325380
  44.1 86.3 %all-gather.5.cloned.1.call-start = ((), (), s32[]{:S(2)}) async-start(), calls=%async_computation.4 | async-start | bytes 2621440 | tf_op jit(solution)/shard_map/all_gather | solution.py:1241
  44.8 354.5 %reduce-scatter.4.cloned.1.call-start = ((), (), s32[]{:S(2)}) async-start(), calls=%async_computation.5 | async-start | bytes 7208960 | tf_op jit(solution)/shard_map/reduce_scatter | solution.py:1171
  53.7 9.1 %copy-start.13 = (f32[8,128,256]{2,1,0:T(8,128)S(1)}, f32[8,128,256]{2,1,0:T(8,128)}, u32[]{:S(2)}) copy-start(f32[8,128,256]{2,1,0:T(8,128)} %get-tuple-element.51) | copy-start | bytes 3145732
  57.6 5.4 copy-start.14
  62.0 3.6 copy-start.2
  62.0 3.6 copy-start.3
  62.9 2.7 copy-start.7
  65.6 61.6 %copy-start.6 = (f32[1,128,2048]{2,1,0:T(8,128)S(1)}, f32[1,128,2048]{2,1,0:T(8,128)}, u32[]{:S(2)}) copy-start(f32[1,128,2048]{2,1,0:T(8,128)} %param.17) | copy-start | bytes 3145732
  317.9 180.6 %reduce-scatter.6.cloned.1.call-start = ((), (), s32[]{:S(2)}) async-start(), calls=%async_computation.6 | async-start | bytes 1310720 | tf_op jit(solution)/shard_map/reduce_scatter | solution.py:1153
  318.2 62.2 %copy-start.1 = (bf16[8,128,1536]{2,1,0:T(8,128)(2,1)S(1)}, bf16[8,128,1536]{2,1,0:T(8,128)(2,1)}, u32[]{:S(2)}) copy-start(bf16[8,128,1536]{2,1,0:T(8,128)(2,1)} %get-tuple-element.55) | copy-start | bytes 9437188
  383.0 1.6 copy-start.24
  384.0 148.5 %reduce-scatter.8.cloned.1.call-start = ((), (), s32[]{:S(2)}) async-start(), calls=%async_computation.7 | async-start | bytes 2621440 | tf_op jit(solution)/shard_map/reduce_scatter | solution.py:1358
  399.3 0.9 copy-start.15
  400.4 47.0 %copy-start.8 = (bf16[8,128,256]{2,1,0:T(8,128)(2,1)S(1)}, bf16[8,128,256]{2,1,0:T(8,128)(2,1)}, u32[]{:S(2)}) copy-start(bf16[8,128,256]{2,1,0:T(8,128)(2,1)} %copy-done.7) | copy-start | bytes 1572868
  447.4 3.9 copy-start.23
  453.1 43.0 %copy-start.5 = (f32[128,8,256]{2,0,1:T(8,128)S(1)}, f32[128,8,256]{2,0,1:T(8,128)}, u32[]{:S(2)}) copy-start(f32[128,8,256]{2,0,1:T(8,128)} %copy-done.4) | copy-start | bytes 3145732
  453.1 44.4 %copy-start.16 = (f32[16,1280]{1,0:T(8,128)S(1)}, f32[16,1280]{1,0:T(8,128)}, u32[]{:S(2)}) copy-start(f32[16,1280]{1,0:T(8,128)} %get-tuple-element.79) | copy-start | bytes 245764
  496.1 23.6 %copy-start.9 = (bf16[8,128,256]{2,1,0:T(8,128)(2,1)S(1)}, bf16[8,128,256]{2,1,0:T(8,128)(2,1)}, u32[]{:S(2)}) copy-start(bf16[8,128,256]{2,1,0:T(8,128)(2,1)} %get-tuple-element.78) | copy-start | bytes 1572868
  520.5 8.3 %copy-start = (f32[1,128,2048]{2,1,0:T(8,128)S(1)}, f32[1,128,2048]{2,1,0:T(8,128)}, u32[]{:S(2)}) copy-start(f32[1,128,2048]{2,1,0:T(8,128)} %param.15) | copy-start | bytes 3145732
  523.0 6.1 %copy-start.22 = (f32[8,128]{1,0:T(8,128)S(1)}, f32[8,128]{1,0:T(8,128)}, u32[]{:S(2)}) copy-start(f32[8,128]{1,0:T(8,128)} %get-tuple-element.81) | copy-start | bytes 12292
  523.0 8.3 %copy-start.11 = (f32[128,2048]{1,0:T(8,128)S(1)}, f32[128,2048]{1,0:T(8,128)}, u32[]{:S(2)}) copy-start(f32[128,2048]{1,0:T(8,128)} %get-tuple-element.69) | copy-start | bytes 3145732
Sparse Core Ops, SparseCore 0:
  44.2 27.1 all-gather.2
  72.9 45.3 all-gather.4
  318.1 81.2 reduce-scatter.3
  402.1 45.0 reduce-scatter.5
  449.4 60.6 reduce-scatter.7
